TPU v7x, 32 devices: a whole 2x2x4 slice. The times are simulated.
32 devices in a mesh: replica: 2 (over y), shard: 16 (over z, x, core).
Axes of the slice: x: 2, y: 2, z: 4, core: 2. Of those that a mesh axis runs over, the one named last changes fastest.
Arguments:
- tokens: bfloat16 [16384, 2048], P(('replica', 'shard')), may hold values from -6 to 6
- block_ids: int32 [32, 512], P(('replica', 'shard')), may hold values from 0 to 3, never falling along the last dimension, each value on 1 to 256 neighbouring positions
- query_weight: bfloat16 [2048, 2048], P('shard'), may hold values from -0.47851562 to 0.47851562
- key_projection_weight: bfloat16 [2048, 512], P('shard'), may hold values from -0.47851562 to 0.47851562
- value_projection_weight: bfloat16 [2048, 512], P('shard'), may hold values from -0.125 to 0.125
- output_weight: bfloat16 [2048, 2048], P('shard'), may hold values from -2.390625 to 2.390625
- gate_weight: bfloat16 [2048, 8192], P('shard'), may hold values from -0.125 to 0.125
- up_weight: bfloat16 [2048, 8192], P('shard'), may hold values from -0.125 to 0.125
- down_weight: bfloat16 [8192, 2048], P('shard'), may hold values from -0.359375 to 0.359375
- attn_gain: bfloat16 [2048], P('shard'), may hold values from 0.5 to 1.5
- mlp_gain: bfloat16 [2048], P('shard'), may hold values from 0.5 to 1.5
- cotangent: bfloat16 [16384, 2048], P(('replica', 'shard')), may hold values from -6 to 6
Outputs:
- output: bfloat16 [16384, 2048], P(('replica', 'shard'))
- input_grad: float32 [16384, 2048], P(('replica', 'shard'))
- query_grad: float32 [2048, 2048], P('shard')
- key_grad: float32 [2048, 512], P('shard')
- value_grad: float32 [2048, 512], P('shard')
- output_grad: float32 [2048, 2048], P('shard')
- gate_grad: float32 [2048, 8192], P('shard')
- up_grad: float32 [2048, 8192], P('shard')
- down_grad: float32 [8192, 2048], P('shard')
- attn_gain_grad: float32 [2048], P('shard')
- mlp_gain_grad: float32 [2048], P('shard')
Inputs may be any that keep to these rules, and one draw needn't show every extreme that they name: `block_ids`: in each row the ids start at 0 and never fall, every id of 0 to 3 appears, a block holds 1 to 256 tokens and one block of every row holds exactly 256.
All inputs are finite; a program needn't handle non-finite values.
Results may differ from a plain program's by a relative error of at most 0.015.
Values may be sent and summed in bfloat16 or wider, within the bound.
No kernel may reach another device: no remote copies, remote signals or barrier semaphores. Data moves between devices by JAX's collectives and lax.ppermute only.
A program may use at most 576 MiB of HBM per device.

v0:
```python
import jax
import jax.numpy as jnp
from jax import lax
from jax.sharding import PartitionSpec as P

QUERY_HEADS = 32
KEY_VALUE_HEADS = 8
HEAD_WIDTH = 64


NORM_EPS = 1e-05
RESIDUAL = 0.22
SCORE_SCALE = 0.015625
ROPE_THETA = 10000000.0


def rope_tables(token_length, width):
    half_width = width // 2
    frequency = ROPE_THETA ** (-(jnp.arange(half_width, dtype=jnp.float32) * 2.0) / width)
    angles = jnp.arange(token_length, dtype=jnp.float32)[:, None] * frequency[None, :]
    cosine_table = jnp.concatenate([jnp.cos(angles), jnp.cos(angles)], axis=1)
    sine_table = jnp.concatenate([jnp.sin(angles), jnp.sin(angles)], axis=1)
    return (cosine_table, sine_table)


def apply_rotary(value_rows, cosine_table, sine_table):
    half_width = value_rows.shape[-1] // 2
    turned = jnp.concatenate([-value_rows[..., half_width:], value_rows[..., :half_width]], axis=-1)
    return value_rows * cosine_table[:, None, :] + turned * sine_table[:, None, :]


def rms_norm(value_rows, gain_vec):
    return (
        value_rows
        * lax.rsqrt(jnp.mean(value_rows * value_rows, axis=-1, keepdims=True) + NORM_EPS)
        * gain_vec
    )


def matrix_product(left_side, right_side):
    return jnp.dot(left_side, right_side, preferred_element_type=jnp.float32)


def contract_rows(left_side, right_side):
    return lax.dot_general(
        left_side, right_side, (((0,), (0,)), ((), ())), preferred_element_type=jnp.float32
    )


def contract_cols(left_side, right_side):
    return lax.dot_general(
        left_side, right_side, (((1,), (1,)), ((), ())), preferred_element_type=jnp.float32
    )


def shards(
    tokens,
    block_ids,
    query_weight,
    key_projection_weight,
    value_projection_weight,
    output_weight,
    gate_weight,
    up_weight,
    down_weight,
    attn_gain,
    mlp_gain,
    cotangent,
):
    token_length = tokens.shape[0]
    heads_per_group = QUERY_HEADS // KEY_VALUE_HEADS
    group_width = heads_per_group * HEAD_WIDTH
    query_all, key_gathered, value_all, output_all, attn_gathered = (
        lax.all_gather(query_weight, "shard", axis=0, tiled=True),
        lax.all_gather(key_projection_weight, "shard", axis=0, tiled=True),
        lax.all_gather(value_projection_weight, "shard", axis=0, tiled=True),
        lax.all_gather(output_weight, "shard", axis=0, tiled=True),
        lax.all_gather(attn_gain, "shard", axis=0, tiled=True),
    )
    gate_all, up_all, down_all, mlp_gathered = (
        lax.all_gather(gate_weight, "shard", axis=0, tiled=True),
        lax.all_gather(up_weight, "shard", axis=0, tiled=True),
        lax.all_gather(down_weight, "shard", axis=0, tiled=True),
        lax.all_gather(mlp_gain, "shard", axis=0, tiled=True),
    )
    attn_scale = attn_gathered.astype(jnp.float32)
    mlp_scale = mlp_gathered.astype(jnp.float32)
    inputs = tokens.astype(jnp.float32)
    seq_ids = block_ids[0]
    visible = seq_ids[None, :] <= seq_ids[:, None]
    cosine_table, sine_table = rope_tables(token_length, HEAD_WIDTH)

    def rotary_flat(flat_projection, head_count):
        return apply_rotary(
            flat_projection.reshape(token_length, head_count, HEAD_WIDTH), cosine_table, sine_table
        ).reshape(token_length, head_count * HEAD_WIDTH)

    first_normed = rms_norm(inputs, attn_scale).astype(jnp.bfloat16)
    query_rows = rotary_flat(matrix_product(first_normed, query_all), QUERY_HEADS).astype(
        jnp.bfloat16
    )
    keys_rotated = rotary_flat(matrix_product(first_normed, key_gathered), KEY_VALUE_HEADS).astype(
        jnp.bfloat16
    )
    value_rows = matrix_product(first_normed, value_all).astype(jnp.bfloat16)

    def group_parts(head_cluster):
        query_part = query_rows[
            :, head_cluster * group_width : (head_cluster + 1) * group_width
        ].reshape(token_length, heads_per_group, HEAD_WIDTH)
        key_part = keys_rotated[:, head_cluster * HEAD_WIDTH : (head_cluster + 1) * HEAD_WIDTH]
        value_part = value_rows[:, head_cluster * HEAD_WIDTH : (head_cluster + 1) * HEAD_WIDTH]
        scores = SCORE_SCALE * jnp.einsum(
            "qgd,td->gqt", query_part, key_part, preferred_element_type=jnp.float32
        )
        scores = jnp.where(visible[None], scores, -1e30)
        return (query_part, key_part, value_part, scores)

    mixed_parts = []
    logsum_parts = []
    for head_cluster in range(KEY_VALUE_HEADS):
        query_part, key_part, value_part, scores = group_parts(head_cluster)
        row_max = jnp.max(scores, axis=-1, keepdims=True)
        logsum = row_max + jnp.log(jnp.sum(jnp.exp(scores - row_max), axis=-1, keepdims=True))
        attend = jnp.exp(scores - logsum).astype(jnp.bfloat16)
        mixed_parts.append(
            jnp.einsum(
                "gqt,td->qgd", attend, value_part, preferred_element_type=jnp.float32
            ).reshape(token_length, group_width)
        )
        logsum_parts.append(logsum)
    mixed = jnp.concatenate(mixed_parts, axis=1).astype(jnp.bfloat16)
    residual = inputs + RESIDUAL * matrix_product(mixed, output_all)
    normed2 = rms_norm(residual, mlp_scale).astype(jnp.bfloat16)
    gating = matrix_product(normed2, gate_all)
    upward = matrix_product(normed2, up_all)
    hidden_act = (jax.nn.silu(gating) * upward).astype(jnp.bfloat16)
    result = residual + RESIDUAL * matrix_product(hidden_act, down_all)
    output = result.astype(jnp.bfloat16)
    gate_all, up_all, down_all, mlp_gathered = (
        lax.all_gather(gate_weight, "shard", axis=0, tiled=True),
        lax.all_gather(up_weight, "shard", axis=0, tiled=True),
        lax.all_gather(down_weight, "shard", axis=0, tiled=True),
        lax.all_gather(mlp_gain, "shard", axis=0, tiled=True),
    )
    grad_out = cotangent.astype(jnp.float32)
    down_in = (RESIDUAL * grad_out).astype(jnp.bfloat16)
    down_shard = lax.psum_scatter(
        contract_rows(hidden_act, down_in), "shard", scatter_dimension=0, tiled=True
    )
    hidden_grad = contract_cols(down_in, down_all)
    _, swiglu_pull = jax.vjp(lambda first, second: jax.nn.silu(first) * second, gating, upward)
    gating_grad, upward_grad = swiglu_pull(hidden_grad)
    gating_grad = gating_grad.astype(jnp.bfloat16)
    upward_grad = upward_grad.astype(jnp.bfloat16)
    gate_shard = lax.psum_scatter(
        contract_rows(normed2, gating_grad), "shard", scatter_dimension=0, tiled=True
    )
    up_shard = lax.psum_scatter(
        contract_rows(normed2, upward_grad), "shard", scatter_dimension=0, tiled=True
    )
    normed2_grad = contract_cols(gating_grad, gate_all) + contract_cols(upward_grad, up_all)
    _, norm2_pull = jax.vjp(rms_norm, residual, mlp_scale)
    residual_part, grad_mlp_gain = norm2_pull(normed2_grad)
    residual_grad = grad_out + residual_part
    query_all, key_gathered, value_all, output_all, attn_gathered = (
        lax.all_gather(query_weight, "shard", axis=0, tiled=True),
        lax.all_gather(key_projection_weight, "shard", axis=0, tiled=True),
        lax.all_gather(value_projection_weight, "shard", axis=0, tiled=True),
        lax.all_gather(output_weight, "shard", axis=0, tiled=True),
        lax.all_gather(attn_gain, "shard", axis=0, tiled=True),
    )
    attn_in = (RESIDUAL * residual_grad).astype(jnp.bfloat16)
    grad_output = contract_rows(mixed, attn_in)
    mixed_grad = contract_cols(attn_in, output_all).astype(jnp.bfloat16)
    query_grads = []
    key_grads = []
    value_grads = []
    for head_cluster in range(KEY_VALUE_HEADS):
        query_part, key_part, value_part, scores = group_parts(head_cluster)
        attend = jnp.exp(scores - logsum_parts[head_cluster])
        grad_part = mixed_grad[
            :, head_cluster * group_width : (head_cluster + 1) * group_width
        ].reshape(token_length, heads_per_group, HEAD_WIDTH)
        attend_grad = jnp.einsum(
            "qgd,td->gqt", grad_part, value_part, preferred_element_type=jnp.float32
        )
        row_delta = jnp.sum(attend * attend_grad, axis=-1, keepdims=True)
        score_grad = (attend * (attend_grad - row_delta)).astype(jnp.bfloat16)
        query_grads.append(
            (
                SCORE_SCALE
                * jnp.einsum(
                    "gqt,td->qgd", score_grad, key_part, preferred_element_type=jnp.float32
                )
            ).reshape(token_length, group_width)
        )
        key_grads.append(
            SCORE_SCALE
            * jnp.einsum("gqt,qgd->td", score_grad, query_part, preferred_element_type=jnp.float32)
        )
        value_grads.append(
            jnp.einsum(
                "gqt,qgd->td",
                attend.astype(jnp.bfloat16),
                grad_part,
                preferred_element_type=jnp.float32,
            )
        )
    queries_grad = jnp.concatenate(query_grads, axis=1)
    keys_grad = jnp.concatenate(key_grads, axis=1)
    value_lin_grad = jnp.concatenate(value_grads, axis=1).astype(jnp.bfloat16)
    _, query_rope_pull = jax.vjp(
        lambda flat_projection: rotary_flat(flat_projection, QUERY_HEADS),
        jnp.zeros((token_length, QUERY_HEADS * HEAD_WIDTH), jnp.float32),
    )
    _, key_rope_pull = jax.vjp(
        lambda flat_projection: rotary_flat(flat_projection, KEY_VALUE_HEADS),
        jnp.zeros((token_length, KEY_VALUE_HEADS * HEAD_WIDTH), jnp.float32),
    )
    query_lin_grad = query_rope_pull(queries_grad)[0].astype(jnp.bfloat16)
    key_lin_grad = key_rope_pull(keys_grad)[0].astype(jnp.bfloat16)
    grad_query = contract_rows(first_normed, query_lin_grad)
    grad_key = contract_rows(first_normed, key_lin_grad)
    grad_value = contract_rows(first_normed, value_lin_grad)
    normed1_grad = (
        contract_cols(query_lin_grad, query_all)
        + contract_cols(key_lin_grad, key_gathered)
        + contract_cols(value_lin_grad, value_all)
    )
    _, norm1_pull = jax.vjp(rms_norm, inputs, attn_scale)
    input_part, grad_attn_gain = norm1_pull(normed1_grad)
    input_grad = residual_grad + input_part
    query_shard, key_shard, value_shard, output_shard, attn_gain_shard, mlp_gain_shard = (
        lax.psum_scatter(grad_query, "shard", scatter_dimension=0, tiled=True),
        lax.psum_scatter(grad_key, "shard", scatter_dimension=0, tiled=True),
        lax.psum_scatter(grad_value, "shard", scatter_dimension=0, tiled=True),
        lax.psum_scatter(grad_output, "shard", scatter_dimension=0, tiled=True),
        lax.psum_scatter(grad_attn_gain, "shard", scatter_dimension=0, tiled=True),
        lax.psum_scatter(grad_mlp_gain, "shard", scatter_dimension=0, tiled=True),
    )
    (
        query_shard,
        key_shard,
        value_shard,
        output_shard,
        gate_shard,
        up_shard,
        down_shard,
        attn_gain_shard,
        mlp_gain_shard,
    ) = lax.psum(
        (
            query_shard,
            key_shard,
            value_shard,
            output_shard,
            gate_shard,
            up_shard,
            down_shard,
            attn_gain_shard,
            mlp_gain_shard,
        ),
        "replica",
    )
    return (
        output,
        input_grad,
        query_shard,
        key_shard,
        value_shard,
        output_shard,
        gate_shard,
        up_shard,
        down_shard,
        attn_gain_shard,
        mlp_gain_shard,
    )


def solution(mesh):
    return jax.shard_map(
        shards,
        mesh=mesh,
        in_specs=(
            P(("replica", "shard"), None),
            P(("replica", "shard"), None),
            P("shard", None),
            P("shard", None),
            P("shard", None),
            P("shard", None),
            P("shard", None),
            P("shard", None),
            P("shard", None),
            P("shard"),
            P("shard"),
            P(("replica", "shard"), None),
        ),
        out_specs=(
            P(("replica", "shard"), None),
            P(("replica", "shard"), None),
            P("shard", None),
            P("shard", None),
            P("shard", None),
            P("shard", None),
            P("shard", None),
            P("shard", None),
            P("shard", None),
            P("shard"),
            P("shard"),
        ),
        check_vma=False,
    )
```

profile of v0, /device:TPU:0, one launch (start us, length us, event | category | flops | bytes accessed | tf_op | source)
XLA Modules:
  0.0 3746.9 jit_solution(17492493865097504098)
XLA Ops:
  12.0 23.1 all-gather
  35.4 2.5 mul.468
  38.0 5.5 copy.142
  43.5 17.5 all-gather.1
  61.8 3.1 fusion.154
  65.5 31.3 all-gather.10.cloned.1.call-done
  96.8 3.8 convolution_convert_fusion.1
  100.5 71.4 %all-gather.14.cloned.1.call-done = bf16[2048,2048]{1,0:T(8,128)(2,1)} async-done(((bf16[128,2048]{1,0:T(8,128)(2,1)}), bf16[2048,2048]{1,0:T(8,128)(2,1)}) %all-gather.14.cloned.1.call-update) | async-done | bytes 8388624 | tf_op jit(solution)/shard_map/all_gather | solution.py:74
  172.0 9.8 fusion.152
  181.7 5.3 copy.143
  187.1 2.7 slice_negate_fusion.1
  189.8 2.5 maximum_multiply_fusion
  192.3 5.4 copy.144
  197.7 5.7 add_convert_fusion.2
  217.8 3.2 fusion.113
  224.0 3.9 fusion.51
  228.0 9.8 exponential_reduce_fusion
  237.8 3.6 convolution_convert_fusion.9
  242.2 7.0 exponential_reduce_fusion.1
  249.3 3.4 convolution_convert_fusion.8
  265.4 7.9 multiply_reduce_fusion.2
  275.7 139.3 %all-gather.18.cloned.1.call-done = bf16[2048,8192]{1,0:T(8,128)(2,1)} async-done(((bf16[128,8192]{1,0:T(8,128)(2,1)}), bf16[2048,8192]{1,0:T(8,128)(2,1)}) %all-gather.18.cloned.1.call-update) | async-done | bytes 33554448 | tf_op jit(solution)/shard_map/all_gather | solution.py:81
  415.0 26.9 fusion.161
  441.9 142.6 %all-gather.20.cloned.1.call-done = bf16[2048,8192]{1,0:T(8,128)(2,1)} async-done(((bf16[128,8192]{1,0:T(8,128)(2,1)}), bf16[2048,8192]{1,0:T(8,128)(2,1)}) %all-gather.20.cloned.1.call-update) | async-done | bytes 33554448 | tf_op jit(solution)/shard_map/all_gather | solution.py:82
  584.5 26.9 fusion.162
  611.4 142.7 %all-gather.22.cloned.1.call-done = bf16[8192,2048]{1,0:T(8,128)(2,1)} async-done(((bf16[512,2048]{1,0:T(8,128)(2,1)}), bf16[8192,2048]{1,0:T(8,128)(2,1)}) %all-gather.22.cloned.1.call-update) | async-done | bytes 33554448 | tf_op jit(solution)/shard_map/all_gather | solution.py:83
  754.2 38.7 %multiply_convert_fusion = (bf16[512,8192]{1,0:T(8,128)(2,1)}, bf16[512,8192]{1,0:T(8,128)(2,1)}, bf16[512,8192]{1,0:T(8,128)(2,1)}) fusion(f32[512,8192]{1,0:T(8,128)} %fusion.161, f32[512,8192]{1,0:T(8,128)} %fusion.162, bf16[8192,2048]{1,0:T(8,128)(2,1)} %all-gather.22.cloned.1.call-done, bf16[512,2048]{1,0:T(8,128)(2,1)} %param.23), kind=kOutput, calls=%fused_computation.4 | convolution fusion | flops 17250123776 | bytes 94371840 | tf_op jit(solution)/shard_map/dot_general | solution.py:51
  792.8 25.5 fusion.163
  818.4 26.8 multiply_reduce_fusion
  845.2 4.0 convert_add_fusion.1
  849.3 9.9 convolution_convert_fusion
  860.2 2.7 fusion.108
  863.1 2.7 fusion.110
  866.0 2.7 fusion.112
  868.8 2.7 fusion.114
  871.7 3.7 fusion.116
  875.7 3.6 fusion.118
  879.6 7.7 fusion.15
  887.4 19.0 fusion.12
  906.4 14.3 fusion.17
  920.8 3.8 fusion.73
  924.5 14.1 fusion.14
  938.6 4.5 fusion.75
  954.4 3.4 fusion.148
  958.8 3.5 fusion.89
  978.9 3.5 fusion.146
  995.3 8.7 fusion.150
  1004.1 13.1 fusion.105
  1018.8 30.3 fusion.166
  1049.1 30.1 fusion.167
  1080.9 29.2 fusion.52
  1110.2 177.2 %reduce-scatter.8.cloned.1.call-done = f32[128,2048]{1,0:T(8,128)} async-done(((f32[2048,2048]{1,0:T(8,128)}), f32[128,2048]{1,0:T(8,128)}) %reduce-scatter.8.cloned.1.call-update) | async-done | bytes 1048592 | tf_op jit(solution)/shard_map/reduce_scatter | solution.py:235
  1287.4 180.6 %reduce-scatter.14.cloned.1.call-done = f32[128,2048]{1,0:T(8,128)} async-done(((f32[2048,2048]{1,0:T(8,128)}), f32[128,2048]{1,0:T(8,128)}) %reduce-scatter.14.cloned.1.call-update) | async-done | bytes 1048592 | tf_op jit(solution)/shard_map/reduce_scatter | solution.py:238
  1468.0 635.8 %reduce-scatter.16.cloned.1.call-done = f32[128,8192]{1,0:T(8,128)} async-done(((f32[2048,8192]{1,0:T(8,128)}), f32[128,8192]{1,0:T(8,128)}) %reduce-scatter.16.cloned.1.call-update) | async-done | bytes 4194320 | tf_op jit(solution)/shard_map/reduce_scatter | solution.py:156
  2103.8 636.1 %reduce-scatter.18.cloned.1.call-done = f32[128,8192]{1,0:T(8,128)} async-done(((f32[2048,8192]{1,0:T(8,128)}), f32[128,8192]{1,0:T(8,128)}) %reduce-scatter.18.cloned.1.call-update) | async-done | bytes 4194320 | tf_op jit(solution)/shard_map/reduce_scatter | solution.py:159
  2739.9 635.8 %reduce-scatter.20.cloned.1.call-done = f32[512,2048]{1,0:T(8,128)} async-done(((f32[8192,2048]{1,0:T(8,128)}), f32[512,2048]{1,0:T(8,128)}) %reduce-scatter.20.cloned.1.call-update) | async-done | bytes 4194320 | tf_op jit(solution)/shard_map/reduce_scatter | solution.py:148
  3379.3 7.2 fusion.164
  3386.6 4.5 fusion.7
  3391.0 59.5 %all-reduce.6 = (f32[2048]{0:T(1024)S(1)}, f32[2048]{0:T(1024)S(1)}) all-reduce(f32[2048]{0:T(1024)S(1)} %get-tuple-element.13, f32[2048]{0:T(1024)S(1)} %copy-done.119), channel_id=9, replica_groups=mesh['replica'=2,'shard'=16] {'shard'}, use_global_device_ids=true, to_apply=%region_43.44.clone | all-reduce | flops 4096 | bytes 32768
  3450.7 5.9 all-reduce.7
  3456.6 7.1 fusion.9
  3463.7 24.9 add_convert_fusion.1
  3488.6 233.7 %all-reduce.11.cloned.1.call-done = (f32[128,2048]{1,0:T(8,128)}, f32[128,512]{1,0:T(8,128)}, f32[128,512]{1,0:T(8,128)}, f32[128,2048]{1,0:T(8,128)}, f32[128,8...) async-done(((f32[128,2048]{1,0:T(8,128)}, f32[128,512]{1,0:T(8,128)}, f32[128,512]{1,0:T(8,128)}, f32[128,2048]{1,0:T(8,128)}, f32[128,8192]{1,0:T(8,128)}, ...) | async-done | bytes 15204368 | tf_op jit(solution)/shard_map/psum | solution.py:252
  3722.3 2.4 copy.260
  (374 shorter events, 104.2 us)
Async XLA Ops:
  7.2 54.6 %all-gather.12.cloned.1.call-start = ((), (), s32[]{:S(2)}) async-start(), calls=%async_computation.8 | async-start | bytes 2228224 | tf_op jit(solution)/shard_map/all_gather | solution.py:75
  7.9 88.8 %all-gather.10.cloned.1.call-start = ((), (), s32[]{:S(2)}) async-start(), calls=%async_computation.7 | async-start | bytes 2228224 | tf_op jit(solution)/shard_map/all_gather | solution.py:76
  8.7 163.3 %all-gather.14.cloned.1.call-start = ((), (), s32[]{:S(2)}) async-start(), calls=%async_computation.9 | async-start | bytes 8912896 | tf_op jit(solution)/shard_map/all_gather | solution.py:74
  9.4 256.0 %all-gather.16.cloned.1.call-start = ((), (), s32[]{:S(2)}) async-start(), calls=%async_computation.10 | async-start | bytes 8912896 | tf_op jit(solution)/shard_map/all_gather | solution.py:77
  10.0 405.0 %all-gather.18.cloned.1.call-start = ((), (), s32[]{:S(2)}) async-start(), calls=%async_computation.11 | async-start | bytes 35651584 | tf_op jit(solution)/shard_map/all_gather | solution.py:81
  10.6 573.9 %all-gather.20.cloned.1.call-start = ((), (), s32[]{:S(2)}) async-start(), calls=%async_computation.12 | async-start | bytes 35651584 | tf_op jit(solution)/shard_map/all_gather | solution.py:82
  11.1 743.0 %all-gather.22.cloned.1.call-start = ((), (), s32[]{:S(2)}) async-start(), calls=%async_computation.13 | async-start | bytes 35651584 | tf_op jit(solution)/shard_map/all_gather | solution.py:83
  11.9 1098.3 %reduce-scatter.10.cloned.1.call-start = ((), (), s32[]{:S(2)}) async-start(), calls=%async_computation.15 | async-start | bytes 4456448 | tf_op jit(solution)/shard_map/reduce_scatter | solution.py:236
  35.1 136.9 %copy-start.86 = (f32[16,1,128]{2,1,0:T(1,128)}, f32[16,1,128]{2,1,0:T(1,128)S(1)}, u32[]{:S(2)}) copy-start(f32[16,1,128]{2,1,0:T(1,128)S(1)} %convert_element_type.154) | copy-start | bytes 24580
  35.4 29.7 copy-start.49
  38.0 23.0 copy-start
  38.0 23.6 copy-start.116
  61.0 212.3 %copy-start.94 = (f32[16,1,128]{2,1,0:T(1,128)}, f32[16,1,128]{2,1,0:T(1,128)S(1)}, u32[]{:S(2)}) copy-start(f32[16,1,128]{2,1,0:T(1,128)S(1)} %convert_element_type.155) | copy-start | bytes 24580
  61.0 128.8 %copy-start.47 = (f32[512,64]{0,1:T(8,128)}, f32[512,64]{0,1:T(8,128)S(1)}, u32[]{:S(2)}) copy-start(f32[512,64]{0,1:T(8,128)S(1)} %pad_maximum_fusion.1) | copy-start | bytes 393220
  61.6 110.4 %copy-start.91 = (f32[512]{0:T(512)}, f32[512]{0:T(512)S(1)}, u32[]{:S(2)}) copy-start(f32[512]{0:T(512)S(1)} %fusion.124) | copy-start | bytes 6148
  61.8 201.6 %copy-start.37 = (pred[512,512]{0,1:T(8,128)(4,1)}, pred[512,512]{0,1:T(8,128)(4,1)S(1)}, u32[]{:S(2)}) copy-start(pred[512,512]{0,1:T(8,128)(4,1)S(1)} %broadcast_compare_fusion) | copy-start | bytes 786436
  65.5 162.5 %copy-start.42 = (bf16[512,512]{0,1:T(8,128)(2,1)}, bf16[512,512]{0,1:T(8,128)(2,1)S(1)}, u32[]{:S(2)}) copy-start(bf16[512,512]{0,1:T(8,128)(2,1)S(1)} %fusion.104) | copy-start | bytes 1572868
  206.7 17.3 copy-start.51
  214.1 9.1 copy-start.53
  221.7 33.6 copy-start.10
  222.5 34.9 copy-start.8
  223.2 36.2 copy-start.6
  224.0 37.4 copy-start.3
  227.9 9.9 copy-start.89
  237.8 11.4 copy-start.102
  237.8 25.6 copy-start.100
  273.3 168.6 %copy-start.117 = (f32[512]{0:T(512)}, f32[512]{0:T(512)S(1)}, u32[]{:S(2)}) copy-start(f32[512]{0:T(512)S(1)} %get-tuple-element.89) | copy-start | bytes 6148
  273.3 168.6 %copy-start.114 = (f32[512]{0:T(512)}, f32[512]{0:T(512)S(1)}, u32[]{:S(2)}) copy-start(f32[512]{0:T(512)S(1)} %fusion.125) | copy-start | bytes 6148
  275.7 308.8 %copy-start.19 = (bf16[512,2048]{1,0:T(8,128)(2,1)}, bf16[512,2048]{1,0:T(8,128)(2,1)S(1)}, u32[]{:S(2)}) copy-start(bf16[512,2048]{1,0:T(8,128)(2,1)S(1)} %multiply_convert_fusion.3) | copy-start | bytes 6291460
  792.8 25.6 copy-start.34
  792.8 25.6 copy-start.95
  792.8 25.6 copy-start.115
  818.4 26.8 copy-start.118
  849.3 9.9 copy-start.36
  871.7 7.7 copy-start.74
  871.7 7.8 copy-start.38
  871.7 7.8 copy-start.97
  871.7 7.8 copy-start.99
  879.5 7.8 copy-start.71
  879.5 7.8 copy-start.101
  879.6 7.8 copy-start.103
  879.6 7.8 copy-start.105
  879.6 7.8 copy-start.107
  879.6 7.8 copy-start.109
  879.6 7.8 copy-start.111
  887.4 19.0 copy-start.4
  906.4 14.3 copy-start.63
  906.4 18.1 copy-start.11
  920.8 28.1 copy-start.21
  924.5 18.6 copy-start.62
  938.6 8.8 copy-start.29
  938.6 8.8 copy-start.31
  938.6 7.4 copy-start.25
  938.6 7.4 copy-start.58
  957.8 152.4 %reduce-scatter.12.cloned.1.call-start = ((), (), s32[]{:S(2)}) async-start(), calls=%async_computation.16 | async-start | bytes 4456448 | tf_op jit(solution)/shard_map/reduce_scatter | solution.py:237
  982.5 305.0 %reduce-scatter.8.cloned.1.call-start = ((), (), s32[]{:S(2)}) async-start(), calls=%async_computation.14 | async-start | bytes 17825792 | tf_op jit(solution)/shard_map/reduce_scatter | solution.py:235
  1004.0 464.0 %reduce-scatter.14.cloned.1.call-start = ((), (), s32[]{:S(2)}) async-start(), calls=%async_computation.17 | async-start | bytes 17825792 | tf_op jit(solution)/shard_map/reduce_scatter | solution.py:238
  1017.2 1086.6 %reduce-scatter.16.cloned.1.call-start = ((), (), s32[]{:S(2)}) async-start(), calls=%async_computation.18 | async-start | bytes 71303168 | tf_op jit(solution)/shard_map/reduce_scatter | solution.py:156
  1049.1 1690.8 %reduce-scatter.18.cloned.1.call-start = ((), (), s32[]{:S(2)}) async-start(), calls=%async_computation.19 | async-start | bytes 71303168 | tf_op jit(solution)/shard_map/reduce_scatter | solution.py:159
  1079.3 2296.5 %reduce-scatter.20.cloned.1.call-start = ((), (), s32[]{:S(2)}) async-start(), calls=%async_computation.20 | async-start | bytes 71303168 | tf_op jit(solution)/shard_map/reduce_scatter | solution.py:148
  1110.1 2612.2 %all-reduce.11.cloned.1.call-start = ((), (), s32[]{:S(2)}) async-start(), calls=%async_computation.21 | async-start | bytes 30408704 | tf_op jit(solution)/shard_map/psum | solution.py:252
  3379.3 7.3 copy-start.93
  3386.5 70.0 %copy-start.113 = (f32[512]{0:T(512)S(1)}, f32[512]{0:T(512)}, u32[]{:S(2)}) copy-start(f32[512]{0:T(512)} %copy-done.112) | copy-start | bytes 6148
  3722.3 8.1 copy-start.46
  (74 other events, 249.5 us)
Sparse Core Ops, SparseCore 0:
  10.2 44.1 all-gather.11
  56.5 40.1 all-gather.9
  98.9 73.0 all-gather.13
  174.0 72.8 all-gather.15
  248.3 166.6 all-gather.17
  416.4 168.0 all-gather.19
  586.1 168.0 all-gather.21
  958.0 72.7 reduce-scatter.9
  1035.2 71.8 reduce-scatter.11
  1111.1 176.3 reduce-scatter.7
  1291.6 176.4 reduce-scatter.13
  1472.1 631.6 reduce-scatter.15
  2108.1 631.8 reduce-scatter.17
  2744.0 631.6 reduce-scatter.19
  3378.6 343.6 all-reduce.10
where the time goes:
time: 3750 us
  waiting for transfers between devices  3030 us (81%)
  matrix products  453 us (12%)
  blocking collectives  106 us (3%)
  local copies, waits for them, and re-layouts  75.1 us (2%)
  other arithmetic  63.7 us (2%)
    reduce_scatter x1, waiting for transfers between devices, shards(): lax.psum_scatter(contract_rows(normed2, upward_grad), 'shard', scatter_di...  636 us
    reduce_scatter x1, waiting for transfers between devices, shards(): lax.psum_scatter(contract_rows(hidden_act, down_in), 'shard', scatter_dim...  636 us
    reduce_scatter x1, waiting for transfers between devices, shards(): lax.psum_scatter(contract_rows(normed2, gating_grad), 'shard', scatter_di...  636 us
    psum x1, waiting for transfers between devices, shards(): lax.psum((query_shard, key_shard, value_shard, output_shard, gate_shard,...  234 us
    reduce_scatter x1, waiting for transfers between devices, shards(): lax.psum_scatter(grad_output, 'shard', scatter_dimension=0, tiled=True)  181 us
    reduce_scatter x1, waiting for transfers between devices, shards(): lax.psum_scatter(grad_query, 'shard', scatter_dimension=0, tiled=True)  177 us
    all_gather x1, waiting for transfers between devices, shards(): lax.all_gather(down_weight, 'shard', axis=0, tiled=True)  143 us
    all_gather x1, waiting for transfers between devices, shards(): lax.all_gather(up_weight, 'shard', axis=0, tiled=True)  143 us
  transfers between devices with their start and end apart: 15, of which 11 were waited for; matrix products, arithmetic and copies ran while one was open for 9% of the time, Pallas kernels for 0%

commit v1 on v0

v1 whole, which is shorter than its diff:
```python
import jax
import jax.numpy as jnp
from jax import lax
from jax.sharding import Mesh
from jax.sharding import PartitionSpec as P

QUERY_HEADS = 32
KEY_VALUE_HEADS = 8
HEAD_WIDTH = 64


NORM_EPS = 1e-05
RESIDUAL = 0.22
SCORE_SCALE = 0.015625
ROPE_THETA = 10000000.0


def rope_tables(token_length, width):
    half_width = width // 2
    frequency = ROPE_THETA ** (-(jnp.arange(half_width, dtype=jnp.float32) * 2.0) / width)
    angles = jnp.arange(token_length, dtype=jnp.float32)[:, None] * frequency[None, :]
    cosine_table = jnp.concatenate([jnp.cos(angles), jnp.cos(angles)], axis=1)
    sine_table = jnp.concatenate([jnp.sin(angles), jnp.sin(angles)], axis=1)
    return (cosine_table, sine_table)


def apply_rotary(value_rows, cosine_table, sine_table):
    half_width = value_rows.shape[-1] // 2
    turned = jnp.concatenate([-value_rows[..., half_width:], value_rows[..., :half_width]], axis=-1)
    return value_rows * cosine_table[:, None, :] + turned * sine_table[:, None, :]


def rms_norm(value_rows, gain_vec):
    return (
        value_rows
        * lax.rsqrt(jnp.mean(value_rows * value_rows, axis=-1, keepdims=True) + NORM_EPS)
        * gain_vec
    )


def matrix_product(left_side, right_side):
    return jnp.dot(left_side, right_side, preferred_element_type=jnp.float32)


def contract_rows(left_side, right_side):
    return lax.dot_general(
        left_side, right_side, (((0,), (0,)), ((), ())), preferred_element_type=jnp.float32
    )


def contract_cols(left_side, right_side):
    return lax.dot_general(
        left_side, right_side, (((1,), (1,)), ((), ())), preferred_element_type=jnp.float32
    )


TENSOR = ("replica", "chip", "core")
INNER = ("chip", "core")
GROUP = ("slow", "chip", "core")


def gather_tokens(rows):
    return lax.all_gather(rows, TENSOR, axis=0, tiled=True)


def scatter_tokens(partial):
    return lax.psum_scatter(partial, TENSOR, scatter_dimension=0, tiled=True)


def take_half(array, axis, replicas):
    part = lax.axis_index("replica")
    return lax.dynamic_index_in_dim(array, part, axis, keepdims=False)


def shards(
    tokens,
    block_ids,
    query_weight,
    key_projection_weight,
    value_projection_weight,
    output_weight,
    gate_weight,
    up_weight,
    down_weight,
    attn_gain,
    mlp_gain,
    cotangent,
):
    token_length, width = tokens.shape
    row_count, hidden_width = gate_weight.shape
    replicas = lax.axis_size("replica")
    slow = lax.axis_size("slow")
    inner = lax.axis_size("chip") * lax.axis_size("core")
    unit = hidden_width // (slow * inner * replicas)
    local_hidden = slow * unit
    heads_per_group = QUERY_HEADS // KEY_VALUE_HEADS
    group_width = heads_per_group * HEAD_WIDTH
    query_width = query_weight.shape[1]
    key_width = key_projection_weight.shape[1]
    lanes = 128

    gain_columns = jnp.pad(
        jnp.stack([attn_gain, mlp_gain], axis=1), ((0, 0), (0, lanes - 2))
    )
    qkv_local = jnp.concatenate(
        [query_weight, key_projection_weight, value_projection_weight, gain_columns], axis=1
    )
    qkv_all = lax.all_gather(qkv_local, GROUP, axis=0, tiled=True)
    output_all = lax.all_gather(output_weight, GROUP, axis=0, tiled=True)

    def column_slices(weight):
        mine = take_half(weight.reshape(row_count, slow, inner, replicas, unit), 3, replicas)
        return mine.transpose(2, 0, 1, 3)

    both = jnp.stack([column_slices(gate_weight), column_slices(up_weight)], axis=2)
    both = lax.all_to_all(both, INNER, split_axis=0, concat_axis=0, tiled=True)
    wide_local = both.reshape(inner * row_count, 2 * local_hidden)
    down_local = take_half(down_weight.reshape(replicas, unit, width), 0, replicas)
    wide_all = lax.all_gather(wide_local, "slow", axis=0, tiled=True)
    down_all = lax.all_gather(down_local, "slow", axis=0, tiled=True)

    gains = qkv_all[:, query_width + 2 * key_width :][:, :2].T.astype(jnp.float32)
    attn_scale, mlp_scale = gains[0], gains[1]
    inputs = tokens.astype(jnp.float32)
    seq_ids = block_ids[0]
    visible = seq_ids[None, :] <= seq_ids[:, None]
    cosine_table, sine_table = rope_tables(token_length, HEAD_WIDTH)

    def rotary_flat(flat_projection, head_count):
        return apply_rotary(
            flat_projection.reshape(token_length, head_count, HEAD_WIDTH), cosine_table, sine_table
        ).reshape(token_length, head_count * HEAD_WIDTH)

    first_normed = rms_norm(inputs, attn_scale).astype(jnp.bfloat16)
    projected = matrix_product(first_normed, qkv_all)
    query_rows = rotary_flat(projected[:, :query_width], QUERY_HEADS).astype(jnp.bfloat16)
    keys_rotated = rotary_flat(
        projected[:, query_width : query_width + key_width], KEY_VALUE_HEADS
    ).astype(jnp.bfloat16)
    value_rows = projected[:, query_width + key_width : query_width + 2 * key_width].astype(
        jnp.bfloat16
    )

    def group_parts(head_cluster):
        query_part = query_rows[
            :, head_cluster * group_width : (head_cluster + 1) * group_width
        ].reshape(token_length, heads_per_group, HEAD_WIDTH)
        key_part = keys_rotated[:, head_cluster * HEAD_WIDTH : (head_cluster + 1) * HEAD_WIDTH]
        value_part = value_rows[:, head_cluster * HEAD_WIDTH : (head_cluster + 1) * HEAD_WIDTH]
        scores = SCORE_SCALE * jnp.einsum(
            "qgd,td->gqt", query_part, key_part, preferred_element_type=jnp.float32
        )
        scores = jnp.where(visible[None], scores, -1e30)
        return (query_part, key_part, value_part, scores)

    mixed_parts = []
    logsum_parts = []
    for head_cluster in range(KEY_VALUE_HEADS):
        query_part, key_part, value_part, scores = group_parts(head_cluster)
        row_max = jnp.max(scores, axis=-1, keepdims=True)
        logsum = row_max + jnp.log(jnp.sum(jnp.exp(scores - row_max), axis=-1, keepdims=True))
        attend = jnp.exp(scores - logsum).astype(jnp.bfloat16)
        mixed_parts.append(
            jnp.einsum(
                "gqt,td->qgd", attend, value_part, preferred_element_type=jnp.float32
            ).reshape(token_length, group_width)
        )
        logsum_parts.append(logsum)
    mixed = jnp.concatenate(mixed_parts, axis=1).astype(jnp.bfloat16)
    residual = inputs + RESIDUAL * matrix_product(mixed, output_all)
    normed2 = rms_norm(residual, mlp_scale).astype(jnp.bfloat16)
    grad_out = cotangent.astype(jnp.float32)
    down_in = (RESIDUAL * grad_out).astype(jnp.bfloat16)
    down_in_all = gather_tokens(down_in)
    normed2_all = gather_tokens(normed2)
    wide = matrix_product(normed2_all, wide_all)
    gating, upward = wide[:, :local_hidden], wide[:, local_hidden:]
    hidden_act = (jax.nn.silu(gating) * upward).astype(jnp.bfloat16)
    mlp_out = scatter_tokens(matrix_product(hidden_act, down_all).astype(jnp.bfloat16))
    output = (residual + RESIDUAL * mlp_out.astype(jnp.float32)).astype(jnp.bfloat16)

    hidden_grad = contract_cols(down_in_all, down_all)
    grad_down = contract_rows(hidden_act, down_in_all).astype(jnp.bfloat16)
    down_part = lax.psum_scatter(grad_down, "slow", scatter_dimension=0, tiled=True)
    _, swiglu_pull = jax.vjp(lambda first, second: jax.nn.silu(first) * second, gating, upward)
    gating_grad, upward_grad = swiglu_pull(hidden_grad)
    wide_in = jnp.concatenate(
        [gating_grad.astype(jnp.bfloat16), upward_grad.astype(jnp.bfloat16)], axis=1
    )
    normed2_grad = scatter_tokens(contract_cols(wide_in, wide_all).astype(jnp.bfloat16)).astype(
        jnp.float32
    )
    grad_wide = contract_rows(normed2_all, wide_in).astype(jnp.bfloat16)
    wide_part = lax.psum_scatter(grad_wide, "slow", scatter_dimension=0, tiled=True)
    wide_part = lax.all_to_all(
        wide_part.reshape(inner, row_count, 2, slow, unit),
        INNER,
        split_axis=0,
        concat_axis=0,
        tiled=True,
    )
    wide_full = lax.all_gather(wide_part, "replica", axis=0, tiled=False)
    wide_full = wide_full.transpose(3, 2, 4, 1, 0, 5).reshape(2, row_count, hidden_width)
    gate_shard = wide_full[0].astype(jnp.float32)
    up_shard = wide_full[1].astype(jnp.float32)
    down_shard = lax.all_gather(down_part, "replica", axis=0, tiled=True).astype(jnp.float32)

    _, norm2_pull = jax.vjp(rms_norm, residual, mlp_scale)
    residual_part, grad_mlp_gain = norm2_pull(normed2_grad)
    residual_grad = grad_out + residual_part
    attn_in = (RESIDUAL * residual_grad).astype(jnp.bfloat16)
    grad_output = contract_rows(mixed, attn_in)
    mixed_grad = contract_cols(attn_in, output_all).astype(jnp.bfloat16)
    query_grads = []
    key_grads = []
    value_grads = []
    for head_cluster in range(KEY_VALUE_HEADS):
        query_part, key_part, value_part, scores = group_parts(head_cluster)
        attend = jnp.exp(scores - logsum_parts[head_cluster])
        grad_part = mixed_grad[
            :, head_cluster * group_width : (head_cluster + 1) * group_width
        ].reshape(token_length, heads_per_group, HEAD_WIDTH)
        attend_grad = jnp.einsum(
            "qgd,td->gqt", grad_part, value_part, preferred_element_type=jnp.float32
        )
        row_delta = jnp.sum(attend * attend_grad, axis=-1, keepdims=True)
        score_grad = (attend * (attend_grad - row_delta)).astype(jnp.bfloat16)
        query_grads.append(
            (
                SCORE_SCALE
                * jnp.einsum(
                    "gqt,td->qgd", score_grad, key_part, preferred_element_type=jnp.float32
                )
            ).reshape(token_length, group_width)
        )
        key_grads.append(
            SCORE_SCALE
            * jnp.einsum("gqt,qgd->td", score_grad, query_part, preferred_element_type=jnp.float32)
        )
        value_grads.append(
            jnp.einsum(
                "gqt,qgd->td",
                attend.astype(jnp.bfloat16),
                grad_part,
                preferred_element_type=jnp.float32,
            )
        )
    queries_grad = jnp.concatenate(query_grads, axis=1)
    keys_grad = jnp.concatenate(key_grads, axis=1)
    value_lin_grad = jnp.concatenate(value_grads, axis=1).astype(jnp.bfloat16)
    _, query_rope_pull = jax.vjp(
        lambda flat_projection: rotary_flat(flat_projection, QUERY_HEADS),
        jnp.zeros((token_length, QUERY_HEADS * HEAD_WIDTH), jnp.float32),
    )
    _, key_rope_pull = jax.vjp(
        lambda flat_projection: rotary_flat(flat_projection, KEY_VALUE_HEADS),
        jnp.zeros((token_length, KEY_VALUE_HEADS * HEAD_WIDTH), jnp.float32),
    )
    query_lin_grad = query_rope_pull(queries_grad)[0].astype(jnp.bfloat16)
    key_lin_grad = key_rope_pull(keys_grad)[0].astype(jnp.bfloat16)
    qkv_in = jnp.concatenate(
        [
            query_lin_grad,
            key_lin_grad,
            value_lin_grad,
            jnp.zeros((token_length, lanes), jnp.bfloat16),
        ],
        axis=1,
    )
    grad_qkv = contract_rows(first_normed, qkv_in).astype(jnp.bfloat16)
    normed1_grad = contract_cols(qkv_in, qkv_all)
    _, norm1_pull = jax.vjp(rms_norm, inputs, attn_scale)
    input_part, grad_attn_gain = norm1_pull(normed1_grad)
    input_grad = residual_grad + input_part
    gain_grads = jnp.stack([grad_attn_gain, grad_mlp_gain], axis=1).astype(jnp.bfloat16)
    grad_qkv = lax.dynamic_update_slice(
        grad_qkv, gain_grads, (0, query_width + 2 * key_width)
    )
    output_shard = lax.psum_scatter(
        grad_output.astype(jnp.bfloat16), GROUP, scatter_dimension=0, tiled=True
    )
    qkv_shard = lax.psum_scatter(grad_qkv, GROUP, scatter_dimension=0, tiled=True)

    def replica_sum(part):
        total = part.astype(jnp.float32)
        for shift in range(1, replicas):
            pairs = [(i, (i + shift) % replicas) for i in range(replicas)]
            total = total + lax.ppermute(part, "replica", pairs).astype(jnp.float32)
        return total

    output_shard = replica_sum(output_shard)
    qkv_shard = replica_sum(qkv_shard)
    query_shard = qkv_shard[:, :query_width]
    key_shard = qkv_shard[:, query_width : query_width + key_width]
    value_shard = qkv_shard[:, query_width + key_width : query_width + 2 * key_width]
    attn_gain_shard = qkv_shard[:, query_width + 2 * key_width]
    mlp_gain_shard = qkv_shard[:, query_width + 2 * key_width + 1]
    return (
        output,
        input_grad,
        query_shard,
        key_shard,
        value_shard,
        output_shard,
        gate_shard,
        up_shard,
        down_shard,
        attn_gain_shard,
        mlp_gain_shard,
    )


def solution(mesh):
    replicas, shard_count = mesh.shape["replica"], mesh.shape["shard"]
    inner = KEY_VALUE_HEADS // replicas
    cores = 2
    split_mesh = Mesh(
        mesh.devices.reshape(replicas, shard_count // inner, inner // cores, cores),
        ("replica", "slow", "chip", "core"),
    )
    everyone = P(("replica", "slow", "chip", "core"), None)
    sharded = P(GROUP, None)
    vector = P(GROUP)
    return jax.shard_map(
        shards,
        mesh=split_mesh,
        in_specs=(everyone, everyone) + (sharded,) * 7 + (vector, vector, everyone),
        out_specs=(everyone, everyone) + (sharded,) * 7 + (vector, vector),
        check_vma=False,
    )
```

time: 3750 us -> 1520 us (0.41)
  waiting for transfers between devices: 3030 us -> 824 us
  blocking collectives: 106 us -> 28.9 us
  local copies, waits for them, and re-layouts: 75.1 us -> 128 us
  matrix products: 453 us -> 414 us
    reduce_scatter x7 -> x6, waiting for transfers between devices: 2270 us -> 450 us  [the longest x2 203 us: scatter_tokens(): return lax.psum_scatter(partial, TENSOR, scatter_dimension=0, tiled=True)]
    psum x1 -> x0, waiting for transfers between devices: 234 us -> none  [shards(): lax.psum((query_shard, key_shard, value_shard, output_shard, gate_shard,...]
    all_gather x7 -> x8, waiting for transfers between devices: 527 us -> 348 us  [the longest x2 180 us: gather_tokens(): return lax.all_gather(rows, TENSOR, axis=0, tiled=True)]
    unnamed x1 -> x0, blocking collectives: 59.5 us -> none
    all_gather x2 -> x0, blocking collectives: 40.6 us -> none  [the longest x1 23.1 us: shards(): lax.all_gather(attn_gain, 'shard', axis=0, tiled=True)]
    dot_general x7 -> x4, matrix products: 118 us -> 90.9 us  [contract_rows(): lax.dot_general(left_side, right_side, (((0,), (0,)), ((), ())), preferre...]
    dot_general x7 -> x4, matrix products: 114 us -> 102 us  [contract_cols(): lax.dot_general(left_side, right_side, (((1,), (1,)), ((), ())), preferre...]
    dot_general x7 -> x4, matrix products: 103 us -> 91.7 us  [matrix_product(): return jnp.dot(left_side, right_side, preferred_element_type=jnp.float32)]
  transfers between devices with their start and end apart: 15 -> 17, of which waited for: 11 -> 11; matrix products, arithmetic and copies ran while one was open for 9% -> 37% of each run, Pallas kernels for 0% -> 0%
where the time goes in v1:
time: 1520 us; the launch traced here: 1510 us
  waiting for transfers between devices  824 us (54%)
  matrix products  414 us (27%)
  local copies, waits for them, and re-layouts  128 us (8%)
  other arithmetic  94.5 us (6%)
  blocking collectives  28.9 us (2%)
  between operations  15.8 us (1%)
    reduce_scatter x2, waiting for transfers between devices, scatter_tokens(): return lax.psum_scatter(partial, TENSOR, scatter_dimension=0, tiled=True)  203 us
    all_gather x2, waiting for transfers between devices, gather_tokens(): return lax.all_gather(rows, TENSOR, axis=0, tiled=True)  180 us
    reduce_scatter x1, waiting for transfers between devices, shards(): lax.psum_scatter(grad_qkv, GROUP, scatter_dimension=0, tiled=True)  137 us
    reduce_scatter x1, waiting for transfers between devices, shards(): lax.psum_scatter(grad_wide, 'slow', scatter_dimension=0, tiled=True)  110 us
    dot_general x4, matrix products, contract_cols(): lax.dot_general(left_side, right_side, (((1,), (1,)), ((), ())), preferre...  102 us
    dot_general x4, matrix products, matrix_product(): return jnp.dot(left_side, right_side, preferred_element_type=jnp.float32)  91.7 us
    dot_general x4, matrix products, contract_rows(): lax.dot_general(left_side, right_side, (((0,), (0,)), ((), ())), preferre...  90.9 us
    all_gather x1, waiting for transfers between devices, shards(): wide_all = lax.all_gather(wide_local, 'slow', axis=0, tiled=True)  79.5 us
  transfers between devices with their start and end apart: 17, of which 11 were waited for; matrix products, arithmetic and copies ran while one was open for 37% of the time, Pallas kernels for 0%

profile of v1, /device:TPU:0, one launch (start us, length us, event | category | flops | bytes accessed | tf_op | source)
XLA Modules:
  0.0 1513.3 jit_solution(9807104447003634390)
XLA Ops:
  11.1 4.1 copy.355
  15.2 4.1 copy.357
  19.2 2.8 constant_dynamic-slice_fusion.1
  28.8 4.5 all-to-all-start
  37.7 5.4 copy.320
  45.4 15.6 %all-to-all-done = bf16[4,128,2,4,256]{4,1,3,2,0:T(8,128)(2,1)} async-done(((bf16[4,128,2,4,256]{4,1,3,2,0:T(8,128)(2,1)}), bf16[4,128,2,4,256]{4,1,3,2,0:T(8,128)(2,1)}, u32[]{:S(2)}, u32[]{:S(2)}) %all-to-all-start) | async-done | bytes 2097184 | tf_op jit(solution)/shard_map/all_to_all | solution.py:116
  61.0 4.5 copy.360
  65.6 4.4 reshape.361
  70.5 48.9 %all-gather.11.cloned.1.call-done = bf16[2048,3200]{1,0:T(8,128)(2,1)} async-done(((bf16[128,3200]{1,0:T(8,128)(2,1)}), bf16[2048,3200]{1,0:T(8,128)(2,1)}) %all-gather.11.cloned.1.call-update) | async-done | bytes 13107216 | tf_op jit(solution)/shard_map/all_gather | solution.py:108
  121.5 13.0 fusion.159
  143.2 5.3 copy.321
  153.8 5.9 copy.322
  159.7 5.9 add_convert_fusion.2
  173.9 3.8 fusion.115
  185.9 2.8 fusion.125
  193.6 7.5 fusion.60
  201.4 10.2 exponential_reduce_fusion
  211.6 3.6 convolution_convert_fusion.13
  216.0 7.2 exponential_reduce_fusion.1
  223.3 3.5 convolution_convert_fusion.12
  245.5 10.4 multiply_reduce_fusion
  260.9 3.5 fusion.13
  264.5 79.5 %all-gather.17.cloned.1.call-done = bf16[2048,2048]{1,0:T(8,128)(2,1)} async-done(((bf16[512,2048]{1,0:T(8,128)(2,1)}), bf16[2048,2048]{1,0:T(8,128)(2,1)}) %all-gather.17.cloned.1.call-update) | async-done | bytes 8388624 | tf_op jit(solution)/shard_map/all_gather | solution.py:119
  344.0 90.3 %all-gather.15.cloned.1.call-done = bf16[4096,2048]{1,0:T(8,128)(2,1)} async-done(((bf16[512,2048]{1,0:T(8,128)(2,1)}), bf16[4096,2048]{1,0:T(8,128)(2,1)}) %all-gather.15.cloned.1.call-update) | async-done | bytes 16777232 | tf_op jit(solution)/shard_map/all_gather | solution.py:63
  434.3 43.5 %fusion.160 = f32[4096,2048]{0,1:T(8,128)} fusion(bf16[4096,2048]{1,0:T(8,128)(2,1)} %all-gather.15.cloned.1.call-done, bf16[2048,2048]{1,0:T(8,128)(2,1)} %all-gather.17.cloned.1.call-done), kind=kOutput, calls=%fused_computation.312 | convolution fusion | flops 34359738368 | bytes 58720256 | tf_op jit(solution)/shard_map/dot_general | solution.py:42
  477.8 39.3 %all-gather.23.cloned.1.call-done = bf16[1,1024,2048]{2,1,0:T(8,128)(2,1)} async-done(((bf16[1,256,2048]{2,1,0:T(8,128)(2,1)}), bf16[1,1024,2048]{2,1,0:T(8,128)(2,1)}) %all-gather.23.cloned.1.call-update) | async-done | bytes 4194320 | tf_op jit(solution)/shard_map/all_gather | solution.py:120
  517.0 90.0 %all-gather.19.cloned.1.call-done = bf16[4096,2048]{1,0:T(8,128)(2,1)} async-done(((bf16[512,2048]{1,0:T(8,128)(2,1)}), bf16[4096,2048]{1,0:T(8,128)(2,1)}) %all-gather.19.cloned.1.call-update) | async-done | bytes 16777232 | tf_op jit(solution)/shard_map/all_gather | solution.py:63
  607.0 36.2 %fusion.2 = (bf16[4096,1024]{0,1:T(8,128)(2,1)}, bf16[4096,1024]{0,1:T(8,128)(2,1)}, bf16[4096,1024]{0,1:T(8,128)(2,1)}) fusion(f32[4096,2048]{0,1:T(8,128)} %fusion.160, bf16[4096,2048]{1,0:T(8,128)(2,1)} %all-gather.19.cloned.1.call-done, bf16[1,1024,2048]{2,1,0:T(8,128)(2,1)} %all-gather.23.cloned.1.call-done), kind=kOutput, calls=%fused_computation.3 | convolution fusion | flops 17246978048 | bytes 79691776 | tf_op jit(solution)/shard_map/dot_general | solution.py:52
  643.2 23.7 %convolution_convert_fusion.4 = bf16[1024,2048]{1,0:T(8,128)(2,1)} fusion(bf16[4096,1024]{0,1:T(8,128)(2,1)} %get-tuple-element.45, bf16[4096,2048]{1,0:T(8,128)(2,1)} %all-gather.19.cloned.1.call-done), kind=kOutput, calls=%fused_computation.112 | convolution fusion | flops 17181966336 | bytes 29360128 | tf_op jit(solution)/shard_map/dot_general | solution.py:46
  667.0 46.1 %fusion.5 = bf16[2048,2048]{1,0:T(8,128)(2,1)} fusion(bf16[4096,2048]{1,0:T(8,128)(2,1)} %all-gather.15.cloned.1.call-done, bf16[4096,1024]{0,1:T(8,128)(2,1)} %get-tuple-element.44, bf16[4096,1024]{0,1:T(8,128)(2,1)} %get-tuple-element.43), kind=kOutput, calls=%fused_computation.18 | convolution fusion | flops 34397487104 | bytes 41943040 | tf_op jit(solution)/shard_map/dot_general | solution.py:46
  713.1 42.5 %convolution_convert_fusion.2 = bf16[4096,2048]{1,0:T(8,128)(2,1)} fusion(bf16[2048,2048]{1,0:T(8,128)(2,1)} %all-gather.17.cloned.1.call-done, bf16[4096,1024]{0,1:T(8,128)(2,1)} %get-tuple-element.44, bf16[4096,1024]{0,1:T(8,128)(2,1)} %get-tuple-element.43), kind=kOutput, calls=%fused_computation.11 | convolution fusion | flops 34401681408 | bytes 41943040 | tf_op jit(solution)/shard_map/dot_general | solution.py:52
  755.8 24.8 %convolution_convert_fusion.1 = bf16[4096,2048]{1,0:T(8,128)(2,1)} fusion(bf16[4096,1024]{0,1:T(8,128)(2,1)} %get-tuple-element.45, bf16[1,1024,2048]{2,1,0:T(8,128)(2,1)} %all-gather.23.cloned.1.call-done), kind=kOutput, calls=%fused_computation.10 | convolution fusion | flops 17188257792 | bytes 29360128 | tf_op jit(solution)/shard_map/dot_general | solution.py:42
  781.4 110.0 %reduce-scatter.15.cloned.1.call-done = bf16[512,2048]{1,0:T(8,128)(2,1)} async-done(((bf16[2048,2048]{1,0:T(8,128)(2,1)}), bf16[512,2048]{1,0:T(8,128)(2,1)}) %reduce-scatter.15.cloned.1.call-update) | async-done | bytes 2097168 | tf_op jit(solution)/shard_map/reduce_scatter | solution.py:194
  891.4 3.3 reshape.372
  895.2 28.9 %all_to_all.10 = bf16[4,128,2,4,256]{4,1,3,2,0:T(8,128)(2,1)} all-to-all(bf16[4,128,2,4,256]{4,1,3,2,0:T(8,128)(2,1)S(1)} %copy.410), channel_id=1, replica_groups=mesh['replica'=2,'slow'=4,'chip'=2,'core'=2] {'chip','core'}, dimensions={0} | all-to-all | bytes 4194304 | tf_op jit(solution)/shard_map/all_to_all | solution.py:195
  924.2 87.6 %reduce-scatter.9.cloned.1.call-done = bf16[512,2048]{1,0:T(8,128)(2,1)} async-done(((bf16[4096,2048]{1,0:T(8,128)(2,1)}), bf16[512,2048]{1,0:T(8,128)(2,1)}) %reduce-scatter.9.cloned.1.call-update) | async-done | bytes 2097168 | tf_op jit(solution)/shard_map/reduce_scatter | solution.py:67
  1011.8 4.3 fusion.14
  1016.1 115.3 %reduce-scatter.7.cloned.1.call-done = bf16[512,2048]{1,0:T(8,128)(2,1)} async-done(((bf16[4096,2048]{1,0:T(8,128)(2,1)}), bf16[512,2048]{1,0:T(8,128)(2,1)}) %reduce-scatter.7.cloned.1.call-update) | async-done | bytes 2097168 | tf_op jit(solution)/shard_map/reduce_scatter | solution.py:67
  1131.4 5.5 convert_add_fusion.1
  1137.0 10.2 convolution_convert_fusion.5
  1150.0 3.7 fusion.114
  1153.7 3.7 fusion.116
  1157.5 3.6 fusion.118
  1161.1 3.7 fusion.120
  1164.8 3.9 fusion.122
  1170.7 5.1 fusion.21
  1175.8 20.2 %fusion.18 = (f32[4,512]{1,0:T(4,128)S(1)}, f32[4,512]{1,0:T(4,128)S(1)}, f32[4,512]{1,0:T(4,128)S(1)}, f32[4,512]{1,0:T(4,128)S(1)}, f32[4,512]{1,0:T(4,128)S(1...) fusion(f32[512,512,4]{1,0,2:T(8,128)} %get-tuple-element.88, f32[4,512]{1,0:T(4,128)S(1)} %copy-done.97, ...), kind=kOutput, calls=%fused_computation.41 | convolution fusion | flops 165662720 | bytes 51085312 | tf_op jit(solution)/shard_map/qgd,td->gqt/dot_general | solution.py:223
  1196.0 14.3 fusion.23
  1211.8 13.9 fusion.20
  1229.5 8.4 convolution_convert_fusion.3
  1238.8 3.4 fusion.85
  1242.2 3.2 fusion.87
  1279.5 13.3 fusion.11
  1293.1 12.8 convolution_convert_fusion
  1305.9 5.2 dynamic_update_slice.3
  1311.2 4.1 convert_element_type.221
  1315.3 5.0 slice_convert_fusion
  1320.3 5.3 copy.412
  1325.6 6.4 reshape.374
  1332.1 7.6 copy.411
  1339.6 6.4 reshape.373
  1347.5 136.7 %reduce-scatter.11.cloned.1.call-done = bf16[128,3200]{1,0:T(8,128)(2,1)} async-done(((bf16[2048,3200]{1,0:T(8,128)(2,1)}), bf16[128,3200]{1,0:T(8,128)(2,1)}) %reduce-scatter.11.cloned.1.call-update) | async-done | bytes 819216 | tf_op jit(solution)/shard_map/reduce_scatter | solution.py:282
  1485.6 7.2 fusion.15
  1494.0 9.6 collective-permute-done
  (372 shorter events, 133.0 us)
Async XLA Ops:
  7.2 252.6 %copy-start = (bf16[512,2048]{1,0:T(8,128)(2,1)S(1)}, bf16[512,2048]{1,0:T(8,128)(2,1)}, u32[]{:S(2)}) copy-start(bf16[512,2048]{1,0:T(8,128)(2,1)} %param.20) | copy-start | bytes 6291460
  7.2 112.2 %all-gather.11.cloned.1.call-start = ((), (), s32[]{:S(2)}) async-start(), calls=%async_computation.8 | async-start | bytes 13926400 | tf_op jit(solution)/shard_map/all_gather | solution.py:108
  10.4 235.2 %all-gather.13.cloned.1.call-start = ((), (), s32[]{:S(2)}) async-start(), calls=%async_computation.9 | async-start | bytes 8912896 | tf_op jit(solution)/shard_map/all_gather | solution.py:109
  28.8 32.2 %all-to-all-start = ((bf16[4,128,2,4,256]{4,1,3,2,0:T(8,128)(2,1)}), bf16[4,128,2,4,256]{4,1,3,2,0:T(8,128)(2,1)}, u32[]{:S(2)}, u32[]{:S(2)}) async-start(bf16[4,128,2,4,256]{4,1,3,2,0:T(8,128)(2,1)} %copy.359), calls=%async_computation | async-start | bytes 4194304 | tf_op jit(solution)/shard_map/all_to_all | solution.py:116
  33.3 310.7 %all-gather.17.cloned.1.call-start = ((), (), s32[]{:S(2)}) async-start(), calls=%async_computation.11 | async-start | bytes 10485760 | tf_op jit(solution)/shard_map/all_gather | solution.py:119
  33.7 9.4 copy-start.44
  33.7 117.5 %copy-start.42 = (f32[512,64]{0,1:T(8,128)}, f32[512,64]{0,1:T(8,128)S(1)}, u32[]{:S(2)}) copy-start(f32[512,64]{0,1:T(8,128)S(1)} %get-tuple-element.98) | copy-start | bytes 393220
  37.7 7.5 copy-start.104
  45.2 24.9 %copy-start.102 = (f32[512]{0:T(512)}, f32[512]{0:T(512)S(1)}, u32[]{:S(2)}) copy-start(f32[512]{0:T(512)S(1)} %fusion.16) | copy-start | bytes 6148
  45.2 76.3 %copy-start.107 = (f32[512]{0:T(512)}, f32[512]{0:T(512)S(1)}, u32[]{:S(2)}) copy-start(f32[512]{0:T(512)S(1)} %fusion.132) | copy-start | bytes 6148
  45.4 197.2 %copy-start.35 = (pred[512,512]{0,1:T(8,128)(4,1)}, pred[512,512]{0,1:T(8,128)(4,1)S(1)}, u32[]{:S(2)}) copy-start(pred[512,512]{0,1:T(8,128)(4,1)S(1)} %broadcast_compare_fusion) | copy-start | bytes 786436
  70.0 364.2 %all-gather.15.cloned.1.call-start = ((), (), s32[]{:S(2)}) async-start(), calls=%async_computation.10 | async-start | bytes 18874368 | tf_op jit(solution)/shard_map/all_gather | solution.py:63
  121.4 13.0 copy-start.98
  121.4 134.5 %copy-start.80 = (f32[2048]{0:T(1024)}, f32[2048]{0:T(1024)S(1)}, u32[]{:S(2)}) copy-start(f32[2048]{0:T(1024)S(1)} %get-tuple-element.17) | copy-start | bytes 24580
  166.8 19.1 %copy-start.46 = (bf16[512,256]{0,1:T(8,128)(2,1)}, bf16[512,256]{0,1:T(8,128)(2,1)S(1)}, u32[]{:S(2)}) copy-start(bf16[512,256]{0,1:T(8,128)(2,1)S(1)} %copy.343) | copy-start | bytes 786436
  168.0 15.2 %copy-start.48 = (bf16[512,256]{0,1:T(8,128)(2,1)}, bf16[512,256]{0,1:T(8,128)(2,1)S(1)}, u32[]{:S(2)}) copy-start(bf16[512,256]{0,1:T(8,128)(2,1)S(1)} %copy.339) | copy-start | bytes 786436
  173.9 27.2 %copy-start.37 = (bf16[512,512]{1,0:T(8,128)(2,1)}, bf16[512,512]{1,0:T(8,128)(2,1)S(1)}, u32[]{:S(2)}) copy-start(bf16[512,512]{1,0:T(8,128)(2,1)S(1)} %add_convert_fusion.4) | copy-start | bytes 1572868
  189.8 11.3 copy-start.54
  191.0 10.1 copy-start.52
  192.9 8.2 copy-start.10
  193.6 45.6 %copy-start.5 = (f32[512,512,4]{1,0,2:T(8,128)}, f32[512,512,4]{1,0,2:T(8,128)S(1)}, u32[]{:S(2)}) copy-start(f32[512,512,4]{1,0,2:T(8,128)S(1)} %fusion.127) | copy-start | bytes 12582916
  193.6 7.5 copy-start.2
  193.6 7.6 copy-start.8
  193.6 7.8 copy-start.64
  211.6 11.6 copy-start.86
  242.6 13.3 copy-start.96
  259.7 257.3 %all-gather.23.cloned.1.call-start = ((), (), s32[]{:S(2)}) async-start(), calls=%async_computation.20 | async-start | bytes 5242880 | tf_op jit(solution)/shard_map/all_gather | solution.py:120
  260.9 346.1 %all-gather.19.cloned.1.call-start = ((), (), s32[]{:S(2)}) async-start(), calls=%async_computation.13 | async-start | bytes 18874368 | tf_op jit(solution)/shard_map/all_gather | solution.py:63
  264.4 516.3 %reduce-scatter.17.cloned.1.call-start = ((), (), s32[]{:S(2)}) async-start(), calls=%async_computation.18 | async-start | bytes 5242880 | tf_op jit(solution)/shard_map/reduce_scatter | solution.py:184
  666.9 224.5 %reduce-scatter.15.cloned.1.call-start = ((), (), s32[]{:S(2)}) async-start(), calls=%async_computation.17 | async-start | bytes 10485760 | tf_op jit(solution)/shard_map/reduce_scatter | solution.py:194
  713.1 298.7 %reduce-scatter.9.cloned.1.call-start = ((), (), s32[]{:S(2)}) async-start(), calls=%async_computation.14 | async-start | bytes 18874368 | tf_op jit(solution)/shard_map/reduce_scatter | solution.py:67
  755.7 375.7 %reduce-scatter.7.cloned.1.call-start = ((), (), s32[]{:S(2)}) async-start(), calls=%async_computation.12 | async-start | bytes 18874368 | tf_op jit(solution)/shard_map/reduce_scatter | solution.py:67
  780.6 530.5 %all-gather.21.cloned.1.call-start = ((), (), s32[]{:S(2)}) async-start(), calls=%async_computation.19 | async-start | bytes 3145728 | tf_op jit(solution)/shard_map/all_gather | solution.py:206
  781.4 533.9 %all-gather.25.cloned.1.call-start = ((), (), s32[]{:S(2)}) async-start(), calls=%async_computation.21 | async-start | bytes 6291456 | tf_op jit(solution)/shard_map/all_gather | solution.py:202
  895.2 116.6 %copy-start.81 = (f32[2048]{0:T(1024)S(1)}, f32[2048]{0:T(1024)}, u32[]{:S(2)}) copy-start(f32[2048]{0:T(1024)} %copy-done.80) | copy-start | bytes 24580
  895.2 116.6 %copy-start.101 = (f32[512]{0:T(512)S(1)}, f32[512]{0:T(512)}, u32[]{:S(2)}) copy-start(f32[512]{0:T(512)} %copy-done.100) | copy-start | bytes 6148
  924.1 92.0 %copy-start.106 = (f32[512]{0:T(512)S(1)}, f32[512]{0:T(512)}, u32[]{:S(2)}) copy-start(f32[512]{0:T(512)} %copy-done.105) | copy-start | bytes 6148
  924.2 421.9 %reduce-scatter.13.cloned.1.call-start = ((), (), s32[]{:S(2)}) async-start(), calls=%async_computation.16 | async-start | bytes 8912896 | tf_op jit(solution)/shard_map/reduce_scatter | solution.py:279
  1011.8 119.6 %copy-start.39 = (bf16[512,2048]{1,0:T(8,128)(2,1)S(1)}, bf16[512,2048]{1,0:T(8,128)(2,1)}, u32[]{:S(2)}) copy-start(bf16[512,2048]{1,0:T(8,128)(2,1)} %reduce-scatter.9.cloned.1.call-done) | copy-start | bytes 6291460
  1137.0 10.2 copy-start.33
  1147.5 23.1 %copy-start.62 = (bf16[512,256]{0,1:T(8,128)(2,1)}, bf16[512,256]{0,1:T(8,128)(2,1)S(1)}, u32[]{:S(2)}) copy-start(bf16[512,256]{0,1:T(8,128)(2,1)S(1)} %copy.385) | copy-start | bytes 786436
  1147.6 28.1 %copy-start.60 = (bf16[512,256]{0,1:T(8,128)(2,1)}, bf16[512,256]{0,1:T(8,128)(2,1)S(1)}, u32[]{:S(2)}) copy-start(bf16[512,256]{0,1:T(8,128)(2,1)S(1)} %copy.389) | copy-start | bytes 786436
  1149.5 11.6 copy-start.70
  1149.6 7.8 copy-start.72
  1149.8 7.7 copy-start.74
  1150.0 7.5 copy-start.76
  1157.5 7.3 copy-start.68
  1161.1 7.6 copy-start.66
  1196.0 14.3 copy-start.58
  1196.0 15.7 %copy-start.11 = (f32[512,512,4]{1,0,2:T(8,128)S(1)}, f32[512,512,4]{1,0,2:T(8,128)}, u32[]{:S(2)}) copy-start(f32[512,512,4]{1,0,2:T(8,128)} %fusion.121) | copy-start | bytes 12582916
  1210.4 15.3 %copy-start.25 = (bf16[4,512,512]{1,2,0:T(8,128)(2,1)}, bf16[4,512,512]{1,2,0:T(8,128)(2,1)S(1)}, u32[]{:S(2)}) copy-start(bf16[4,512,512]{1,2,0:T(8,128)(2,1)S(1)} %get-tuple-element.81) | copy-start | bytes 6291460
  1211.8 13.9 copy-start.65
  1211.8 15.3 %copy-start.57 = (bf16[512,256]{0,1:T(8,128)(2,1)S(1)}, bf16[512,256]{0,1:T(8,128)(2,1)}, u32[]{:S(2)}) copy-start(bf16[512,256]{0,1:T(8,128)(2,1)} %copy.331) | copy-start | bytes 786436
  1225.6 12.2 copy-start.30
  1237.8 7.5 copy-start.47
  1237.9 8.9 copy-start.21
  1237.9 246.3 %reduce-scatter.11.cloned.1.call-start = ((), (), s32[]{:S(2)}) async-start(), calls=%async_computation.15 | async-start | bytes 13926400 | tf_op jit(solution)/shard_map/reduce_scatter | solution.py:282
  1238.1 7.3 copy-start.22
  1238.1 8.7 copy-start.55
  1279.5 13.3 copy-start.59
  1346.1 146.8 %collective-permute-start.1 = (bf16[128,2048]{1,0:T(8,128)(2,1)}, bf16[128,2048]{1,0:T(8,128)(2,1)S(1)}, u32[]{:S(2)}, u32[]{:S(2)}) collective-permute-start(bf16[128,2048]{1,0:T(8,128)(2,1)} %reduce-scatter.13.cloned.1.call-done), channel_id=1, source_target_pairs={{0,16},{16,0},{1,17},{17,1},{2,18},{18,2},{3,19},{19,3},{4,20},{20... | collective-permute-start | bytes 1572872 | tf_op jit(solution)/shard_map/ppermute | solution.py:288
  1484.2 19.4 %collective-permute-start = (bf16[128,3200]{1,0:T(8,128)(2,1)}, bf16[128,3200]{1,0:T(8,128)(2,1)S(1)}, u32[]{:S(2)}, u32[]{:S(2)}) collective-permute-start(bf16[128,3200]{1,0:T(8,128)(2,1)} %reduce-scatter.11.cloned.1.call-done), channel_id=1, source_target_pairs={{0,16},{16,0},{1,17},{17,1},{2,18},{18,2},{3,19},{19,3},{4,20},{20... | collective-permute-start | bytes 2457608 | tf_op jit(solution)/shard_map/ppermute | solution.py:288
  1485.6 17.9 %copy-start.78 = (bf16[128,3200]{1,0:T(8,128)(2,1)S(1)}, bf16[128,3200]{1,0:T(8,128)(2,1)}, u32[]{:S(2)}) copy-start(bf16[128,3200]{1,0:T(8,128)(2,1)} %reduce-scatter.11.cloned.1.call-done) | copy-start | bytes 2457604
  1485.6 20.7 %copy-start.1 = (bf16[512,2048]{1,0:T(8,128)(2,1)S(1)}, bf16[512,2048]{1,0:T(8,128)(2,1)}, u32[]{:S(2)}) copy-start(bf16[512,2048]{1,0:T(8,128)(2,1)} %param.20) | copy-start | bytes 6291460
  (62 other events, 239.5 us)
Sparse Core Ops, SparseCore 0:
  10.9 108.5 all-gather.10
  121.6 72.5 all-gather.12
  195.8 148.1 all-gather.16
  346.3 87.9 all-gather.14
  436.3 80.7 all-gather.22
  518.8 88.2 all-gather.18
  667.1 76.7 reduce-scatter.16
  746.2 145.1 reduce-scatter.14
  895.0 116.7 reduce-scatter.8
  1015.2 116.1 reduce-scatter.6
  1133.0 33.0 all-gather.20
  1167.5 56.7 all-gather.24
  1238.0 103.9 reduce-scatter.12
  1345.9 138.2 reduce-scatter.10

commit v2 on v1

v2 whole, which is shorter than its diff:
```python
import jax
import jax.numpy as jnp
from jax import lax
from jax.experimental import pallas as pl
from jax.experimental.pallas import tpu as pltpu
from jax.sharding import Mesh
from jax.sharding import PartitionSpec as P


QUERY_HEADS = 32
KEY_VALUE_HEADS = 8
HEAD_WIDTH = 64


NORM_EPS = 1e-05
RESIDUAL = 0.22
SCORE_SCALE = 0.015625
ROPE_THETA = 10000000.0


def rope_tables(token_length, width):
    half_width = width // 2
    frequency = ROPE_THETA ** (-(jnp.arange(half_width, dtype=jnp.float32) * 2.0) / width)
    angles = jnp.arange(token_length, dtype=jnp.float32)[:, None] * frequency[None, :]
    cosine_table = jnp.concatenate([jnp.cos(angles), jnp.cos(angles)], axis=1)
    sine_table = jnp.concatenate([jnp.sin(angles), jnp.sin(angles)], axis=1)
    return (cosine_table, sine_table)


def rms_norm(value_rows, gain_vec):
    return (
        value_rows
        * lax.rsqrt(jnp.mean(value_rows * value_rows, axis=-1, keepdims=True) + NORM_EPS)
        * gain_vec
    )


def matrix_product(left_side, right_side):
    return jnp.dot(left_side, right_side, preferred_element_type=jnp.float32)


def contract_rows(left_side, right_side):
    return lax.dot_general(
        left_side, right_side, (((0,), (0,)), ((), ())), preferred_element_type=jnp.float32
    )


def contract_cols(left_side, right_side):
    return lax.dot_general(
        left_side, right_side, (((1,), (1,)), ((), ())), preferred_element_type=jnp.float32
    )


GROUP = ("slow", "chip", "core")
LANES = 128


def swap(value, axis):
    return lax.ppermute(value, axis, [(0, 1), (1, 0)])


def order(first_is_zero, one, other):
    return jnp.where(first_is_zero, one, other), jnp.where(first_is_zero, other, one)


def add_parts(*parts):
    total = parts[0].astype(jnp.float32)
    for part in parts[1:]:
        total = total + part.astype(jnp.float32)
    return total


def gather_tokens(rows):
    half = rows.shape[0] // 2
    beside = swap(rows, "chip")
    across = swap(rows, "replica")
    corner_low = swap(beside[:half], "replica")
    corner_high = swap(across[half:], "chip")
    plane = [rows, beside, across, corner_low, corner_high]
    return plane, [swap(part, "core") for part in plane]


def narrow(value):
    return value.astype(jnp.bfloat16)


def scatter_pieces(mine, partner):
    partner = [swap(part, "core") for part in partner]
    own, beside, across, corner = (
        add_parts(keep, send) for keep, send in zip(mine, partner, strict=True)
    )
    half = own.shape[0] // 2
    corner = narrow(corner)
    beside_low = swap(narrow(beside[:half]), "chip")
    across_high = swap(narrow(across[half:]), "replica")
    corner_low = swap(corner[:half], "chip")
    corner_high = swap(corner[half:], "replica")
    across_low = narrow(add_parts(narrow(across[:half]), corner_low))
    beside_high = narrow(add_parts(narrow(beside[half:]), corner_high))
    across_low = swap(across_low, "replica")
    beside_high = swap(beside_high, "chip")
    return jnp.concatenate(
        [
            add_parts(own[:half], beside_low, across_low),
            add_parts(own[half:], across_high, beside_high),
        ],
        axis=0,
    )


def gather_weight(weight):
    return lax.all_gather(weight, GROUP, axis=0, tiled=True)


def turned_lanes(value):
    lane = lax.broadcasted_iota(jnp.int32, value.shape, 1) % HEAD_WIDTH
    half = HEAD_WIDTH // 2
    return jnp.where(
        lane < half,
        pltpu.roll(value, LANES - half, 1),
        pltpu.roll(value, half, 1),
    )


def rotate_lanes(value, cosine, sine, sign):
    columns = []
    for start in range(0, value.shape[1], LANES):
        part = value[:, start : start + LANES]
        columns.append(part * cosine + sign * (turned_lanes(part) * sine))
    return columns[0] if len(columns) == 1 else jnp.concatenate(columns, axis=1)


def cross_dot(left_side, right_side):
    return lax.dot_general(
        left_side, right_side, (((1,), (1,)), ((), ())), preferred_element_type=jnp.float32
    )


def set_bias(bias, key_ids, query_ids):
    @pl.when(pl.program_id(0) == 0)
    def _():
        bias[...] = jnp.where(key_ids[...] <= query_ids[...], 0.0, -1e30)


def attend_forward(
    query, key, value, cosine, sine, key_ids, query_ids, query_out, key_out, value_out, mixed_out,
    logsum_out, bias,
):
    set_bias(bias, key_ids, query_ids)
    rotated = rotate_lanes(query[...], cosine[...], sine[...], 1.0)
    query_out[...] = (rotated.astype(jnp.bfloat16).astype(jnp.float32) * SCORE_SCALE).astype(
        jnp.bfloat16
    )
    key_out[...] = rotate_lanes(key[...], cosine[...], sine[...], 1.0).astype(jnp.bfloat16)
    value_out[...] = value[...].astype(jnp.bfloat16)
    turned_values = value[...].T.astype(jnp.bfloat16)
    heads = query.shape[1] // HEAD_WIDTH
    share = heads * HEAD_WIDTH // key.shape[1]
    outputs = []
    for head in range(heads):
        lanes = slice(head * HEAD_WIDTH, (head + 1) * HEAD_WIDTH)
        group = slice(head // share * HEAD_WIDTH, (head // share + 1) * HEAD_WIDTH)
        scores = cross_dot(key_out[:, group], query_out[:, lanes]) + bias[...]
        top = jnp.max(scores, axis=0, keepdims=True)
        weights = jnp.exp(scores - top)
        total = jnp.sum(weights, axis=0, keepdims=True)
        logsum_out[head : head + 1, :] = top + jnp.log(total)
        attend = (weights * (1.0 / total)).astype(jnp.bfloat16)
        outputs.append(
            jnp.dot(turned_values[group], attend, preferred_element_type=jnp.float32)
        )
    mixed_out[...] = jnp.concatenate(outputs, axis=0).T.astype(jnp.bfloat16)


def attend_backward(
    query, key, value, mixed_grad, logsum, cosine, sine, key_ids, query_ids, query_out, key_out,
    value_out, bias,
):
    set_bias(bias, key_ids, query_ids)
    heads = query.shape[1] // HEAD_WIDTH
    groups = key.shape[1] // HEAD_WIDTH
    share = heads // groups
    turned_keys = key[...].astype(jnp.float32).T.astype(jnp.bfloat16)
    query_grads = []
    key_grads = []
    value_grads = []
    for group_index in range(groups):
        group = slice(group_index * HEAD_WIDTH, (group_index + 1) * HEAD_WIDTH)
        key_grad = value_grad = None
        for head in range(group_index * share, (group_index + 1) * share):
            lanes = slice(head * HEAD_WIDTH, (head + 1) * HEAD_WIDTH)
            scores = cross_dot(key[:, group], query[:, lanes]) + bias[...]
            attend = jnp.exp(scores - logsum[head : head + 1, :])
            attend_grad = cross_dot(value[:, group], mixed_grad[:, lanes])
            delta = jnp.sum(attend * attend_grad, axis=0, keepdims=True)
            score_grad = (attend * (attend_grad - delta)).astype(jnp.bfloat16)
            value_term = matrix_product(attend.astype(jnp.bfloat16), mixed_grad[:, lanes])
            key_term = matrix_product(score_grad, query[:, lanes])
            value_grad = value_term if value_grad is None else value_grad + value_term
            key_grad = key_term if key_grad is None else key_grad + key_term
            query_grads.append(matrix_product(turned_keys[group], score_grad))
        key_grads.append(key_grad)
        value_grads.append(value_grad)
    query_grad = SCORE_SCALE * jnp.concatenate(query_grads, axis=0).T
    key_grad = jnp.concatenate(key_grads, axis=1)
    query_out[...] = rotate_lanes(query_grad, cosine[...], sine[...], -1.0).astype(jnp.bfloat16)
    key_out[...] = rotate_lanes(key_grad, cosine[...], sine[...], -1.0).astype(jnp.bfloat16)
    value_out[...] = jnp.concatenate(value_grads, axis=1).astype(jnp.bfloat16)


def hidden_backward(wide, grads, down, wide_out):
    hidden = down.shape[0]
    hidden_grad = cross_dot(grads[...], down[...])
    gating, upward = wide[:, :hidden], wide[:, hidden:]
    gate = 1.0 / (1.0 + jnp.exp(-gating))
    active = gating * gate
    wide_out[:, :hidden] = (hidden_grad * upward * (gate + active * (1.0 - gate))).astype(
        jnp.bfloat16
    )
    wide_out[:, hidden:] = (hidden_grad * active).astype(jnp.bfloat16)


def hidden_backward_call(wide, grads, down):
    rows, both = wide.shape
    width = grads.shape[1]
    block = 512

    def rows_of(columns):
        return pl.BlockSpec((block, columns), lambda step: (step, 0))

    return pl.pallas_call(
        hidden_backward,
        grid=(rows // block,),
        in_specs=[
            rows_of(both),
            rows_of(width),
            pl.BlockSpec(down.shape, lambda step: (0, 0)),
        ],
        out_specs=rows_of(both),
        out_shape=jax.ShapeDtypeStruct((rows, both), jnp.bfloat16),
        compiler_params=pltpu.CompilerParams(
            dimension_semantics=("arbitrary",), vmem_limit_bytes=56 * 1024 * 1024
        ),
        cost_estimate=pl.CostEstimate(
            flops=rows * both * width,
            bytes_accessed=rows * (both * 6 + width * 2) + down.size * 2,
            transcendentals=rows * both // 2,
        ),
        name="hidden_backward",
    )(wide, grads, down)


def kernel_cost(length, passes):
    return pl.CostEstimate(
        flops=2 * passes * QUERY_HEADS * HEAD_WIDTH * length * length,
        bytes_accessed=12 * length * QUERY_HEADS * HEAD_WIDTH,
        transcendentals=QUERY_HEADS * length * length,
    )


def attention_calls(length):
    step_keys = LANES
    steps = KEY_VALUE_HEADS * HEAD_WIDTH // step_keys
    step_queries = QUERY_HEADS * HEAD_WIDTH // steps
    step_heads = step_queries // HEAD_WIDTH
    key_start = QUERY_HEADS * HEAD_WIDTH // step_keys

    def columns(block, first):
        return pl.BlockSpec((length, block), lambda step: (0, step + first))

    def fixed(*shape):
        return pl.BlockSpec(shape, lambda step: (0, 0))

    tables = [
        fixed(length, LANES),
        fixed(length, LANES),
        fixed(length, 1),
        fixed(1, length),
    ]
    logsum = pl.BlockSpec((step_heads, length), lambda step: (step, 0))
    query_shape = jax.ShapeDtypeStruct((length, QUERY_HEADS * HEAD_WIDTH), jnp.bfloat16)
    key_shape = jax.ShapeDtypeStruct((length, KEY_VALUE_HEADS * HEAD_WIDTH), jnp.bfloat16)
    params = pltpu.CompilerParams(
        dimension_semantics=("arbitrary",), vmem_limit_bytes=48 * 1024 * 1024
    )
    forward = pl.pallas_call(
        attend_forward,
        grid=(steps,),
        in_specs=[
            columns(step_queries, 0),
            columns(step_keys, key_start),
            columns(step_keys, key_start + steps),
            *tables,
        ],
        out_specs=[
            columns(step_queries, 0),
            columns(step_keys, 0),
            columns(step_keys, 0),
            columns(step_queries, 0),
            logsum,
        ],
        out_shape=[
            query_shape,
            key_shape,
            key_shape,
            query_shape,
            jax.ShapeDtypeStruct((QUERY_HEADS, length), jnp.float32),
        ],
        scratch_shapes=[pltpu.VMEM((length, length), jnp.float32)],
        compiler_params=params,
        cost_estimate=kernel_cost(length, 2),
        name="attend_forward",
    )
    backward = pl.pallas_call(
        attend_backward,
        grid=(steps,),
        in_specs=[
            columns(step_queries, 0),
            columns(step_keys, 0),
            columns(step_keys, 0),
            columns(step_queries, 0),
            logsum,
            *tables,
        ],
        out_specs=[columns(step_queries, 0), columns(step_keys, 0), columns(step_keys, 0)],
        out_shape=[query_shape, key_shape, key_shape],
        scratch_shapes=[pltpu.VMEM((length, length), jnp.float32)],
        compiler_params=params,
        cost_estimate=kernel_cost(length, 5),
        name="attend_backward",
    )
    return forward, backward


def layer(
    tokens,
    block_ids,
    query_weight,
    key_projection_weight,
    value_projection_weight,
    output_weight,
    gate_weight,
    up_weight,
    down_weight,
    attn_gain,
    mlp_gain,
    cotangent,
):
    token_length, _ = tokens.shape
    row_count, hidden_width = gate_weight.shape
    slow = lax.axis_size("slow")
    unit = hidden_width // (slow * 8)
    local_hidden = slow * unit
    query_width = query_weight.shape[1]
    key_width = key_projection_weight.shape[1]
    qkv_width = query_width + 2 * key_width
    first_replica = lax.axis_index("replica") == 0
    first_chip = lax.axis_index("chip") == 0
    first_core = lax.axis_index("core") == 0

    gain_columns = jnp.pad(
        jnp.stack([attn_gain, mlp_gain], axis=1), ((0, 0), (0, LANES - 2))
    )
    qkv_local = jnp.concatenate(
        [query_weight, key_projection_weight, value_projection_weight, gain_columns], axis=1
    )
    qkv_all = gather_weight(qkv_local)
    output_all = gather_weight(output_weight)

    def column_slices(weight, member):
        pieces = []
        for step in range(slow):
            start = (step * 4 + member) * 2 * unit
            pieces.append(
                jnp.where(
                    first_replica,
                    weight[:, start : start + unit],
                    weight[:, start + unit : start + 2 * unit],
                )
            )
        return pieces

    packed = [
        jnp.concatenate(
            column_slices(gate_weight, member) + column_slices(up_weight, member), axis=1
        )
        for member in range(4)
    ]
    near, far = order(
        first_chip,
        jnp.concatenate(packed[:2], axis=0),
        jnp.concatenate(packed[2:], axis=0),
    )
    wide_blocks = []
    for block in order(first_chip, near, swap(far, "chip")):
        near, far = order(first_core, block[:row_count], block[row_count:])
        wide_blocks.extend(order(first_core, near, swap(far, "core")))
    wide_local = jnp.concatenate(wide_blocks, axis=0)
    down_local = jnp.where(first_replica, down_weight[:unit], down_weight[unit:])
    wide_all = lax.all_gather(wide_local, "slow", axis=0, tiled=True)
    down_all = lax.all_gather(down_local, "slow", axis=0, tiled=True)

    gains = qkv_all[:, qkv_width:][:, :2].T.astype(jnp.float32)
    attn_scale, mlp_scale = gains[0], gains[1]
    inputs = tokens.astype(jnp.float32)
    cosine_table, sine_table = rope_tables(token_length, HEAD_WIDTH)
    signs = jnp.where(jnp.arange(HEAD_WIDTH) < HEAD_WIDTH // 2, -1.0, 1.0)
    tables = (
        jnp.tile(cosine_table, (1, LANES // HEAD_WIDTH)),
        jnp.tile(sine_table * signs, (1, LANES // HEAD_WIDTH)),
        block_ids.T,
        block_ids,
    )
    attend_forward_call, attend_backward_call = attention_calls(token_length)
    first_normed = rms_norm(inputs, attn_scale).astype(jnp.bfloat16)
    projected = matrix_product(first_normed, qkv_all)
    query_rows, key_rows, value_rows, mixed, logsum = attend_forward_call(
        projected, projected, projected, *tables
    )
    residual = inputs + RESIDUAL * matrix_product(mixed, output_all)
    normed2 = rms_norm(residual, mlp_scale).astype(jnp.bfloat16)
    plane, partners = gather_tokens(normed2)
    normed2_all = jnp.concatenate(plane + partners, axis=0)
    grad_out = cotangent.astype(jnp.float32)
    down_in = (RESIDUAL * grad_out).astype(jnp.bfloat16)
    plane, partners = gather_tokens(down_in)
    down_in_all = jnp.concatenate(plane + partners, axis=0)
    wide = matrix_product(normed2_all, wide_all)
    gating, upward = wide[:, :local_hidden], wide[:, local_hidden:]
    hidden_act = (jax.nn.silu(gating) * upward).astype(jnp.bfloat16)
    grad_down = narrow(contract_rows(hidden_act, down_in_all))
    down_part = lax.psum_scatter(grad_down, "slow", scatter_dimension=0, tiled=True)

    def pieces_of(plane_rows):
        return [plane_rows[i * token_length : (i + 1) * token_length] for i in range(4)]

    def to_owners(rows, weight, product):
        partner = narrow(product(rows[4 * token_length :], weight))
        mine = narrow(product(rows[: 4 * token_length], weight))
        return scatter_pieces(pieces_of(mine), pieces_of(partner))

    mlp_out = to_owners(hidden_act, down_all, matrix_product)
    output = (residual + RESIDUAL * mlp_out).astype(jnp.bfloat16)
    wide_in = hidden_backward_call(wide, down_in_all, down_all)
    normed2_grad = to_owners(wide_in, wide_all, contract_cols)
    parts = []
    for start in (0, local_hidden):
        grad = narrow(contract_rows(normed2_all, wide_in[:, start : start + local_hidden]))
        parts.append(lax.psum_scatter(grad, "slow", scatter_dimension=0, tiled=True))

    def exchange(part):
        near, far = order(first_chip, part[: 2 * row_count], part[2 * row_count :])
        low, high = order(first_chip, near, swap(far, "chip"))
        members = []
        for block in (low, high):
            near, far = order(first_core, block[:row_count], block[row_count:])
            members.extend(order(first_core, near, swap(far, "core")))
        members = jnp.concatenate(members, axis=0)
        sources = order(first_replica, members, swap(members, "replica"))
        pieces = []
        for step in range(slow):
            for member in range(4):
                for source in sources:
                    pieces.append(
                        source[
                            member * row_count : (member + 1) * row_count,
                            step * unit : (step + 1) * unit,
                        ]
                    )
        return jnp.concatenate(pieces, axis=1).astype(jnp.float32)

    gate_shard, up_shard = exchange(parts[0]), exchange(parts[1])
    down_shard = jnp.concatenate(
        order(first_replica, down_part, swap(down_part, "replica")), axis=0
    ).astype(jnp.float32)

    _, norm2_pull = jax.vjp(rms_norm, residual, mlp_scale)
    residual_part, grad_mlp_gain = norm2_pull(normed2_grad)
    residual_grad = grad_out + residual_part

    def member_columns(left):
        blocks = {}
        for chip in range(2):
            for core in range(2):
                blocks[chip, core] = jnp.concatenate(
                    [
                        left[:, start : start + row_count]
                        for start in (
                            (step * 4 + chip * 2 + core) * row_count for step in range(slow)
                        )
                    ],
                    axis=1,
                )
        near = [order(first_chip, blocks[0, core], blocks[1, core]) for core in range(2)]
        chips = [order(first_core, near[0][chip], near[1][chip]) for chip in range(2)]
        return [[chips[chip][core] for chip in range(2)] for core in range(2)]

    def weight_part(left, right):
        half = right.shape[1] // 2
        sides = order(first_replica, right[:, :half], right[:, half:])
        blocks = member_columns(left)
        products = []
        for chips in (blocks[1], blocks[0]):
            products.append(
                [
                    narrow(contract_rows(chips[chip], sides[side]))
                    for side, chip in ((0, 0), (0, 1), (1, 0), (1, 1))
                ]
            )
        partner, mine = products
        return narrow(scatter_pieces(mine, partner))

    def both_sides(part):
        return jnp.concatenate(
            order(first_replica, part, swap(part, "replica")), axis=1
        ).astype(jnp.float32)

    attn_in = (RESIDUAL * residual_grad).astype(jnp.bfloat16)
    output_part = weight_part(mixed, attn_in)
    output_part = lax.psum_scatter(output_part, "slow", scatter_dimension=0, tiled=True)
    output_shard = both_sides(output_part)
    mixed_grad = contract_cols(attn_in, output_all).astype(jnp.bfloat16)
    query_lin_grad, key_lin_grad, value_lin_grad = attend_backward_call(
        query_rows, key_rows, value_rows, mixed_grad, logsum, *tables
    )
    qkv_in = jnp.concatenate([query_lin_grad, key_lin_grad, value_lin_grad], axis=1)
    qkv_sum = weight_part(first_normed, qkv_in)
    normed1_grad = contract_cols(qkv_in, qkv_all[:, :qkv_width])
    _, norm1_pull = jax.vjp(rms_norm, inputs, attn_scale)
    input_part, grad_attn_gain = norm1_pull(normed1_grad)
    input_grad = residual_grad + input_part
    gain_grads = jnp.stack([grad_attn_gain, grad_mlp_gain], axis=0)
    for axis in ("core", "chip", "replica"):
        gain_grads = gain_grads + swap(gain_grads, axis)
    gain_rows = jnp.pad(member_columns(gain_grads)[0][0].T, ((0, 0), (0, LANES - 2)))
    qkv_sum = jnp.concatenate([qkv_sum, gain_rows.astype(jnp.bfloat16)], axis=1)
    qkv_part = lax.psum_scatter(qkv_sum, "slow", scatter_dimension=0, tiled=True)
    qkv_shard = both_sides(qkv_part[:, : qkv_width // 2])
    attn_gain_shard = qkv_part[:, qkv_width // 2].astype(jnp.float32)
    mlp_gain_shard = qkv_part[:, qkv_width // 2 + 1].astype(jnp.float32)
    return (
        output,
        input_grad,
        qkv_shard[:, :query_width],
        qkv_shard[:, query_width : query_width + key_width],
        qkv_shard[:, query_width + key_width :],
        output_shard,
        gate_shard,
        up_shard,
        down_shard,
        attn_gain_shard,
        mlp_gain_shard,
    )


def solution(mesh):
    replicas, shard_count = mesh.shape["replica"], mesh.shape["shard"]
    inner = KEY_VALUE_HEADS // replicas
    cores = 2
    split_mesh = Mesh(
        mesh.devices.reshape(replicas, shard_count // inner, inner // cores, cores),
        ("replica", "slow", "chip", "core"),
    )
    everyone = P(("replica", "slow", "chip", "core"), None)
    sharded = P(GROUP, None)
    vector = P(GROUP)
    return jax.shard_map(
        layer,
        mesh=split_mesh,
        in_specs=(everyone, everyone) + (sharded,) * 7 + (vector, vector, everyone),
        out_specs=(everyone, everyone) + (sharded,) * 7 + (vector, vector),
        check_vma=False,
    )
```

time: 1520 us -> 1150 us (0.76)
  waiting for transfers between devices: 824 us -> 539 us
  matrix products: 414 us -> 247 us
  Pallas kernels: 0 us -> 83.3 us
  starting transfers between devices: 8.55 us -> 62.4 us
  local copies, waits for them, and re-layouts: 128 us -> 99 us
  blocking collectives: 28.9 us -> 0 us
    reduce_scatter x6 -> x5, waiting for transfers between devices: 450 us -> 48.5 us  [the longest x1 48.5 us: layer(): lax.psum_scatter(grad_down, 'slow', scatter_dimension=0, tiled=True)]
    ppermute x2 -> x75, waiting for transfers between devices: 9.55 us -> 377 us  [swap(): return lax.ppermute(value, axis, [(0, 1), (1, 0)])]
    all_gather x8 -> x4, waiting for transfers between devices: 348 us -> 112 us  [the longest x1 52.8 us: layer(): wide_all = lax.all_gather(wide_local, 'slow', axis=0, tiled=True)]
    dot_general x48 -> x0, matrix products: 129 us -> none  [the longest x8 45.8 us: shards(): jnp.einsum('qgd,td->gqt', grad_part, value_part, preferred_element_type=j...]
    pallas_call x0 -> x3, Pallas kernels: none -> 83.3 us  [the longest x1 30.8 us: hidden_backward_call(): pl.pallas_call(hidden_backward, grid=(rows // block,), in_specs=[rows_of(...]
    ppermute x2 -> x75, starting transfers between devices: 2.86 us -> 61.5 us  [swap(): return lax.ppermute(value, axis, [(0, 1), (1, 0)])]
    unnamed x230 -> x187, local copies, waits for them, and re-layouts: 30.2 us -> 66.9 us
    dot_general x4, matrix products: 102 us -> 65.8 us  [contract_cols(): lax.dot_general(left_side, right_side, (((1,), (1,)), ((), ())), preferre...]
  transfers between devices with their start and end apart: 17 -> 84, of which waited for: 11 -> 38; matrix products, arithmetic and copies ran while one was open for 37% -> 34% of each run, Pallas kernels for 0% -> 5%
where the time goes in v2:
time: 1150 us
  waiting for transfers between devices  539 us (47%)
  matrix products  247 us (21%)
  other arithmetic  102 us (9%)
  local copies, waits for them, and re-layouts  99 us (9%)
  Pallas kernels  83.3 us (7%)
  starting transfers between devices  62.4 us (5%)
  between operations  15.6 us (1%)
    ppermute x75, waiting for transfers between devices, swap(): return lax.ppermute(value, axis, [(0, 1), (1, 0)])  377 us
    dot_general x5, matrix products, matrix_product(): return jnp.dot(left_side, right_side, preferred_element_type=jnp.float32)  91.1 us
    dot_general x19, matrix products, contract_rows(): lax.dot_general(left_side, right_side, (((0,), (0,)), ((), ())), preferre...  89.8 us
    unnamed x187, local copies, waits for them, and re-layouts  66.9 us
    dot_general x4, matrix products, contract_cols(): lax.dot_general(left_side, right_side, (((1,), (1,)), ((), ())), preferre...  65.8 us
    ppermute x75, starting transfers between devices, swap(): return lax.ppermute(value, axis, [(0, 1), (1, 0)])  61.5 us
    all_gather x1, waiting for transfers between devices, layer(): wide_all = lax.all_gather(wide_local, 'slow', axis=0, tiled=True)  52.8 us
    reduce_scatter x1, waiting for transfers between devices, layer(): lax.psum_scatter(grad_down, 'slow', scatter_dimension=0, tiled=True)  48.5 us
  transfers between devices with their start and end apart: 84, of which 38 were waited for; matrix products, arithmetic and copies ran while one was open for 34% of the time, Pallas kernels for 5%

profile of v2, /device:TPU:0, one launch (start us, length us, event | category | flops | bytes accessed | tf_op | source)
XLA Modules:
  0.0 1147.8 jit_solution(7346692589652476412)
XLA Ops:
  20.2 3.1 collective-permute-start.9
  23.3 32.0 %collective-permute-done.9 = bf16[256,2048]{1,0:T(8,128)(2,1)} collective-permute-done((bf16[256,2048]{1,0:T(8,128)(2,1)S(1)}, bf16[256,2048]{1,0:T(8,128)(2,1)}, u32[]{:S(2)}, u32[]{:S(2)}) %collective-permute-start.9) | collective-permute-done | bytes 1048608 | tf_op jit(solution)/shard_map/ppermute | solution.py:59
  75.5 38.0 %collective-permute-done.23 = bf16[512,2048]{1,0:T(8,128)(2,1)} collective-permute-done((bf16[512,2048]{1,0:T(8,128)(2,1)}, bf16[512,2048]{1,0:T(8,128)(2,1)}, u32[]{:S(2)}, u32[]{:S(2)}) %collective-permute-start.23) | collective-permute-done | bytes 2097184 | tf_op jit(solution)/shard_map/ppermute | solution.py:59
  113.4 2.3 slice.1120
  117.2 25.3 %collective-permute-done.22 = bf16[512,2048]{1,0:T(8,128)(2,1)} collective-permute-done((bf16[512,2048]{1,0:T(8,128)(2,1)}, bf16[512,2048]{1,0:T(8,128)(2,1)}, u32[]{:S(2)}, u32[]{:S(2)}) %collective-permute-start.22) | collective-permute-done | bytes 2097184 | tf_op jit(solution)/shard_map/ppermute | solution.py:59
  151.1 12.6 %fusion.66.query.key.value = f32[512,3200]{1,0:T(8,128)} fusion(bf16[512,2048]{1,0:T(8,128)(2,1)S(1)} %fusion.19, bf16[2048,3200]{1,0:T(8,128)(2,1)} %all-gather.5.cloned.1.call-done), kind=kOutput, calls=%fused_computation.355 | convolution fusion | flops 6710886400 | bytes 21757952 | tf_op jit(solution)/shard_map/dot_general | solution.py:39
  163.6 22.8 %attend_forward.1 = (bf16[512,2048]{1,0:T(8,128)(2,1)S(1)}, bf16[512,512]{1,0:T(8,128)(2,1)S(1)}, bf16[512,512]{1,0:T(8,128)(2,1)S(1)}, bf16[512,2048]{1,0:T(8,128)(2,1)S(1)}, f32[32,512]{1,0:T(8,128)S(1)}) custom-call(f32[512,3200]{1,0:T(8,128)} %fusion.66.query.key.value, f32[512,3200]{1,0:T(8,128)} %fusion.66.query.key.value, ...), custom_call_target="tpu_custom_call" | custom-call | flops 2147483648 | bytes 12582912 | tf_op jit(solution)/shard_map/attend_forward/pallas_call | solution.py:417
  188.6 36.9 %all-gather.7.cloned.1.call-done = bf16[2048,2048]{1,0:T(8,128)(2,1)} async-done(((bf16[128,2048]{1,0:T(8,128)(2,1)}), bf16[2048,2048]{1,0:T(8,128)(2,1)}) %all-gather.7.cloned.1.call-update) | async-done | bytes 8388624 | tf_op jit(solution)/shard_map/all_gather | solution.py:112
  225.5 8.7 multiply_reduce_fusion.2
  237.7 3.4 constant_dynamic-update-slice_fusion.50
  242.6 3.2 constant_dynamic-update-slice_fusion.49
  245.8 2.3 constant_dynamic-update-slice_fusion.48
  251.0 3.3 constant_dynamic-update-slice_fusion.46
  254.2 3.2 constant_dynamic-update-slice_fusion.45
  257.4 3.2 constant_dynamic-update-slice_fusion.44
  261.7 23.1 %collective-permute-done = bf16[512,2048]{1,0:T(8,128)(2,1)S(1)} collective-permute-done((bf16[512,2048]{1,0:T(8,128)(2,1)S(1)}, bf16[512,2048]{1,0:T(8,128)(2,1)S(1)}, u32[]{:S(2)}, u32[]{:S(2)}) %collective-permute-start) | collective-permute-done | bytes 2097184 | tf_op jit(solution)/shard_map/ppermute | solution.py:59
  285.9 2.8 collective-permute-done.1
  297.9 15.2 %collective-permute-done.3 = bf16[256,2048]{1,0:T(8,128)(2,1)S(1)} collective-permute-done((bf16[256,2048]{1,0:T(8,128)(2,1)S(1)}, bf16[256,2048]{1,0:T(8,128)(2,1)S(1)}, u32[]{:S(2)}, u32[]{:S(2)}) %collective-permute-start.3) | collective-permute-done | bytes 1048608 | tf_op jit(solution)/shard_map/ppermute | solution.py:59
  323.0 52.8 %all-gather.9.cloned.1.call-done = bf16[2048,2048]{1,0:T(8,128)(2,1)} async-done(((bf16[512,2048]{1,0:T(8,128)(2,1)}), bf16[2048,2048]{1,0:T(8,128)(2,1)}) %all-gather.9.cloned.1.call-update) | async-done | bytes 8388624 | tf_op jit(solution)/shard_map/all_gather | solution.py:400
  375.9 43.4 %fusion.67.wide = f32[4096,2048]{1,0:T(8,128)} fusion(bf16[4096,2048]{1,0:T(8,128)(2,1)} %constant_dynamic-update-slice_fusion, bf16[2048,2048]{1,0:T(8,128)(2,1)} %all-gather.9.cloned.1.call-done), kind=kOutput, calls=%fused_computation.356 | convolution fusion | flops 34359738368 | bytes 58720256 | tf_op jit(solution)/shard_map/dot_general | solution.py:39
  419.3 15.2 %fusion = bf16[4096,1024]{1,0:T(8,128)(2,1)} fusion(f32[4096,2048]{1,0:T(8,128)} %fusion.67.wide), kind=kLoop, calls=%fused_computation.1 | loop fusion | flops 25165824 | bytes 41943040 | tf_op jit(solution)/shard_map/convert_element_type | solution.py:430
  434.4 22.4 %all-gather.11.cloned.1.call-done.down = bf16[1024,2048]{1,0:T(8,128)(2,1)} async-done(((bf16[256,2048]{1,0:T(8,128)(2,1)}), bf16[1024,2048]{1,0:T(8,128)(2,1)}) %all-gather.11.cloned.1.call-update) | async-done | bytes 4194320 | tf_op jit(solution)/shard_map/all_gather | solution.py:401
  456.8 30.8 %hidden_backward.1 = bf16[4096,2048]{1,0:T(8,128)(2,1)} custom-call(f32[4096,2048]{1,0:T(8,128)} %fusion.67.wide, bf16[4096,2048]{1,0:T(8,128)(2,1)} %constant_dynamic-update-slice_fusion.42.grads, bf16[1024,2048]{1,0:T(8,128)(2,1)} %all-gather.11.cloned.1.call-done.down), custom_call_target="tpu_custom_call" | custom-call | flops 17179869184 | bytes 71303168 | tf_op jit(solution)/shard_map/hidden_backward/pallas_call | solution.py:231
  487.6 22.8 %fusion.14 = bf16[2048,2048]{1,0:T(8,128)(2,1)S(1)} fusion(bf16[2048,2048]{1,0:T(8,128)(2,1)} %all-gather.9.cloned.1.call-done, bf16[4096,2048]{1,0:T(8,128)(2,1)} %hidden_backward.1), kind=kOutput, calls=%fused_computation.18 | convolution fusion | flops 17184063488 | bytes 25165824 | tf_op jit(solution)/shard_map/dot_general | solution.py:49
  510.5 4.2 fusion.57
  515.7 14.1 %convolution_convert_fusion = bf16[2048,2048]{1,0:T(8,128)(2,1)} fusion(bf16[1024,2048]{1,0:T(8,128)(2,1)S(1)} %copy-done.15, bf16[4096,1024]{1,0:T(8,128)(2,1)} %fusion), kind=kOutput, calls=%fused_computation.19 | convolution fusion | flops 8594128896 | bytes 16777216 | tf_op jit(solution)/shard_map/dot_general | solution.py:39
  529.9 6.0 fusion.58
  535.9 22.1 %fusion.11 = bf16[2048,2048]{1,0:T(8,128)(2,1)} fusion(bf16[2048,2048]{1,0:T(8,128)(2,1)} %all-gather.9.cloned.1.call-done, bf16[4096,2048]{1,0:T(8,128)(2,1)S(1)} %bitcast.46), kind=kOutput, calls=%fused_computation.17 | convolution fusion | flops 17184063488 | bytes 25165824 | tf_op jit(solution)/shard_map/dot_general | solution.py:49
  559.0 12.3 %convolution_convert_fusion.1 = bf16[2048,2048]{1,0:T(8,128)(2,1)S(1)} fusion(bf16[1024,2048]{1,0:T(8,128)(2,1)} %all-gather.11.cloned.1.call-done.down, bf16[4096,1024]{1,0:T(8,128)(2,1)} %fusion), kind=kOutput, calls=%fused_computation.20 | convolution fusion | flops 8594128896 | bytes 16777216 | tf_op jit(solution)/shard_map/dot_general | solution.py:39
  571.4 5.9 add_convert_fusion.1
  584.9 6.1 add_convert_fusion.4
  594.8 33.4 %collective-permute-done.36 = bf16[256,2048]{1,0:T(8,128)(2,1)} collective-permute-done((bf16[256,2048]{1,0:T(8,128)(2,1)}, bf16[256,2048]{1,0:T(8,128)(2,1)}, u32[]{:S(2)}, u32[]{:S(2)}) %collective-permute-start.36) | collective-permute-done | bytes 1048608 | tf_op jit(solution)/shard_map/ppermute | solution.py:59
  633.8 16.3 %collective-permute-done.17 = bf16[256,2048]{1,0:T(8,128)(2,1)S(1)} collective-permute-done((bf16[256,2048]{1,0:T(8,128)(2,1)S(1)}, bf16[256,2048]{1,0:T(8,128)(2,1)S(1)}, u32[]{:S(2)}, u32[]{:S(2)}) %collective-permute-start.17) | collective-permute-done | bytes 1048608 | tf_op jit(solution)/shard_map/ppermute | solution.py:59
  658.2 18.5 %collective-permute-done.37 = bf16[256,2048]{1,0:T(8,128)(2,1)S(1)} collective-permute-done((bf16[256,2048]{1,0:T(8,128)(2,1)S(1)}, bf16[256,2048]{1,0:T(8,128)(2,1)S(1)}, u32[]{:S(2)}, u32[]{:S(2)}) %collective-permute-start.37) | collective-permute-done | bytes 1048608 | tf_op jit(solution)/shard_map/ppermute | solution.py:59
  678.2 2.9 fusion.37
  682.2 16.4 %collective-permute-done.14 = bf16[256,2048]{1,0:T(8,128)(2,1)S(1)} collective-permute-done((bf16[256,2048]{1,0:T(8,128)(2,1)}, bf16[256,2048]{1,0:T(8,128)(2,1)S(1)}, u32[]{:S(2)}, u32[]{:S(2)}) %collective-permute-start.14) | collective-permute-done | bytes 1048608 | tf_op jit(solution)/shard_map/ppermute | solution.py:59
  699.2 21.0 %collective-permute-done.18 = bf16[256,2048]{1,0:T(8,128)(2,1)S(1)} collective-permute-done((bf16[256,2048]{1,0:T(8,128)(2,1)S(1)}, bf16[256,2048]{1,0:T(8,128)(2,1)S(1)}, u32[]{:S(2)}, u32[]{:S(2)}) %collective-permute-start.18) | collective-permute-done | bytes 1048608 | tf_op jit(solution)/shard_map/ppermute | solution.py:59
  721.8 3.9 multiply_convert_fusion
  738.7 9.0 collective-permute-done.60
  752.8 6.1 collective-permute-done.57
  758.9 2.9 collective-permute-done.62
  761.8 9.7 collective-permute-done.61
  773.3 23.9 %fusion.29 = bf16[2048,1024]{1,0:T(8,128)(2,1)} fusion(bf16[4096,2048]{1,0:T(8,128)(2,1)} %constant_dynamic-update-slice_fusion, bf16[4096,2048]{1,0:T(8,128)(2,1)} %hidden_backward.1), kind=kOutput, calls=%fused_computation.52 | convolution fusion | flops 17181966336 | bytes 29360128 | tf_op jit(solution)/shard_map/dot_general | solution.py:43
  797.2 23.9 %fusion.32 = bf16[2048,1024]{1,0:T(8,128)(2,1)} fusion(bf16[4096,2048]{1,0:T(8,128)(2,1)} %constant_dynamic-update-slice_fusion, bf16[4096,2048]{1,0:T(8,128)(2,1)} %hidden_backward.1), kind=kOutput, calls=%fused_computation.53 | convolution fusion | flops 17181966336 | bytes 29360128 | tf_op jit(solution)/shard_map/dot_general | solution.py:43
  824.8 24.1 %convolution_convert_fusion.2 = bf16[1024,2048]{1,0:T(8,128)(2,1)} fusion(bf16[4096,1024]{1,0:T(8,128)(2,1)} %fusion, bf16[4096,2048]{1,0:T(8,128)(2,1)} %constant_dynamic-update-slice_fusion.42.grads), kind=kOutput, calls=%fused_computation.54 | convolution fusion | flops 17181966336 | bytes 29360128 | tf_op jit(solution)/shard_map/dot_general | solution.py:43
  849.0 10.0 convolution_convert_fusion.11.mixed_grad
  859.0 29.7 %attend_backward.1 = (bf16[512,2048]{1,0:T(8,128)(2,1)S(1)}, bf16[512,512]{1,0:T(8,128)(2,1)S(1)}, bf16[512,512]{1,0:T(8,128)(2,1)S(1)}) custom-call(bf16[512,2048]{1,0:T(8,128)(2,1)} %copy-done.1, bf16[512,512]{1,0:T(8,128)(2,1)S(1)} %get-tuple-element.21.key, bf16[512,512]{1,0:T(8,128)(2,1)S(1)} %copy-done.3, ...), custom_call_target="tpu_custom_call" | custom-call | flops 5368709120 | bytes 12582912 | tf_op jit(solution)/shard_map/attend_backward/pallas_call | solution.py:523
  890.6 10.9 fusion.20
  912.2 3.1 fusion.22
  915.8 2.7 collective-permute-done.45
  920.8 2.6 add_convert_fusion.8
  929.3 10.9 collective-permute-done.46
  942.7 3.0 collective-permute-done.49
  952.0 5.1 collective-permute-done.43
  957.1 5.5 collective-permute-done.48
  962.6 15.6 %collective-permute-done.47 = bf16[256,1536]{1,0:T(8,128)(2,1)} collective-permute-done((bf16[256,1536]{1,0:T(8,128)(2,1)}, bf16[256,1536]{1,0:T(8,128)(2,1)}, u32[]{:S(2)}, u32[]{:S(2)}) %collective-permute-start.47) | collective-permute-done | bytes 786464 | tf_op jit(solution)/shard_map/ppermute | solution.py:59
  978.2 2.5 fusion.45
  988.3 48.5 %reduce-scatter.14.cloned.1.call-done = bf16[256,2048]{1,0:T(8,128)(2,1)} async-done(((bf16[1024,2048]{1,0:T(8,128)(2,1)}), bf16[256,2048]{1,0:T(8,128)(2,1)}) %reduce-scatter.14.cloned.1.call-update) | async-done | bytes 1048592 | tf_op jit(solution)/shard_map/reduce_scatter | solution.py:432
  1046.3 16.7 %collective-permute-done.74 = bf16[256,2048]{1,0:T(8,128)(2,1)S(1)} collective-permute-done((bf16[256,2048]{1,0:T(8,128)(2,1)}, bf16[256,2048]{1,0:T(8,128)(2,1)S(1)}, u32[]{:S(2)}, u32[]{:S(2)}) %collective-permute-start.74) | collective-permute-done | bytes 1048608 | tf_op jit(solution)/shard_map/ppermute | solution.py:59
  1063.2 2.6 maximum_convert_fusion
  1065.7 19.8 %collective-permute-done.73 = bf16[512,1024]{1,0:T(8,128)(2,1)S(1)} collective-permute-done((bf16[512,1024]{1,0:T(8,128)(2,1)S(1)}, bf16[512,1024]{1,0:T(8,128)(2,1)S(1)}, u32[]{:S(2)}, u32[]{:S(2)}) %collective-permute-start.73) | collective-permute-done | bytes 1048608 | tf_op jit(solution)/shard_map/ppermute | solution.py:59
  1088.0 18.5 %collective-permute-done.69 = bf16[512,1024]{1,0:T(8,128)(2,1)S(1)} collective-permute-done((bf16[512,1024]{1,0:T(8,128)(2,1)S(1)}, bf16[512,1024]{1,0:T(8,128)(2,1)S(1)}, u32[]{:S(2)}, u32[]{:S(2)}) %collective-permute-start.69) | collective-permute-done | bytes 1048608 | tf_op jit(solution)/shard_map/ppermute | solution.py:59
  1129.5 4.0 convert_element_type.492
  1134.2 4.1 convert_element_type.490
  (466 shorter events, 205.3 us)
Async XLA Ops:
  7.2 140.0 %all-gather.5.cloned.1.call-start = ((), (), s32[]{:S(2)}) async-start(), calls=%async_computation.5 | async-start | bytes 13926400 | tf_op jit(solution)/shard_map/all_gather | solution.py:112
  10.2 215.3 %all-gather.7.cloned.1.call-start = ((), (), s32[]{:S(2)}) async-start(), calls=%async_computation.6 | async-start | bytes 8912896 | tf_op jit(solution)/shard_map/all_gather | solution.py:112
  11.0 364.9 %all-gather.9.cloned.1.call-start = ((), (), s32[]{:S(2)}) async-start(), calls=%async_computation.7 | async-start | bytes 10485760 | tf_op jit(solution)/shard_map/all_gather | solution.py:400
  20.2 35.1 %collective-permute-start.9 = (bf16[256,2048]{1,0:T(8,128)(2,1)S(1)}, bf16[256,2048]{1,0:T(8,128)(2,1)}, u32[]{:S(2)}, u32[]{:S(2)}) collective-permute-start(bf16[256,2048]{1,0:T(8,128)(2,1)S(1)} %broadcast_select_fusion.12), channel_id=1, source_target_pairs={{0,2},{2,0},{1,3},{3,1},{4,6},{6,4},{5,7},{7,5},{8,10},{10,8},{9,1... | collective-permute-start | bytes 3145736 | tf_op jit(solution)/shard_map/ppermute | solution.py:59
  61.6 395.2 %all-gather.11.cloned.1.call-start = ((), (), s32[]{:S(2)}) async-start(), calls=%async_computation.8 | async-start | bytes 5242880 | tf_op jit(solution)/shard_map/all_gather | solution.py:401
  64.9 172.0 %collective-permute-start.26 = (bf16[512,2048]{1,0:T(8,128)(2,1)}, bf16[512,2048]{1,0:T(8,128)(2,1)}, u32[]{:S(2)}, u32[]{:S(2)}) collective-permute-start(bf16[512,2048]{1,0:T(8,128)(2,1)} %fusion.21), channel_id=1, source_target_pairs={{0,1},{1,0},{2,3},{3,2},{4,5},{5,4},{6,7},{7,6},{8,9},{9,8},{10,11... | collective-permute-start | bytes 6291464 | tf_op jit(solution)/shard_map/ppermute | solution.py:59
  65.3 48.1 %collective-permute-start.23 = (bf16[512,2048]{1,0:T(8,128)(2,1)}, bf16[512,2048]{1,0:T(8,128)(2,1)}, u32[]{:S(2)}, u32[]{:S(2)}) collective-permute-start(bf16[512,2048]{1,0:T(8,128)(2,1)} %fusion.21), channel_id=1, source_target_pairs={{0,16},{16,0},{1,17},{17,1},{2,18},{18,2},{3,19},{19,3},{4,20},{20... | collective-permute-start | bytes 6291464 | tf_op jit(solution)/shard_map/ppermute | solution.py:59
  67.0 75.6 %collective-permute-start.22 = (bf16[512,2048]{1,0:T(8,128)(2,1)}, bf16[512,2048]{1,0:T(8,128)(2,1)}, u32[]{:S(2)}, u32[]{:S(2)}) collective-permute-start(bf16[512,2048]{1,0:T(8,128)(2,1)} %fusion.21), channel_id=1, source_target_pairs={{0,2},{2,0},{1,3},{3,1},{4,6},{6,4},{5,7},{7,5},{8,10},{10,8},{9,1... | collective-permute-start | bytes 6291464 | tf_op jit(solution)/shard_map/ppermute | solution.py:59
  69.5 912.6 %reduce-scatter.8.cloned.1.call-start = ((), (), s32[]{:S(2)}) async-start(), calls=%async_computation.10 | async-start | bytes 1310720 | tf_op jit(solution)/shard_map/reduce_scatter | solution.py:520
  115.7 132.4 %collective-permute-start.25 = (bf16[256,2048]{1,0:T(8,128)(2,1)}, bf16[256,2048]{1,0:T(8,128)(2,1)}, u32[]{:S(2)}, u32[]{:S(2)}) collective-permute-start(bf16[256,2048]{1,0:T(8,128)(2,1)} %slice.1120), channel_id=1, source_target_pairs={{0,2},{2,0},{1,3},{3,1},{4,6},{6,4},{5,7},{7,5},{8,10},{10,8},{9,1... | collective-permute-start | bytes 3145736 | tf_op jit(solution)/shard_map/ppermute | solution.py:59
  144.9 96.3 %collective-permute-start.24 = (bf16[256,2048]{1,0:T(8,128)(2,1)}, bf16[256,2048]{1,0:T(8,128)(2,1)}, u32[]{:S(2)}, u32[]{:S(2)}) collective-permute-start(bf16[256,2048]{1,0:T(8,128)(2,1)} %slice.1119), channel_id=1, source_target_pairs={{0,16},{16,0},{1,17},{17,1},{2,18},{18,2},{3,19},{19,3},{4,20},{20... | collective-permute-start | bytes 3145736 | tf_op jit(solution)/shard_map/ppermute | solution.py:59
  146.3 111.1 %collective-permute-start.28 = (bf16[512,2048]{1,0:T(8,128)(2,1)}, bf16[512,2048]{1,0:T(8,128)(2,1)}, u32[]{:S(2)}, u32[]{:S(2)}) collective-permute-start(bf16[512,2048]{1,0:T(8,128)(2,1)} %collective-permute-done.23), channel_id=1, source_target_pairs={{0,1},{1,0},{2,3},{3,2},{4,5},{5,4},{6,7},{7,6},{8,9},{9,8},{10,11... | collective-permute-start | bytes 6291464 | tf_op jit(solution)/shard_map/ppermute | solution.py:59
  146.4 104.1 %collective-permute-start.27 = (bf16[512,2048]{1,0:T(8,128)(2,1)}, bf16[512,2048]{1,0:T(8,128)(2,1)}, u32[]{:S(2)}, u32[]{:S(2)}) collective-permute-start(bf16[512,2048]{1,0:T(8,128)(2,1)} %collective-permute-done.22), channel_id=1, source_target_pairs={{0,1},{1,0},{2,3},{3,2},{4,5},{5,4},{6,7},{7,6},{8,9},{9,8},{10,11... | collective-permute-start | bytes 6291464 | tf_op jit(solution)/shard_map/ppermute | solution.py:59
  237.0 47.8 %collective-permute-start = (bf16[512,2048]{1,0:T(8,128)(2,1)S(1)}, bf16[512,2048]{1,0:T(8,128)(2,1)S(1)}, u32[]{:S(2)}, u32[]{:S(2)}) collective-permute-start(bf16[512,2048]{1,0:T(8,128)(2,1)S(1)} %get-tuple-element.38), channel_id=1, source_target_pairs={{0,2},{2,0},{1,3},{3,1},{4,6},{6,4},{5,7},{7,5},{8,10},{10,8},{9,1... | collective-permute-start | bytes 6291464 | tf_op jit(solution)/shard_map/ppermute | solution.py:59
  241.1 47.5 %collective-permute-start.1 = (bf16[512,2048]{1,0:T(8,128)(2,1)S(1)}, bf16[512,2048]{1,0:T(8,128)(2,1)S(1)}, u32[]{:S(2)}, u32[]{:S(2)}) collective-permute-start(bf16[512,2048]{1,0:T(8,128)(2,1)S(1)} %get-tuple-element.38), channel_id=1, source_target_pairs={{0,16},{16,0},{1,17},{17,1},{2,18},{18,2},{3,19},{19,3},{4,20},{20... | collective-permute-start | bytes 6291464 | tf_op jit(solution)/shard_map/ppermute | solution.py:59
  250.5 34.4 %collective-permute-start.30 = (bf16[256,2048]{1,0:T(8,128)(2,1)}, bf16[256,2048]{1,0:T(8,128)(2,1)S(1)}, u32[]{:S(2)}, u32[]{:S(2)}) collective-permute-start(bf16[256,2048]{1,0:T(8,128)(2,1)} %collective-permute-done.25), channel_id=1, source_target_pairs={{0,1},{1,0},{2,3},{3,2},{4,5},{5,4},{6,7},{7,6},{8,9},{9,8},{10,11... | collective-permute-start | bytes 3145736 | tf_op jit(solution)/shard_map/ppermute | solution.py:59
  260.6 55.8 %collective-permute-start.4 = (bf16[512,2048]{1,0:T(8,128)(2,1)S(1)}, bf16[512,2048]{1,0:T(8,128)(2,1)S(1)}, u32[]{:S(2)}, u32[]{:S(2)}) collective-permute-start(bf16[512,2048]{1,0:T(8,128)(2,1)S(1)} %get-tuple-element.38), channel_id=1, source_target_pairs={{0,1},{1,0},{2,3},{3,2},{4,5},{5,4},{6,7},{7,6},{8,9},{9,8},{10,11... | collective-permute-start | bytes 6291464 | tf_op jit(solution)/shard_map/ppermute | solution.py:59
  284.8 33.1 %collective-permute-start.5 = (bf16[512,2048]{1,0:T(8,128)(2,1)S(1)}, bf16[512,2048]{1,0:T(8,128)(2,1)S(1)}, u32[]{:S(2)}, u32[]{:S(2)}) collective-permute-start(bf16[512,2048]{1,0:T(8,128)(2,1)S(1)} %collective-permute-done), channel_id=1, source_target_pairs={{0,1},{1,0},{2,3},{3,2},{4,5},{5,4},{6,7},{7,6},{8,9},{9,8},{10,11... | collective-permute-start | bytes 6291464 | tf_op jit(solution)/shard_map/ppermute | solution.py:59
  288.7 24.3 %collective-permute-start.3 = (bf16[256,2048]{1,0:T(8,128)(2,1)S(1)}, bf16[256,2048]{1,0:T(8,128)(2,1)S(1)}, u32[]{:S(2)}, u32[]{:S(2)}) collective-permute-start(bf16[256,2048]{1,0:T(8,128)(2,1)S(1)} %slice.1094), channel_id=1, source_target_pairs={{0,2},{2,0},{1,3},{3,1},{4,6},{6,4},{5,7},{7,5},{8,10},{10,8},{9,1... | collective-permute-start | bytes 3145736 | tf_op jit(solution)/shard_map/ppermute | solution.py:59
  290.2 24.1 %collective-permute-start.2 = (bf16[256,2048]{1,0:T(8,128)(2,1)S(1)}, bf16[256,2048]{1,0:T(8,128)(2,1)S(1)}, u32[]{:S(2)}, u32[]{:S(2)}) collective-permute-start(bf16[256,2048]{1,0:T(8,128)(2,1)S(1)} %slice.1093), channel_id=1, source_target_pairs={{0,16},{16,0},{1,17},{17,1},{2,18},{18,2},{3,19},{19,3},{4,20},{20... | collective-permute-start | bytes 3145736 | tf_op jit(solution)/shard_map/ppermute | solution.py:59
  291.8 27.6 %collective-permute-start.6 = (bf16[512,2048]{1,0:T(8,128)(2,1)S(1)}, bf16[512,2048]{1,0:T(8,128)(2,1)S(1)}, u32[]{:S(2)}, u32[]{:S(2)}) collective-permute-start(bf16[512,2048]{1,0:T(8,128)(2,1)S(1)} %collective-permute-done.1), channel_id=1, source_target_pairs={{0,1},{1,0},{2,3},{3,2},{4,5},{5,4},{6,7},{7,6},{8,9},{9,8},{10,11... | collective-permute-start | bytes 6291464 | tf_op jit(solution)/shard_map/ppermute | solution.py:59
  514.7 43.3 %collective-permute-start.34 = (bf16[512,2048]{1,0:T(8,128)(2,1)}, bf16[512,2048]{1,0:T(8,128)(2,1)S(1)}, u32[]{:S(2)}, u32[]{:S(2)}) collective-permute-start(bf16[512,2048]{1,0:T(8,128)(2,1)} %get-tuple-element.43), channel_id=1, source_target_pairs={{0,1},{1,0},{2,3},{3,2},{4,5},{5,4},{6,7},{7,6},{8,9},{9,8},{10,11... | collective-permute-start | bytes 6291464 | tf_op jit(solution)/shard_map/ppermute | solution.py:59
  514.7 43.8 %collective-permute-start.35 = (bf16[512,2048]{1,0:T(8,128)(2,1)}, bf16[512,2048]{1,0:T(8,128)(2,1)S(1)}, u32[]{:S(2)}, u32[]{:S(2)}) collective-permute-start(bf16[512,2048]{1,0:T(8,128)(2,1)} %get-tuple-element.44), channel_id=1, source_target_pairs={{0,1},{1,0},{2,3},{3,2},{4,5},{5,4},{6,7},{7,6},{8,9},{9,8},{10,11... | collective-permute-start | bytes 6291464 | tf_op jit(solution)/shard_map/ppermute | solution.py:59
  515.2 43.4 %collective-permute-start.32 = (bf16[512,2048]{1,0:T(8,128)(2,1)}, bf16[512,2048]{1,0:T(8,128)(2,1)}, u32[]{:S(2)}, u32[]{:S(2)}) collective-permute-start(bf16[512,2048]{1,0:T(8,128)(2,1)} %get-tuple-element.45), channel_id=1, source_target_pairs={{0,1},{1,0},{2,3},{3,2},{4,5},{5,4},{6,7},{7,6},{8,9},{9,8},{10,11... | collective-permute-start | bytes 6291464 | tf_op jit(solution)/shard_map/ppermute | solution.py:59
  515.2 56.2 %collective-permute-start.31 = (bf16[512,2048]{1,0:T(8,128)(2,1)}, bf16[512,2048]{1,0:T(8,128)(2,1)}, u32[]{:S(2)}, u32[]{:S(2)}) collective-permute-start(bf16[512,2048]{1,0:T(8,128)(2,1)} %get-tuple-element.46), channel_id=1, source_target_pairs={{0,1},{1,0},{2,3},{3,2},{4,5},{5,4},{6,7},{7,6},{8,9},{9,8},{10,11... | collective-permute-start | bytes 6291464 | tf_op jit(solution)/shard_map/ppermute | solution.py:59
  535.9 46.5 %collective-permute-start.15 = (bf16[512,2048]{1,0:T(8,128)(2,1)}, bf16[512,2048]{1,0:T(8,128)(2,1)}, u32[]{:S(2)}, u32[]{:S(2)}) collective-permute-start(bf16[512,2048]{1,0:T(8,128)(2,1)} %get-tuple-element.51), channel_id=1, source_target_pairs={{0,1},{1,0},{2,3},{3,2},{4,5},{5,4},{6,7},{7,6},{8,9},{9,8},{10,11... | collective-permute-start | bytes 6291464 | tf_op jit(solution)/shard_map/ppermute | solution.py:59
  558.0 25.8 %collective-permute-start.16 = (bf16[512,2048]{1,0:T(8,128)(2,1)}, bf16[512,2048]{1,0:T(8,128)(2,1)}, u32[]{:S(2)}, u32[]{:S(2)}) collective-permute-start(bf16[512,2048]{1,0:T(8,128)(2,1)} %get-tuple-element.52), channel_id=1, source_target_pairs={{0,1},{1,0},{2,3},{3,2},{4,5},{5,4},{6,7},{7,6},{8,9},{9,8},{10,11... | collective-permute-start | bytes 6291464 | tf_op jit(solution)/shard_map/ppermute | solution.py:59
  558.5 25.9 %collective-permute-start.13 = (bf16[512,2048]{1,0:T(8,128)(2,1)}, bf16[512,2048]{1,0:T(8,128)(2,1)}, u32[]{:S(2)}, u32[]{:S(2)}) collective-permute-start(bf16[512,2048]{1,0:T(8,128)(2,1)} %get-tuple-element.53), channel_id=1, source_target_pairs={{0,1},{1,0},{2,3},{3,2},{4,5},{5,4},{6,7},{7,6},{8,9},{9,8},{10,11... | collective-permute-start | bytes 6291464 | tf_op jit(solution)/shard_map/ppermute | solution.py:59
  558.6 26.3 %collective-permute-start.12 = (bf16[512,2048]{1,0:T(8,128)(2,1)}, bf16[512,2048]{1,0:T(8,128)(2,1)}, u32[]{:S(2)}, u32[]{:S(2)}) collective-permute-start(bf16[512,2048]{1,0:T(8,128)(2,1)} %get-tuple-element.54), channel_id=1, source_target_pairs={{0,1},{1,0},{2,3},{3,2},{4,5},{5,4},{6,7},{7,6},{8,9},{9,8},{10,11... | collective-permute-start | bytes 6291464 | tf_op jit(solution)/shard_map/ppermute | solution.py:59
  579.4 76.7 %collective-permute-start.33 = (bf16[256,2048]{1,0:T(8,128)(2,1)}, bf16[256,2048]{1,0:T(8,128)(2,1)}, u32[]{:S(2)}, u32[]{:S(2)}) collective-permute-start(bf16[256,2048]{1,0:T(8,128)(2,1)} %slice.1128), channel_id=1, source_target_pairs={{0,2},{2,0},{1,3},{3,1},{4,6},{6,4},{5,7},{7,5},{8,10},{10,8},{9,1... | collective-permute-start | bytes 3145736 | tf_op jit(solution)/shard_map/ppermute | solution.py:59
  582.3 75.3 %collective-permute-start.38 = (bf16[256,2048]{1,0:T(8,128)(2,1)}, bf16[256,2048]{1,0:T(8,128)(2,1)}, u32[]{:S(2)}, u32[]{:S(2)}) collective-permute-start(bf16[256,2048]{1,0:T(8,128)(2,1)} %slice.1136), channel_id=1, source_target_pairs={{0,16},{16,0},{1,17},{17,1},{2,18},{18,2},{3,19},{19,3},{4,20},{20... | collective-permute-start | bytes 3145736 | tf_op jit(solution)/shard_map/ppermute | solution.py:59
  583.8 44.4 %collective-permute-start.36 = (bf16[256,2048]{1,0:T(8,128)(2,1)}, bf16[256,2048]{1,0:T(8,128)(2,1)}, u32[]{:S(2)}, u32[]{:S(2)}) collective-permute-start(bf16[256,2048]{1,0:T(8,128)(2,1)} %get-tuple-element.108), channel_id=1, source_target_pairs={{0,2},{2,0},{1,3},{3,1},{4,6},{6,4},{5,7},{7,5},{8,10},{10,8},{9,1... | collective-permute-start | bytes 3145736 | tf_op jit(solution)/shard_map/ppermute | solution.py:59
  584.4 47.0 %collective-permute-start.39 = (bf16[256,2048]{1,0:T(8,128)(2,1)}, bf16[256,2048]{1,0:T(8,128)(2,1)}, u32[]{:S(2)}, u32[]{:S(2)}) collective-permute-start(bf16[256,2048]{1,0:T(8,128)(2,1)} %get-tuple-element.109), channel_id=1, source_target_pairs={{0,16},{16,0},{1,17},{17,1},{2,18},{18,2},{3,19},{19,3},{4,20},{20... | collective-permute-start | bytes 3145736 | tf_op jit(solution)/shard_map/ppermute | solution.py:59
  593.3 56.9 %collective-permute-start.17 = (bf16[256,2048]{1,0:T(8,128)(2,1)S(1)}, bf16[256,2048]{1,0:T(8,128)(2,1)S(1)}, u32[]{:S(2)}, u32[]{:S(2)}) collective-permute-start(bf16[256,2048]{1,0:T(8,128)(2,1)S(1)} %get-tuple-element.110), channel_id=1, source_target_pairs={{0,2},{2,0},{1,3},{3,1},{4,6},{6,4},{5,7},{7,5},{8,10},{10,8},{9,1... | collective-permute-start | bytes 3145736 | tf_op jit(solution)/shard_map/ppermute | solution.py:59
  628.2 26.0 %collective-permute-start.20 = (bf16[256,2048]{1,0:T(8,128)(2,1)S(1)}, bf16[256,2048]{1,0:T(8,128)(2,1)S(1)}, u32[]{:S(2)}, u32[]{:S(2)}) collective-permute-start(bf16[256,2048]{1,0:T(8,128)(2,1)S(1)} %get-tuple-element.111), channel_id=1, source_target_pairs={{0,16},{16,0},{1,17},{17,1},{2,18},{18,2},{3,19},{19,3},{4,20},{20... | collective-permute-start | bytes 3145736 | tf_op jit(solution)/shard_map/ppermute | solution.py:59
  631.4 45.4 %collective-permute-start.37 = (bf16[256,2048]{1,0:T(8,128)(2,1)S(1)}, bf16[256,2048]{1,0:T(8,128)(2,1)S(1)}, u32[]{:S(2)}, u32[]{:S(2)}) collective-permute-start(bf16[256,2048]{1,0:T(8,128)(2,1)S(1)} %add_convert_fusion.13), channel_id=1, source_target_pairs={{0,16},{16,0},{1,17},{17,1},{2,18},{18,2},{3,19},{19,3},{4,20},{20... | collective-permute-start | bytes 3145736 | tf_op jit(solution)/shard_map/ppermute | solution.py:59
  650.1 28.1 %collective-permute-start.40 = (bf16[256,2048]{1,0:T(8,128)(2,1)S(1)}, bf16[256,2048]{1,0:T(8,128)(2,1)S(1)}, u32[]{:S(2)}, u32[]{:S(2)}) collective-permute-start(bf16[256,2048]{1,0:T(8,128)(2,1)S(1)} %add_convert_fusion.12), channel_id=1, source_target_pairs={{0,2},{2,0},{1,3},{3,1},{4,6},{6,4},{5,7},{7,5},{8,10},{10,8},{9,1... | collective-permute-start | bytes 3145736 | tf_op jit(solution)/shard_map/ppermute | solution.py:59
  654.3 44.4 %collective-permute-start.14 = (bf16[256,2048]{1,0:T(8,128)(2,1)}, bf16[256,2048]{1,0:T(8,128)(2,1)S(1)}, u32[]{:S(2)}, u32[]{:S(2)}) collective-permute-start(bf16[256,2048]{1,0:T(8,128)(2,1)} %slice.1108), channel_id=1, source_target_pairs={{0,2},{2,0},{1,3},{3,1},{4,6},{6,4},{5,7},{7,5},{8,10},{10,8},{9,1... | collective-permute-start | bytes 3145736 | tf_op jit(solution)/shard_map/ppermute | solution.py:59
  656.1 43.0 %collective-permute-start.19 = (bf16[256,2048]{1,0:T(8,128)(2,1)}, bf16[256,2048]{1,0:T(8,128)(2,1)S(1)}, u32[]{:S(2)}, u32[]{:S(2)}) collective-permute-start(bf16[256,2048]{1,0:T(8,128)(2,1)} %slice.1116), channel_id=1, source_target_pairs={{0,16},{16,0},{1,17},{17,1},{2,18},{18,2},{3,19},{19,3},{4,20},{20... | collective-permute-start | bytes 3145736 | tf_op jit(solution)/shard_map/ppermute | solution.py:59
  657.7 62.5 %collective-permute-start.18 = (bf16[256,2048]{1,0:T(8,128)(2,1)S(1)}, bf16[256,2048]{1,0:T(8,128)(2,1)S(1)}, u32[]{:S(2)}, u32[]{:S(2)}) collective-permute-start(bf16[256,2048]{1,0:T(8,128)(2,1)S(1)} %add_convert_fusion.15), channel_id=1, source_target_pairs={{0,16},{16,0},{1,17},{17,1},{2,18},{18,2},{3,19},{19,3},{4,20},{20... | collective-permute-start | bytes 3145736 | tf_op jit(solution)/shard_map/ppermute | solution.py:59
  676.7 43.5 %collective-permute-start.21 = (bf16[256,2048]{1,0:T(8,128)(2,1)S(1)}, bf16[256,2048]{1,0:T(8,128)(2,1)S(1)}, u32[]{:S(2)}, u32[]{:S(2)}) collective-permute-start(bf16[256,2048]{1,0:T(8,128)(2,1)S(1)} %add_convert_fusion.14), channel_id=1, source_target_pairs={{0,2},{2,0},{1,3},{3,1},{4,6},{6,4},{5,7},{7,5},{8,10},{10,8},{9,1... | collective-permute-start | bytes 3145736 | tf_op jit(solution)/shard_map/ppermute | solution.py:59
  731.4 20.6 %collective-permute-start.55 = (bf16[512,1024]{1,0:T(8,128)(2,1)S(1)}, bf16[512,1024]{1,0:T(8,128)(2,1)S(1)}, u32[]{:S(2)}, u32[]{:S(2)}) collective-permute-start(bf16[512,1024]{1,0:T(8,128)(2,1)S(1)} %convolution_convert_fusion.18), channel_id=1, source_target_pairs={{0,1},{1,0},{2,3},{3,2},{4,5},{5,4},{6,7},{7,6},{8,9},{9,8},{10,11... | collective-permute-start | bytes 3145736 | tf_op jit(solution)/shard_map/ppermute | solution.py:59
  734.9 24.0 %collective-permute-start.57 = (bf16[256,1024]{1,0:T(8,128)(2,1)S(1)}, bf16[256,1024]{1,0:T(8,128)(2,1)S(1)}, u32[]{:S(2)}, u32[]{:S(2)}) collective-permute-start(bf16[256,1024]{1,0:T(8,128)(2,1)S(1)} %slice.1186), channel_id=1, source_target_pairs={{0,2},{2,0},{1,3},{3,1},{4,6},{6,4},{5,7},{7,5},{8,10},{10,8},{9,1... | collective-permute-start | bytes 1572872 | tf_op jit(solution)/shard_map/ppermute | solution.py:59
  738.1 23.8 %collective-permute-start.62 = (bf16[256,1024]{1,0:T(8,128)(2,1)S(1)}, bf16[256,1024]{1,0:T(8,128)(2,1)S(1)}, u32[]{:S(2)}, u32[]{:S(2)}) collective-permute-start(bf16[256,1024]{1,0:T(8,128)(2,1)S(1)} %slice.1190), channel_id=1, source_target_pairs={{0,16},{16,0},{1,17},{17,1},{2,18},{18,2},{3,19},{19,3},{4,20},{20... | collective-permute-start | bytes 1572872 | tf_op jit(solution)/shard_map/ppermute | solution.py:59
  747.9 23.7 %collective-permute-start.61 = (bf16[256,1024]{1,0:T(8,128)(2,1)S(1)}, bf16[256,1024]{1,0:T(8,128)(2,1)S(1)}, u32[]{:S(2)}, u32[]{:S(2)}) collective-permute-start(bf16[256,1024]{1,0:T(8,128)(2,1)S(1)} %add_convert_fusion.19), channel_id=1, source_target_pairs={{0,16},{16,0},{1,17},{17,1},{2,18},{18,2},{3,19},{19,3},{4,20},{20... | collective-permute-start | bytes 1572872 | tf_op jit(solution)/shard_map/ppermute | solution.py:59
  750.8 20.8 %collective-permute-start.64 = (bf16[256,1024]{1,0:T(8,128)(2,1)S(1)}, bf16[256,1024]{1,0:T(8,128)(2,1)S(1)}, u32[]{:S(2)}, u32[]{:S(2)}) collective-permute-start(bf16[256,1024]{1,0:T(8,128)(2,1)S(1)} %add_convert_fusion.18), channel_id=1, source_target_pairs={{0,2},{2,0},{1,3},{3,1},{4,6},{6,4},{5,7},{7,5},{8,10},{10,8},{9,1... | collective-permute-start | bytes 1572872 | tf_op jit(solution)/shard_map/ppermute | solution.py:59
  773.2 210.4 %reduce-scatter.10.cloned.1.call-start = ((), (), s32[]{:S(2)}) async-start(), calls=%async_computation.11 | async-start | bytes 5242880 | tf_op jit(solution)/shard_map/reduce_scatter | solution.py:449
  797.2 188.6 %reduce-scatter.12.cloned.1.call-start = ((), (), s32[]{:S(2)}) async-start(), calls=%async_computation.12 | async-start | bytes 5242880 | tf_op jit(solution)/shard_map/reduce_scatter | solution.py:449
  821.2 215.6 %reduce-scatter.14.cloned.1.call-start = ((), (), s32[]{:S(2)}) async-start(), calls=%async_computation.13 | async-start | bytes 5242880 | tf_op jit(solution)/shard_map/reduce_scatter | solution.py:432
  848.9 277.4 %reduce-scatter.6.cloned.1.call-start = ((), (), s32[]{:S(2)}) async-start(), calls=%async_computation.9 | async-start | bytes 2129920 | tf_op jit(solution)/shard_map/reduce_scatter | solution.py:537
  908.0 41.9 %collective-permute-start.41 = (bf16[512,1536]{1,0:T(8,128)(2,1)}, bf16[512,1536]{1,0:T(8,128)(2,1)S(1)}, u32[]{:S(2)}, u32[]{:S(2)}) collective-permute-start(bf16[512,1536]{1,0:T(8,128)(2,1)} %convolution_convert_fusion.9), channel_id=1, source_target_pairs={{0,1},{1,0},{2,3},{3,2},{4,5},{5,4},{6,7},{7,6},{8,9},{9,8},{10,11... | collective-permute-start | bytes 4718600 | tf_op jit(solution)/shard_map/ppermute | solution.py:59
  908.6 18.1 %collective-permute-start.44 = (bf16[512,1536]{1,0:T(8,128)(2,1)S(1)}, bf16[512,1536]{1,0:T(8,128)(2,1)S(1)}, u32[]{:S(2)}, u32[]{:S(2)}) collective-permute-start(bf16[512,1536]{1,0:T(8,128)(2,1)S(1)} %convolution_convert_fusion.5), channel_id=1, source_target_pairs={{0,1},{1,0},{2,3},{3,2},{4,5},{5,4},{6,7},{7,6},{8,9},{9,8},{10,11... | collective-permute-start | bytes 4718600 | tf_op jit(solution)/shard_map/ppermute | solution.py:59
  919.6 20.5 %collective-permute-start.46 = (bf16[256,1536]{1,0:T(8,128)(2,1)S(1)}, bf16[256,1536]{1,0:T(8,128)(2,1)S(1)}, u32[]{:S(2)}, u32[]{:S(2)}) collective-permute-start(bf16[256,1536]{1,0:T(8,128)(2,1)S(1)} %get-tuple-element.146), channel_id=1, source_target_pairs={{0,2},{2,0},{1,3},{3,1},{4,6},{6,4},{5,7},{7,5},{8,10},{10,8},{9,1... | collective-permute-start | bytes 2359304 | tf_op jit(solution)/shard_map/ppermute | solution.py:59
  924.3 32.8 %collective-permute-start.43 = (bf16[256,1536]{1,0:T(8,128)(2,1)}, bf16[256,1536]{1,0:T(8,128)(2,1)}, u32[]{:S(2)}, u32[]{:S(2)}) collective-permute-start(bf16[256,1536]{1,0:T(8,128)(2,1)} %slice.1158), channel_id=1, source_target_pairs={{0,2},{2,0},{1,3},{3,1},{4,6},{6,4},{5,7},{7,5},{8,10},{10,8},{9,1... | collective-permute-start | bytes 2359304 | tf_op jit(solution)/shard_map/ppermute | solution.py:59
  925.2 20.4 %collective-permute-start.49 = (bf16[256,1536]{1,0:T(8,128)(2,1)S(1)}, bf16[256,1536]{1,0:T(8,128)(2,1)S(1)}, u32[]{:S(2)}, u32[]{:S(2)}) collective-permute-start(bf16[256,1536]{1,0:T(8,128)(2,1)S(1)} %get-tuple-element.147), channel_id=1, source_target_pairs={{0,16},{16,0},{1,17},{17,1},{2,18},{18,2},{3,19},{19,3},{4,20},{20... | collective-permute-start | bytes 2359304 | tf_op jit(solution)/shard_map/ppermute | solution.py:59
  928.7 33.9 %collective-permute-start.48 = (bf16[256,1536]{1,0:T(8,128)(2,1)}, bf16[256,1536]{1,0:T(8,128)(2,1)}, u32[]{:S(2)}, u32[]{:S(2)}) collective-permute-start(bf16[256,1536]{1,0:T(8,128)(2,1)} %slice.1162), channel_id=1, source_target_pairs={{0,16},{16,0},{1,17},{17,1},{2,18},{18,2},{3,19},{19,3},{4,20},{20... | collective-permute-start | bytes 2359304 | tf_op jit(solution)/shard_map/ppermute | solution.py:59
  941.2 37.0 %collective-permute-start.47 = (bf16[256,1536]{1,0:T(8,128)(2,1)}, bf16[256,1536]{1,0:T(8,128)(2,1)}, u32[]{:S(2)}, u32[]{:S(2)}) collective-permute-start(bf16[256,1536]{1,0:T(8,128)(2,1)} %add_convert_fusion.17), channel_id=1, source_target_pairs={{0,16},{16,0},{1,17},{17,1},{2,18},{18,2},{3,19},{19,3},{4,20},{20... | collective-permute-start | bytes 2359304 | tf_op jit(solution)/shard_map/ppermute | solution.py:59
  946.8 31.4 %collective-permute-start.50 = (bf16[256,1536]{1,0:T(8,128)(2,1)}, bf16[256,1536]{1,0:T(8,128)(2,1)}, u32[]{:S(2)}, u32[]{:S(2)}) collective-permute-start(bf16[256,1536]{1,0:T(8,128)(2,1)} %add_convert_fusion.16), channel_id=1, source_target_pairs={{0,2},{2,0},{1,3},{3,1},{4,6},{6,4},{5,7},{7,5},{8,10},{10,8},{9,1... | collective-permute-start | bytes 2359304 | tf_op jit(solution)/shard_map/ppermute | solution.py:59
  982.1 56.2 %collective-permute-start.65 = (bf16[128,1024]{1,0:T(8,128)(2,1)}, bf16[128,1024]{1,0:T(8,128)(2,1)}, u32[]{:S(2)}, u32[]{:S(2)}) collective-permute-start(bf16[128,1024]{1,0:T(8,128)(2,1)} %reduce-scatter.8.cloned.1.call-done), channel_id=1, source_target_pairs={{0,16},{16,0},{1,17},{17,1},{2,18},{18,2},{3,19},{19,3},{4,20},{20... | collective-permute-start | bytes 786440 | tf_op jit(solution)/shard_map/ppermute | solution.py:59
  984.9 55.5 %collective-permute-start.66 = (bf16[256,1024]{1,0:T(8,128)(2,1)S(1)}, bf16[256,1024]{1,0:T(8,128)(2,1)S(1)}, u32[]{:S(2)}, u32[]{:S(2)}) collective-permute-start(bf16[256,1024]{1,0:T(8,128)(2,1)S(1)} %broadcast_select_fusion.20), channel_id=1, source_target_pairs={{0,2},{2,0},{1,3},{3,1},{4,6},{6,4},{5,7},{7,5},{8,10},{10,8},{9,1... | collective-permute-start | bytes 1572872 | tf_op jit(solution)/shard_map/ppermute | solution.py:59
  987.1 53.4 %collective-permute-start.70 = (bf16[256,1024]{1,0:T(8,128)(2,1)S(1)}, bf16[256,1024]{1,0:T(8,128)(2,1)S(1)}, u32[]{:S(2)}, u32[]{:S(2)}) collective-permute-start(bf16[256,1024]{1,0:T(8,128)(2,1)S(1)} %broadcast_select_fusion.16), channel_id=1, source_target_pairs={{0,2},{2,0},{1,3},{3,1},{4,6},{6,4},{5,7},{7,5},{8,10},{10,8},{9,1... | collective-permute-start | bytes 1572872 | tf_op jit(solution)/shard_map/ppermute | solution.py:59
  1036.8 26.2 %collective-permute-start.74 = (bf16[256,2048]{1,0:T(8,128)(2,1)}, bf16[256,2048]{1,0:T(8,128)(2,1)S(1)}, u32[]{:S(2)}, u32[]{:S(2)}) collective-permute-start(bf16[256,2048]{1,0:T(8,128)(2,1)} %reduce-scatter.14.cloned.1.call-done), channel_id=1, source_target_pairs={{0,16},{16,0},{1,17},{17,1},{2,18},{18,2},{3,19},{19,3},{4,20},{20... | collective-permute-start | bytes 3145736 | tf_op jit(solution)/shard_map/ppermute | solution.py:59
  1043.8 41.7 %collective-permute-start.73 = (bf16[512,1024]{1,0:T(8,128)(2,1)S(1)}, bf16[512,1024]{1,0:T(8,128)(2,1)S(1)}, u32[]{:S(2)}, u32[]{:S(2)}) collective-permute-start(bf16[512,1024]{1,0:T(8,128)(2,1)S(1)} %pad_maximum_fusion.6), channel_id=1, source_target_pairs={{0,16},{16,0},{1,17},{17,1},{2,18},{18,2},{3,19},{19,3},{4,20},{20... | collective-permute-start | bytes 3145736 | tf_op jit(solution)/shard_map/ppermute | solution.py:59
  1044.8 61.7 %collective-permute-start.69 = (bf16[512,1024]{1,0:T(8,128)(2,1)S(1)}, bf16[512,1024]{1,0:T(8,128)(2,1)S(1)}, u32[]{:S(2)}, u32[]{:S(2)}) collective-permute-start(bf16[512,1024]{1,0:T(8,128)(2,1)S(1)} %pad_maximum_fusion.5), channel_id=1, source_target_pairs={{0,16},{16,0},{1,17},{17,1},{2,18},{18,2},{3,19},{19,3},{4,20},{20... | collective-permute-start | bytes 3145736 | tf_op jit(solution)/shard_map/ppermute | solution.py:59
  (73 other events, 913.1 us)
Sparse Core Ops, SparseCore 0:
  10.8 136.2 all-gather.4
  149.3 76.1 all-gather.6
  227.6 148.1 all-gather.8
  377.9 78.9 all-gather.10
  773.4 25.4 reduce-scatter.7
  801.6 75.3 reduce-scatter.9
  879.8 77.2 reduce-scatter.11
  959.5 77.2 reduce-scatter.13
  1039.1 37.9 reduce-scatter.5

commit v3 on v2

--- a/solution.py
+++ b/solution.py
@@ -51,7 +51,8 @@
     )
 
 
-GROUP = ("slow", "chip", "core")
+REPLICA_AXIS, SLOW_AXIS, CHIP_AXIS, CORE_AXIS = "replica", "slow", "chip", "core"
+GROUP = (SLOW_AXIS, CHIP_AXIS, CORE_AXIS)
 LANES = 128
 
 
@@ -72,12 +73,12 @@
 
 def gather_tokens(rows):
     half = rows.shape[0] // 2
-    beside = swap(rows, "chip")
-    across = swap(rows, "replica")
-    corner_low = swap(beside[:half], "replica")
-    corner_high = swap(across[half:], "chip")
+    beside = swap(rows, CHIP_AXIS)
+    across = swap(rows, REPLICA_AXIS)
+    corner_low = swap(beside[:half], REPLICA_AXIS)
+    corner_high = swap(across[half:], CHIP_AXIS)
     plane = [rows, beside, across, corner_low, corner_high]
-    return plane, [swap(part, "core") for part in plane]
+    return plane, [swap(part, CORE_AXIS) for part in plane]
 
 
 def narrow(value):
@@ -85,20 +86,20 @@
 
 
 def scatter_pieces(mine, partner):
-    partner = [swap(part, "core") for part in partner]
+    partner = [swap(part, CORE_AXIS) for part in partner]
     own, beside, across, corner = (
         add_parts(keep, send) for keep, send in zip(mine, partner, strict=True)
     )
     half = own.shape[0] // 2
     corner = narrow(corner)
-    beside_low = swap(narrow(beside[:half]), "chip")
-    across_high = swap(narrow(across[half:]), "replica")
-    corner_low = swap(corner[:half], "chip")
-    corner_high = swap(corner[half:], "replica")
+    beside_low = swap(narrow(beside[:half]), CHIP_AXIS)
+    across_high = swap(narrow(across[half:]), REPLICA_AXIS)
+    corner_low = swap(corner[:half], CHIP_AXIS)
+    corner_high = swap(corner[half:], REPLICA_AXIS)
     across_low = narrow(add_parts(narrow(across[:half]), corner_low))
     beside_high = narrow(add_parts(narrow(beside[half:]), corner_high))
-    across_low = swap(across_low, "replica")
-    beside_high = swap(beside_high, "chip")
+    across_low = swap(across_low, REPLICA_AXIS)
+    beside_high = swap(beside_high, CHIP_AXIS)
     return jnp.concatenate(
         [
             add_parts(own[:half], beside_low, across_low),
@@ -246,7 +247,7 @@
             bytes_accessed=rows * (both * 6 + width * 2) + down.size * 2,
             transcendentals=rows * both // 2,
         ),
-        name="hidden_backward",
+        name="hb",
     )(wide, grads, down)
 
 
@@ -309,7 +310,7 @@
         scratch_shapes=[pltpu.VMEM((length, length), jnp.float32)],
         compiler_params=params,
         cost_estimate=kernel_cost(length, 2),
-        name="attend_forward",
+        name="af",
     )
     backward = pl.pallas_call(
         attend_backward,
@@ -327,7 +328,7 @@
         scratch_shapes=[pltpu.VMEM((length, length), jnp.float32)],
         compiler_params=params,
         cost_estimate=kernel_cost(length, 5),
-        name="attend_backward",
+        name="ab",
     )
     return forward, backward
 
@@ -348,15 +349,15 @@
 ):
     token_length, _ = tokens.shape
     row_count, hidden_width = gate_weight.shape
-    slow = lax.axis_size("slow")
+    slow = lax.axis_size(SLOW_AXIS)
     unit = hidden_width // (slow * 8)
     local_hidden = slow * unit
     query_width = query_weight.shape[1]
     key_width = key_projection_weight.shape[1]
     qkv_width = query_width + 2 * key_width
-    first_replica = lax.axis_index("replica") == 0
-    first_chip = lax.axis_index("chip") == 0
-    first_core = lax.axis_index("core") == 0
+    first_replica = lax.axis_index(REPLICA_AXIS) == 0
+    first_chip = lax.axis_index(CHIP_AXIS) == 0
+    first_core = lax.axis_index(CORE_AXIS) == 0
 
     gain_columns = jnp.pad(
         jnp.stack([attn_gain, mlp_gain], axis=1), ((0, 0), (0, LANES - 2))
@@ -392,13 +393,13 @@
         jnp.concatenate(packed[2:], axis=0),
     )
     wide_blocks = []
-    for block in order(first_chip, near, swap(far, "chip")):
+    for block in order(first_chip, near, swap(far, CHIP_AXIS)):
         near, far = order(first_core, block[:row_count], block[row_count:])
-        wide_blocks.extend(order(first_core, near, swap(far, "core")))
+        wide_blocks.extend(order(first_core, near, swap(far, CORE_AXIS)))
     wide_local = jnp.concatenate(wide_blocks, axis=0)
     down_local = jnp.where(first_replica, down_weight[:unit], down_weight[unit:])
-    wide_all = lax.all_gather(wide_local, "slow", axis=0, tiled=True)
-    down_all = lax.all_gather(down_local, "slow", axis=0, tiled=True)
+    wide_all = lax.all_gather(wide_local, SLOW_AXIS, axis=0, tiled=True)
+    down_all = lax.all_gather(down_local, SLOW_AXIS, axis=0, tiled=True)
 
     gains = qkv_all[:, qkv_width:][:, :2].T.astype(jnp.float32)
     attn_scale, mlp_scale = gains[0], gains[1]
@@ -417,7 +418,8 @@
     query_rows, key_rows, value_rows, mixed, logsum = attend_forward_call(
         projected, projected, projected, *tables
     )
-    residual = inputs + RESIDUAL * matrix_product(mixed, output_all)
+    attn_out = matrix_product(mixed, output_all)
+    residual = inputs + RESIDUAL * attn_out
     normed2 = rms_norm(residual, mlp_scale).astype(jnp.bfloat16)
     plane, partners = gather_tokens(normed2)
     normed2_all = jnp.concatenate(plane + partners, axis=0)
@@ -429,7 +431,7 @@
     gating, upward = wide[:, :local_hidden], wide[:, local_hidden:]
     hidden_act = (jax.nn.silu(gating) * upward).astype(jnp.bfloat16)
     grad_down = narrow(contract_rows(hidden_act, down_in_all))
-    down_part = lax.psum_scatter(grad_down, "slow", scatter_dimension=0, tiled=True)
+    down_part = lax.psum_scatter(grad_down, SLOW_AXIS, scatter_dimension=0, tiled=True)
 
     def pieces_of(plane_rows):
         return [plane_rows[i * token_length : (i + 1) * token_length] for i in range(4)]
@@ -446,17 +448,17 @@
     parts = []
     for start in (0, local_hidden):
         grad = narrow(contract_rows(normed2_all, wide_in[:, start : start + local_hidden]))
-        parts.append(lax.psum_scatter(grad, "slow", scatter_dimension=0, tiled=True))
+        parts.append(lax.psum_scatter(grad, SLOW_AXIS, scatter_dimension=0, tiled=True))
 
     def exchange(part):
         near, far = order(first_chip, part[: 2 * row_count], part[2 * row_count :])
-        low, high = order(first_chip, near, swap(far, "chip"))
+        low, high = order(first_chip, near, swap(far, CHIP_AXIS))
         members = []
         for block in (low, high):
             near, far = order(first_core, block[:row_count], block[row_count:])
-            members.extend(order(first_core, near, swap(far, "core")))
+            members.extend(order(first_core, near, swap(far, CORE_AXIS)))
         members = jnp.concatenate(members, axis=0)
-        sources = order(first_replica, members, swap(members, "replica"))
+        sources = order(first_replica, members, swap(members, REPLICA_AXIS))
         pieces = []
         for step in range(slow):
             for member in range(4):
@@ -471,7 +473,7 @@
 
     gate_shard, up_shard = exchange(parts[0]), exchange(parts[1])
     down_shard = jnp.concatenate(
-        order(first_replica, down_part, swap(down_part, "replica")), axis=0
+        order(first_replica, down_part, swap(down_part, REPLICA_AXIS)), axis=0
     ).astype(jnp.float32)
 
     _, norm2_pull = jax.vjp(rms_norm, residual, mlp_scale)
@@ -512,12 +514,12 @@
 
     def both_sides(part):
         return jnp.concatenate(
-            order(first_replica, part, swap(part, "replica")), axis=1
+            order(first_replica, part, swap(part, REPLICA_AXIS)), axis=1
         ).astype(jnp.float32)
 
     attn_in = (RESIDUAL * residual_grad).astype(jnp.bfloat16)
     output_part = weight_part(mixed, attn_in)
-    output_part = lax.psum_scatter(output_part, "slow", scatter_dimension=0, tiled=True)
+    output_part = lax.psum_scatter(output_part, SLOW_AXIS, scatter_dimension=0, tiled=True)
     output_shard = both_sides(output_part)
     mixed_grad = contract_cols(attn_in, output_all).astype(jnp.bfloat16)
     query_lin_grad, key_lin_grad, value_lin_grad = attend_backward_call(
@@ -530,11 +532,11 @@
     input_part, grad_attn_gain = norm1_pull(normed1_grad)
     input_grad = residual_grad + input_part
     gain_grads = jnp.stack([grad_attn_gain, grad_mlp_gain], axis=0)
-    for axis in ("core", "chip", "replica"):
+    for axis in (CORE_AXIS, CHIP_AXIS, REPLICA_AXIS):
         gain_grads = gain_grads + swap(gain_grads, axis)
     gain_rows = jnp.pad(member_columns(gain_grads)[0][0].T, ((0, 0), (0, LANES - 2)))
     qkv_sum = jnp.concatenate([qkv_sum, gain_rows.astype(jnp.bfloat16)], axis=1)
-    qkv_part = lax.psum_scatter(qkv_sum, "slow", scatter_dimension=0, tiled=True)
+    qkv_part = lax.psum_scatter(qkv_sum, SLOW_AXIS, scatter_dimension=0, tiled=True)
     qkv_shard = both_sides(qkv_part[:, : qkv_width // 2])
     attn_gain_shard = qkv_part[:, qkv_width // 2].astype(jnp.float32)
     mlp_gain_shard = qkv_part[:, qkv_width // 2 + 1].astype(jnp.float32)
@@ -554,14 +556,14 @@
 
 
 def solution(mesh):
-    replicas, shard_count = mesh.shape["replica"], mesh.shape["shard"]
+    replicas, shard_count = mesh.shape[REPLICA_AXIS], mesh.shape["shard"]
     inner = KEY_VALUE_HEADS // replicas
     cores = 2
     split_mesh = Mesh(
         mesh.devices.reshape(replicas, shard_count // inner, inner // cores, cores),
-        ("replica", "slow", "chip", "core"),
-    )
-    everyone = P(("replica", "slow", "chip", "core"), None)
+        (REPLICA_AXIS, *GROUP),
+    )
+    everyone = P((REPLICA_AXIS, *GROUP), None)
     sharded = P(GROUP, None)
     vector = P(GROUP)
     return jax.shard_map(

time: 1150 us -> 1150 us (level)
  no operation moved by 1% of the time
where the time goes in v3:
time: 1150 us
  waiting for transfers between devices  539 us (47%)
  matrix products  247 us (21%)
  other arithmetic  102 us (9%)
  local copies, waits for them, and re-layouts  99 us (9%)
  Pallas kernels  83.3 us (7%)
  starting transfers between devices  62.4 us (5%)
  between operations  15.6 us (1%)
    ppermute x75, waiting for transfers between devices, swap(): return lax.ppermute(value, axis, [(0, 1), (1, 0)])  377 us
    dot_general x5, matrix products, matrix_product(): return jnp.dot(left_side, right_side, preferred_element_type=jnp.float32)  91.1 us
    dot_general x19, matrix products, contract_rows(): lax.dot_general(left_side, right_side, (((0,), (0,)), ((), ())), preferre...  89.8 us
    unnamed x187, local copies, waits for them, and re-layouts  66.9 us
    dot_general x4, matrix products, contract_cols(): lax.dot_general(left_side, right_side, (((1,), (1,)), ((), ())), preferre...  65.8 us
    ppermute x75, starting transfers between devices, swap(): return lax.ppermute(value, axis, [(0, 1), (1, 0)])  61.5 us
    all_gather x1, waiting for transfers between devices, layer(): wide_all = lax.all_gather(wide_local, SLOW_AXIS, axis=0, tiled=True)  52.8 us
    reduce_scatter x1, waiting for transfers between devices, layer(): lax.psum_scatter(grad_down, SLOW_AXIS, scatter_dimension=0, tiled=True)  48.5 us
  transfers between devices with their start and end apart: 84, of which 38 were waited for; matrix products, arithmetic and copies ran while one was open for 34% of the time, Pallas kernels for 5%

profile of v3, /device:TPU:0, one launch (start us, length us, event | category | flops | bytes accessed | tf_op | source)
XLA Modules:
  0.0 1147.8 jit_solution(7346692589652476412)
XLA Ops:
  20.2 3.1 collective-permute-start.9
  23.3 32.0 %collective-permute-done.9 = bf16[256,2048]{1,0:T(8,128)(2,1)} collective-permute-done((bf16[256,2048]{1,0:T(8,128)(2,1)S(1)}, bf16[256,2048]{1,0:T(8,128)(2,1)}, u32[]{:S(2)}, u32[]{:S(2)}) %collective-permute-start.9) | collective-permute-done | bytes 1048608 | tf_op jit(solution)/shard_map/ppermute | solution.py:60
  75.5 38.0 %collective-permute-done.23 = bf16[512,2048]{1,0:T(8,128)(2,1)} collective-permute-done((bf16[512,2048]{1,0:T(8,128)(2,1)}, bf16[512,2048]{1,0:T(8,128)(2,1)}, u32[]{:S(2)}, u32[]{:S(2)}) %collective-permute-start.23) | collective-permute-done | bytes 2097184 | tf_op jit(solution)/shard_map/ppermute | solution.py:60
  113.4 2.3 slice.1120
  117.2 25.3 %collective-permute-done.22 = bf16[512,2048]{1,0:T(8,128)(2,1)} collective-permute-done((bf16[512,2048]{1,0:T(8,128)(2,1)}, bf16[512,2048]{1,0:T(8,128)(2,1)}, u32[]{:S(2)}, u32[]{:S(2)}) %collective-permute-start.22) | collective-permute-done | bytes 2097184 | tf_op jit(solution)/shard_map/ppermute | solution.py:60
  151.1 12.6 %fusion.66.query.key.value = f32[512,3200]{1,0:T(8,128)} fusion(bf16[512,2048]{1,0:T(8,128)(2,1)S(1)} %fusion.19, bf16[2048,3200]{1,0:T(8,128)(2,1)} %all-gather.5.cloned.1.call-done), kind=kOutput, calls=%fused_computation.355 | convolution fusion | flops 6710886400 | bytes 21757952 | tf_op jit(solution)/shard_map/dot_general | solution.py:39
  163.6 22.8 %af.1 = (bf16[512,2048]{1,0:T(8,128)(2,1)S(1)}, bf16[512,512]{1,0:T(8,128)(2,1)S(1)}, bf16[512,512]{1,0:T(8,128)(2,1)S(1)}, bf16[512,2048]{1,0:T(8,128)(2,1)S(1)}, f32[32,512]{1,0:T(8,128)S(1)}) custom-call(f32[512,3200]{1,0:T(8,128)} %fusion.66.query.key.value, f32[512,3200]{1,0:T(8,128)} %fusion.66.query.key.value, f32[512,3200]{1,0:T(8,128)} %fusion.66.query.key.value, ...), custom_call_target="tpu_custom_call" | custom-call | flops 2147483648 | bytes 12582912 | tf_op jit(solution)/shard_map/af/pallas_call | solution.py:418
  188.6 36.9 %all-gather.7.cloned.1.call-done = bf16[2048,2048]{1,0:T(8,128)(2,1)} async-done(((bf16[128,2048]{1,0:T(8,128)(2,1)}), bf16[2048,2048]{1,0:T(8,128)(2,1)}) %all-gather.7.cloned.1.call-update) | async-done | bytes 8388624 | tf_op jit(solution)/shard_map/all_gather | solution.py:113
  225.5 8.7 multiply_reduce_fusion.2
  237.7 3.4 constant_dynamic-update-slice_fusion.50
  242.6 3.2 constant_dynamic-update-slice_fusion.49
  245.8 2.3 constant_dynamic-update-slice_fusion.48
  251.0 3.3 constant_dynamic-update-slice_fusion.46
  254.2 3.2 constant_dynamic-update-slice_fusion.45
  257.4 3.2 constant_dynamic-update-slice_fusion.44
  261.7 23.1 %collective-permute-done = bf16[512,2048]{1,0:T(8,128)(2,1)S(1)} collective-permute-done((bf16[512,2048]{1,0:T(8,128)(2,1)S(1)}, bf16[512,2048]{1,0:T(8,128)(2,1)S(1)}, u32[]{:S(2)}, u32[]{:S(2)}) %collective-permute-start) | collective-permute-done | bytes 2097184 | tf_op jit(solution)/shard_map/ppermute | solution.py:60
  285.9 2.8 collective-permute-done.1
  297.9 15.2 %collective-permute-done.3 = bf16[256,2048]{1,0:T(8,128)(2,1)S(1)} collective-permute-done((bf16[256,2048]{1,0:T(8,128)(2,1)S(1)}, bf16[256,2048]{1,0:T(8,128)(2,1)S(1)}, u32[]{:S(2)}, u32[]{:S(2)}) %collective-permute-start.3) | collective-permute-done | bytes 1048608 | tf_op jit(solution)/shard_map/ppermute | solution.py:60
  323.0 52.8 %all-gather.9.cloned.1.call-done = bf16[2048,2048]{1,0:T(8,128)(2,1)} async-done(((bf16[512,2048]{1,0:T(8,128)(2,1)}), bf16[2048,2048]{1,0:T(8,128)(2,1)}) %all-gather.9.cloned.1.call-update) | async-done | bytes 8388624 | tf_op jit(solution)/shard_map/all_gather | solution.py:401
  375.9 43.4 %fusion.67.wide = f32[4096,2048]{1,0:T(8,128)} fusion(bf16[4096,2048]{1,0:T(8,128)(2,1)} %constant_dynamic-update-slice_fusion, bf16[2048,2048]{1,0:T(8,128)(2,1)} %all-gather.9.cloned.1.call-done), kind=kOutput, calls=%fused_computation.356 | convolution fusion | flops 34359738368 | bytes 58720256 | tf_op jit(solution)/shard_map/dot_general | solution.py:39
  419.3 15.2 %fusion = bf16[4096,1024]{1,0:T(8,128)(2,1)} fusion(f32[4096,2048]{1,0:T(8,128)} %fusion.67.wide), kind=kLoop, calls=%fused_computation.1 | loop fusion | flops 25165824 | bytes 41943040 | tf_op jit(solution)/shard_map/convert_element_type | solution.py:432
  434.4 22.4 %all-gather.11.cloned.1.call-done.down = bf16[1024,2048]{1,0:T(8,128)(2,1)} async-done(((bf16[256,2048]{1,0:T(8,128)(2,1)}), bf16[1024,2048]{1,0:T(8,128)(2,1)}) %all-gather.11.cloned.1.call-update) | async-done | bytes 4194320 | tf_op jit(solution)/shard_map/all_gather | solution.py:402
  456.8 30.8 %hb.1 = bf16[4096,2048]{1,0:T(8,128)(2,1)} custom-call(f32[4096,2048]{1,0:T(8,128)} %fusion.67.wide, bf16[4096,2048]{1,0:T(8,128)(2,1)} %constant_dynamic-update-slice_fusion.42.grads, bf16[1024,2048]{1,0:T(8,128)(2,1)} %all-gather.11.cloned.1.call-done.down), custom_call_target="tpu_custom_call" | custom-call | flops 17179869184 | bytes 71303168 | tf_op jit(solution)/shard_map/hb/pallas_call | solution.py:232
  487.6 22.8 %fusion.14 = bf16[2048,2048]{1,0:T(8,128)(2,1)S(1)} fusion(bf16[2048,2048]{1,0:T(8,128)(2,1)} %all-gather.9.cloned.1.call-done, bf16[4096,2048]{1,0:T(8,128)(2,1)} %hb.1), kind=kOutput, calls=%fused_computation.18 | convolution fusion | flops 17184063488 | bytes 25165824 | tf_op jit(solution)/shard_map/dot_general | solution.py:49
  510.5 4.2 fusion.57
  515.7 14.1 %convolution_convert_fusion = bf16[2048,2048]{1,0:T(8,128)(2,1)} fusion(bf16[1024,2048]{1,0:T(8,128)(2,1)S(1)} %copy-done.15, bf16[4096,1024]{1,0:T(8,128)(2,1)} %fusion), kind=kOutput, calls=%fused_computation.19 | convolution fusion | flops 8594128896 | bytes 16777216 | tf_op jit(solution)/shard_map/dot_general | solution.py:39
  529.9 6.0 fusion.58
  535.9 22.1 %fusion.11 = bf16[2048,2048]{1,0:T(8,128)(2,1)} fusion(bf16[2048,2048]{1,0:T(8,128)(2,1)} %all-gather.9.cloned.1.call-done, bf16[4096,2048]{1,0:T(8,128)(2,1)S(1)} %bitcast.46), kind=kOutput, calls=%fused_computation.17 | convolution fusion | flops 17184063488 | bytes 25165824 | tf_op jit(solution)/shard_map/dot_general | solution.py:49
  559.0 12.3 %convolution_convert_fusion.1 = bf16[2048,2048]{1,0:T(8,128)(2,1)S(1)} fusion(bf16[1024,2048]{1,0:T(8,128)(2,1)} %all-gather.11.cloned.1.call-done.down, bf16[4096,1024]{1,0:T(8,128)(2,1)} %fusion), kind=kOutput, calls=%fused_computation.20 | convolution fusion | flops 8594128896 | bytes 16777216 | tf_op jit(solution)/shard_map/dot_general | solution.py:39
  571.4 5.9 add_convert_fusion.1
  584.9 6.1 add_convert_fusion.4
  594.8 33.4 %collective-permute-done.36 = bf16[256,2048]{1,0:T(8,128)(2,1)} collective-permute-done((bf16[256,2048]{1,0:T(8,128)(2,1)}, bf16[256,2048]{1,0:T(8,128)(2,1)}, u32[]{:S(2)}, u32[]{:S(2)}) %collective-permute-start.36) | collective-permute-done | bytes 1048608 | tf_op jit(solution)/shard_map/ppermute | solution.py:60
  633.8 16.3 %collective-permute-done.17 = bf16[256,2048]{1,0:T(8,128)(2,1)S(1)} collective-permute-done((bf16[256,2048]{1,0:T(8,128)(2,1)S(1)}, bf16[256,2048]{1,0:T(8,128)(2,1)S(1)}, u32[]{:S(2)}, u32[]{:S(2)}) %collective-permute-start.17) | collective-permute-done | bytes 1048608 | tf_op jit(solution)/shard_map/ppermute | solution.py:60
  658.2 18.5 %collective-permute-done.37 = bf16[256,2048]{1,0:T(8,128)(2,1)S(1)} collective-permute-done((bf16[256,2048]{1,0:T(8,128)(2,1)S(1)}, bf16[256,2048]{1,0:T(8,128)(2,1)S(1)}, u32[]{:S(2)}, u32[]{:S(2)}) %collective-permute-start.37) | collective-permute-done | bytes 1048608 | tf_op jit(solution)/shard_map/ppermute | solution.py:60
  678.2 2.9 fusion.37
  682.2 16.4 %collective-permute-done.14 = bf16[256,2048]{1,0:T(8,128)(2,1)S(1)} collective-permute-done((bf16[256,2048]{1,0:T(8,128)(2,1)}, bf16[256,2048]{1,0:T(8,128)(2,1)S(1)}, u32[]{:S(2)}, u32[]{:S(2)}) %collective-permute-start.14) | collective-permute-done | bytes 1048608 | tf_op jit(solution)/shard_map/ppermute | solution.py:60
  699.2 21.0 %collective-permute-done.18 = bf16[256,2048]{1,0:T(8,128)(2,1)S(1)} collective-permute-done((bf16[256,2048]{1,0:T(8,128)(2,1)S(1)}, bf16[256,2048]{1,0:T(8,128)(2,1)S(1)}, u32[]{:S(2)}, u32[]{:S(2)}) %collective-permute-start.18) | collective-permute-done | bytes 1048608 | tf_op jit(solution)/shard_map/ppermute | solution.py:60
  721.8 3.9 multiply_convert_fusion
  738.7 9.0 collective-permute-done.60
  752.8 6.1 collective-permute-done.57
  758.9 2.9 collective-permute-done.62
  761.8 9.7 collective-permute-done.61
  773.3 23.9 %fusion.29 = bf16[2048,1024]{1,0:T(8,128)(2,1)} fusion(bf16[4096,2048]{1,0:T(8,128)(2,1)} %constant_dynamic-update-slice_fusion, bf16[4096,2048]{1,0:T(8,128)(2,1)} %hb.1), kind=kOutput, calls=%fused_computation.52 | convolution fusion | flops 17181966336 | bytes 29360128 | tf_op jit(solution)/shard_map/dot_general | solution.py:43
  797.2 23.9 %fusion.32 = bf16[2048,1024]{1,0:T(8,128)(2,1)} fusion(bf16[4096,2048]{1,0:T(8,128)(2,1)} %constant_dynamic-update-slice_fusion, bf16[4096,2048]{1,0:T(8,128)(2,1)} %hb.1), kind=kOutput, calls=%fused_computation.53 | convolution fusion | flops 17181966336 | bytes 29360128 | tf_op jit(solution)/shard_map/dot_general | solution.py:43
  824.8 24.1 %convolution_convert_fusion.2 = bf16[1024,2048]{1,0:T(8,128)(2,1)} fusion(bf16[4096,1024]{1,0:T(8,128)(2,1)} %fusion, bf16[4096,2048]{1,0:T(8,128)(2,1)} %constant_dynamic-update-slice_fusion.42.grads), kind=kOutput, calls=%fused_computation.54 | convolution fusion | flops 17181966336 | bytes 29360128 | tf_op jit(solution)/shard_map/dot_general | solution.py:43
  849.0 10.0 convolution_convert_fusion.11.mixed_grad
  859.0 29.7 %ab.1 = (bf16[512,2048]{1,0:T(8,128)(2,1)S(1)}, bf16[512,512]{1,0:T(8,128)(2,1)S(1)}, bf16[512,512]{1,0:T(8,128)(2,1)S(1)}) custom-call(bf16[512,2048]{1,0:T(8,128)(2,1)} %copy-done.1, bf16[512,512]{1,0:T(8,128)(2,1)S(1)} %get-tuple-element.21.key, bf16[512,512]{1,0:T(8,128)(2,1)S(1)} %copy-done.3, bf16[512,2048]{1,0:T(8,128)(2,1)} %convolution_convert_fusion.11.mixed_grad, ...), custom_call_target="tpu_custom_call" | custom-call | flops 5368709120 | bytes 12582912 | tf_op jit(solution)/shard_map/ab/pallas_call | solution.py:525
  890.6 10.9 fusion.20
  912.2 3.1 fusion.22
  915.8 2.7 collective-permute-done.45
  920.8 2.6 add_convert_fusion.8
  929.3 10.9 collective-permute-done.46
  942.7 3.0 collective-permute-done.49
  952.0 5.1 collective-permute-done.43
  957.1 5.5 collective-permute-done.48
  962.6 15.6 %collective-permute-done.47 = bf16[256,1536]{1,0:T(8,128)(2,1)} collective-permute-done((bf16[256,1536]{1,0:T(8,128)(2,1)}, bf16[256,1536]{1,0:T(8,128)(2,1)}, u32[]{:S(2)}, u32[]{:S(2)}) %collective-permute-start.47) | collective-permute-done | bytes 786464 | tf_op jit(solution)/shard_map/ppermute | solution.py:60
  978.2 2.5 fusion.45
  988.3 48.5 %reduce-scatter.14.cloned.1.call-done = bf16[256,2048]{1,0:T(8,128)(2,1)} async-done(((bf16[1024,2048]{1,0:T(8,128)(2,1)}), bf16[256,2048]{1,0:T(8,128)(2,1)}) %reduce-scatter.14.cloned.1.call-update) | async-done | bytes 1048592 | tf_op jit(solution)/shard_map/reduce_scatter | solution.py:434
  1046.3 16.7 %collective-permute-done.74 = bf16[256,2048]{1,0:T(8,128)(2,1)S(1)} collective-permute-done((bf16[256,2048]{1,0:T(8,128)(2,1)}, bf16[256,2048]{1,0:T(8,128)(2,1)S(1)}, u32[]{:S(2)}, u32[]{:S(2)}) %collective-permute-start.74) | collective-permute-done | bytes 1048608 | tf_op jit(solution)/shard_map/ppermute | solution.py:60
  1063.2 2.6 maximum_convert_fusion
  1065.7 19.8 %collective-permute-done.73 = bf16[512,1024]{1,0:T(8,128)(2,1)S(1)} collective-permute-done((bf16[512,1024]{1,0:T(8,128)(2,1)S(1)}, bf16[512,1024]{1,0:T(8,128)(2,1)S(1)}, u32[]{:S(2)}, u32[]{:S(2)}) %collective-permute-start.73) | collective-permute-done | bytes 1048608 | tf_op jit(solution)/shard_map/ppermute | solution.py:60
  1088.0 18.5 %collective-permute-done.69 = bf16[512,1024]{1,0:T(8,128)(2,1)S(1)} collective-permute-done((bf16[512,1024]{1,0:T(8,128)(2,1)S(1)}, bf16[512,1024]{1,0:T(8,128)(2,1)S(1)}, u32[]{:S(2)}, u32[]{:S(2)}) %collective-permute-start.69) | collective-permute-done | bytes 1048608 | tf_op jit(solution)/shard_map/ppermute | solution.py:60
  1129.5 4.0 convert_element_type.492
  1134.2 4.1 convert_element_type.490
  (466 shorter events, 205.3 us)
Async XLA Ops:
  7.2 140.0 %all-gather.5.cloned.1.call-start = ((), (), s32[]{:S(2)}) async-start(), calls=%async_computation.5 | async-start | bytes 13926400 | tf_op jit(solution)/shard_map/all_gather | solution.py:113
  10.2 215.3 %all-gather.7.cloned.1.call-start = ((), (), s32[]{:S(2)}) async-start(), calls=%async_computation.6 | async-start | bytes 8912896 | tf_op jit(solution)/shard_map/all_gather | solution.py:113
  11.0 364.9 %all-gather.9.cloned.1.call-start = ((), (), s32[]{:S(2)}) async-start(), calls=%async_computation.7 | async-start | bytes 10485760 | tf_op jit(solution)/shard_map/all_gather | solution.py:401
  20.2 35.1 %collective-permute-start.9 = (bf16[256,2048]{1,0:T(8,128)(2,1)S(1)}, bf16[256,2048]{1,0:T(8,128)(2,1)}, u32[]{:S(2)}, u32[]{:S(2)}) collective-permute-start(bf16[256,2048]{1,0:T(8,128)(2,1)S(1)} %broadcast_select_fusion.12), channel_id=1, source_target_pairs={{0,2},{2,0},{1,3},{3,1},{4,6},{6,4},{5,7},{7,5},{8,10},{10,8},{9,1... | collective-permute-start | bytes 3145736 | tf_op jit(solution)/shard_map/ppermute | solution.py:60
  61.6 395.2 %all-gather.11.cloned.1.call-start = ((), (), s32[]{:S(2)}) async-start(), calls=%async_computation.8 | async-start | bytes 5242880 | tf_op jit(solution)/shard_map/all_gather | solution.py:402
  64.9 172.0 %collective-permute-start.26 = (bf16[512,2048]{1,0:T(8,128)(2,1)}, bf16[512,2048]{1,0:T(8,128)(2,1)}, u32[]{:S(2)}, u32[]{:S(2)}) collective-permute-start(bf16[512,2048]{1,0:T(8,128)(2,1)} %fusion.21), channel_id=1, source_target_pairs={{0,1},{1,0},{2,3},{3,2},{4,5},{5,4},{6,7},{7,6},{8,9},{9,8},{10,11... | collective-permute-start | bytes 6291464 | tf_op jit(solution)/shard_map/ppermute | solution.py:60
  65.3 48.1 %collective-permute-start.23 = (bf16[512,2048]{1,0:T(8,128)(2,1)}, bf16[512,2048]{1,0:T(8,128)(2,1)}, u32[]{:S(2)}, u32[]{:S(2)}) collective-permute-start(bf16[512,2048]{1,0:T(8,128)(2,1)} %fusion.21), channel_id=1, source_target_pairs={{0,16},{16,0},{1,17},{17,1},{2,18},{18,2},{3,19},{19,3},{4,20},{20... | collective-permute-start | bytes 6291464 | tf_op jit(solution)/shard_map/ppermute | solution.py:60
  67.0 75.6 %collective-permute-start.22 = (bf16[512,2048]{1,0:T(8,128)(2,1)}, bf16[512,2048]{1,0:T(8,128)(2,1)}, u32[]{:S(2)}, u32[]{:S(2)}) collective-permute-start(bf16[512,2048]{1,0:T(8,128)(2,1)} %fusion.21), channel_id=1, source_target_pairs={{0,2},{2,0},{1,3},{3,1},{4,6},{6,4},{5,7},{7,5},{8,10},{10,8},{9,1... | collective-permute-start | bytes 6291464 | tf_op jit(solution)/shard_map/ppermute | solution.py:60
  69.5 912.6 %reduce-scatter.8.cloned.1.call-start = ((), (), s32[]{:S(2)}) async-start(), calls=%async_computation.10 | async-start | bytes 1310720 | tf_op jit(solution)/shard_map/reduce_scatter | solution.py:522
  115.7 132.4 %collective-permute-start.25 = (bf16[256,2048]{1,0:T(8,128)(2,1)}, bf16[256,2048]{1,0:T(8,128)(2,1)}, u32[]{:S(2)}, u32[]{:S(2)}) collective-permute-start(bf16[256,2048]{1,0:T(8,128)(2,1)} %slice.1120), channel_id=1, source_target_pairs={{0,2},{2,0},{1,3},{3,1},{4,6},{6,4},{5,7},{7,5},{8,10},{10,8},{9,1... | collective-permute-start | bytes 3145736 | tf_op jit(solution)/shard_map/ppermute | solution.py:60
  144.9 96.3 %collective-permute-start.24 = (bf16[256,2048]{1,0:T(8,128)(2,1)}, bf16[256,2048]{1,0:T(8,128)(2,1)}, u32[]{:S(2)}, u32[]{:S(2)}) collective-permute-start(bf16[256,2048]{1,0:T(8,128)(2,1)} %slice.1119), channel_id=1, source_target_pairs={{0,16},{16,0},{1,17},{17,1},{2,18},{18,2},{3,19},{19,3},{4,20},{20... | collective-permute-start | bytes 3145736 | tf_op jit(solution)/shard_map/ppermute | solution.py:60
  146.3 111.1 %collective-permute-start.28 = (bf16[512,2048]{1,0:T(8,128)(2,1)}, bf16[512,2048]{1,0:T(8,128)(2,1)}, u32[]{:S(2)}, u32[]{:S(2)}) collective-permute-start(bf16[512,2048]{1,0:T(8,128)(2,1)} %collective-permute-done.23), channel_id=1, source_target_pairs={{0,1},{1,0},{2,3},{3,2},{4,5},{5,4},{6,7},{7,6},{8,9},{9,8},{10,11... | collective-permute-start | bytes 6291464 | tf_op jit(solution)/shard_map/ppermute | solution.py:60
  146.4 104.1 %collective-permute-start.27 = (bf16[512,2048]{1,0:T(8,128)(2,1)}, bf16[512,2048]{1,0:T(8,128)(2,1)}, u32[]{:S(2)}, u32[]{:S(2)}) collective-permute-start(bf16[512,2048]{1,0:T(8,128)(2,1)} %collective-permute-done.22), channel_id=1, source_target_pairs={{0,1},{1,0},{2,3},{3,2},{4,5},{5,4},{6,7},{7,6},{8,9},{9,8},{10,11... | collective-permute-start | bytes 6291464 | tf_op jit(solution)/shard_map/ppermute | solution.py:60
  237.0 47.8 %collective-permute-start = (bf16[512,2048]{1,0:T(8,128)(2,1)S(1)}, bf16[512,2048]{1,0:T(8,128)(2,1)S(1)}, u32[]{:S(2)}, u32[]{:S(2)}) collective-permute-start(bf16[512,2048]{1,0:T(8,128)(2,1)S(1)} %get-tuple-element.38), channel_id=1, source_target_pairs={{0,2},{2,0},{1,3},{3,1},{4,6},{6,4},{5,7},{7,5},{8,10},{10,8},{9,1... | collective-permute-start | bytes 6291464 | tf_op jit(solution)/shard_map/ppermute | solution.py:60
  241.1 47.5 %collective-permute-start.1 = (bf16[512,2048]{1,0:T(8,128)(2,1)S(1)}, bf16[512,2048]{1,0:T(8,128)(2,1)S(1)}, u32[]{:S(2)}, u32[]{:S(2)}) collective-permute-start(bf16[512,2048]{1,0:T(8,128)(2,1)S(1)} %get-tuple-element.38), channel_id=1, source_target_pairs={{0,16},{16,0},{1,17},{17,1},{2,18},{18,2},{3,19},{19,3},{4,20},{20... | collective-permute-start | bytes 6291464 | tf_op jit(solution)/shard_map/ppermute | solution.py:60
  250.5 34.4 %collective-permute-start.30 = (bf16[256,2048]{1,0:T(8,128)(2,1)}, bf16[256,2048]{1,0:T(8,128)(2,1)S(1)}, u32[]{:S(2)}, u32[]{:S(2)}) collective-permute-start(bf16[256,2048]{1,0:T(8,128)(2,1)} %collective-permute-done.25), channel_id=1, source_target_pairs={{0,1},{1,0},{2,3},{3,2},{4,5},{5,4},{6,7},{7,6},{8,9},{9,8},{10,11... | collective-permute-start | bytes 3145736 | tf_op jit(solution)/shard_map/ppermute | solution.py:60
  260.6 55.8 %collective-permute-start.4 = (bf16[512,2048]{1,0:T(8,128)(2,1)S(1)}, bf16[512,2048]{1,0:T(8,128)(2,1)S(1)}, u32[]{:S(2)}, u32[]{:S(2)}) collective-permute-start(bf16[512,2048]{1,0:T(8,128)(2,1)S(1)} %get-tuple-element.38), channel_id=1, source_target_pairs={{0,1},{1,0},{2,3},{3,2},{4,5},{5,4},{6,7},{7,6},{8,9},{9,8},{10,11... | collective-permute-start | bytes 6291464 | tf_op jit(solution)/shard_map/ppermute | solution.py:60
  284.8 33.1 %collective-permute-start.5 = (bf16[512,2048]{1,0:T(8,128)(2,1)S(1)}, bf16[512,2048]{1,0:T(8,128)(2,1)S(1)}, u32[]{:S(2)}, u32[]{:S(2)}) collective-permute-start(bf16[512,2048]{1,0:T(8,128)(2,1)S(1)} %collective-permute-done), channel_id=1, source_target_pairs={{0,1},{1,0},{2,3},{3,2},{4,5},{5,4},{6,7},{7,6},{8,9},{9,8},{10,11... | collective-permute-start | bytes 6291464 | tf_op jit(solution)/shard_map/ppermute | solution.py:60
  288.7 24.3 %collective-permute-start.3 = (bf16[256,2048]{1,0:T(8,128)(2,1)S(1)}, bf16[256,2048]{1,0:T(8,128)(2,1)S(1)}, u32[]{:S(2)}, u32[]{:S(2)}) collective-permute-start(bf16[256,2048]{1,0:T(8,128)(2,1)S(1)} %slice.1094), channel_id=1, source_target_pairs={{0,2},{2,0},{1,3},{3,1},{4,6},{6,4},{5,7},{7,5},{8,10},{10,8},{9,1... | collective-permute-start | bytes 3145736 | tf_op jit(solution)/shard_map/ppermute | solution.py:60
  290.2 24.1 %collective-permute-start.2 = (bf16[256,2048]{1,0:T(8,128)(2,1)S(1)}, bf16[256,2048]{1,0:T(8,128)(2,1)S(1)}, u32[]{:S(2)}, u32[]{:S(2)}) collective-permute-start(bf16[256,2048]{1,0:T(8,128)(2,1)S(1)} %slice.1093), channel_id=1, source_target_pairs={{0,16},{16,0},{1,17},{17,1},{2,18},{18,2},{3,19},{19,3},{4,20},{20... | collective-permute-start | bytes 3145736 | tf_op jit(solution)/shard_map/ppermute | solution.py:60
  291.8 27.6 %collective-permute-start.6 = (bf16[512,2048]{1,0:T(8,128)(2,1)S(1)}, bf16[512,2048]{1,0:T(8,128)(2,1)S(1)}, u32[]{:S(2)}, u32[]{:S(2)}) collective-permute-start(bf16[512,2048]{1,0:T(8,128)(2,1)S(1)} %collective-permute-done.1), channel_id=1, source_target_pairs={{0,1},{1,0},{2,3},{3,2},{4,5},{5,4},{6,7},{7,6},{8,9},{9,8},{10,11... | collective-permute-start | bytes 6291464 | tf_op jit(solution)/shard_map/ppermute | solution.py:60
  514.7 43.3 %collective-permute-start.34 = (bf16[512,2048]{1,0:T(8,128)(2,1)}, bf16[512,2048]{1,0:T(8,128)(2,1)S(1)}, u32[]{:S(2)}, u32[]{:S(2)}) collective-permute-start(bf16[512,2048]{1,0:T(8,128)(2,1)} %get-tuple-element.43), channel_id=1, source_target_pairs={{0,1},{1,0},{2,3},{3,2},{4,5},{5,4},{6,7},{7,6},{8,9},{9,8},{10,11... | collective-permute-start | bytes 6291464 | tf_op jit(solution)/shard_map/ppermute | solution.py:60
  514.7 43.8 %collective-permute-start.35 = (bf16[512,2048]{1,0:T(8,128)(2,1)}, bf16[512,2048]{1,0:T(8,128)(2,1)S(1)}, u32[]{:S(2)}, u32[]{:S(2)}) collective-permute-start(bf16[512,2048]{1,0:T(8,128)(2,1)} %get-tuple-element.44), channel_id=1, source_target_pairs={{0,1},{1,0},{2,3},{3,2},{4,5},{5,4},{6,7},{7,6},{8,9},{9,8},{10,11... | collective-permute-start | bytes 6291464 | tf_op jit(solution)/shard_map/ppermute | solution.py:60
  515.2 43.4 %collective-permute-start.32 = (bf16[512,2048]{1,0:T(8,128)(2,1)}, bf16[512,2048]{1,0:T(8,128)(2,1)}, u32[]{:S(2)}, u32[]{:S(2)}) collective-permute-start(bf16[512,2048]{1,0:T(8,128)(2,1)} %get-tuple-element.45), channel_id=1, source_target_pairs={{0,1},{1,0},{2,3},{3,2},{4,5},{5,4},{6,7},{7,6},{8,9},{9,8},{10,11... | collective-permute-start | bytes 6291464 | tf_op jit(solution)/shard_map/ppermute | solution.py:60
  515.2 56.2 %collective-permute-start.31 = (bf16[512,2048]{1,0:T(8,128)(2,1)}, bf16[512,2048]{1,0:T(8,128)(2,1)}, u32[]{:S(2)}, u32[]{:S(2)}) collective-permute-start(bf16[512,2048]{1,0:T(8,128)(2,1)} %get-tuple-element.46), channel_id=1, source_target_pairs={{0,1},{1,0},{2,3},{3,2},{4,5},{5,4},{6,7},{7,6},{8,9},{9,8},{10,11... | collective-permute-start | bytes 6291464 | tf_op jit(solution)/shard_map/ppermute | solution.py:60
  535.9 46.5 %collective-permute-start.15 = (bf16[512,2048]{1,0:T(8,128)(2,1)}, bf16[512,2048]{1,0:T(8,128)(2,1)}, u32[]{:S(2)}, u32[]{:S(2)}) collective-permute-start(bf16[512,2048]{1,0:T(8,128)(2,1)} %get-tuple-element.51), channel_id=1, source_target_pairs={{0,1},{1,0},{2,3},{3,2},{4,5},{5,4},{6,7},{7,6},{8,9},{9,8},{10,11... | collective-permute-start | bytes 6291464 | tf_op jit(solution)/shard_map/ppermute | solution.py:60
  558.0 25.8 %collective-permute-start.16 = (bf16[512,2048]{1,0:T(8,128)(2,1)}, bf16[512,2048]{1,0:T(8,128)(2,1)}, u32[]{:S(2)}, u32[]{:S(2)}) collective-permute-start(bf16[512,2048]{1,0:T(8,128)(2,1)} %get-tuple-element.52), channel_id=1, source_target_pairs={{0,1},{1,0},{2,3},{3,2},{4,5},{5,4},{6,7},{7,6},{8,9},{9,8},{10,11... | collective-permute-start | bytes 6291464 | tf_op jit(solution)/shard_map/ppermute | solution.py:60
  558.5 25.9 %collective-permute-start.13 = (bf16[512,2048]{1,0:T(8,128)(2,1)}, bf16[512,2048]{1,0:T(8,128)(2,1)}, u32[]{:S(2)}, u32[]{:S(2)}) collective-permute-start(bf16[512,2048]{1,0:T(8,128)(2,1)} %get-tuple-element.53), channel_id=1, source_target_pairs={{0,1},{1,0},{2,3},{3,2},{4,5},{5,4},{6,7},{7,6},{8,9},{9,8},{10,11... | collective-permute-start | bytes 6291464 | tf_op jit(solution)/shard_map/ppermute | solution.py:60
  558.6 26.3 %collective-permute-start.12 = (bf16[512,2048]{1,0:T(8,128)(2,1)}, bf16[512,2048]{1,0:T(8,128)(2,1)}, u32[]{:S(2)}, u32[]{:S(2)}) collective-permute-start(bf16[512,2048]{1,0:T(8,128)(2,1)} %get-tuple-element.54), channel_id=1, source_target_pairs={{0,1},{1,0},{2,3},{3,2},{4,5},{5,4},{6,7},{7,6},{8,9},{9,8},{10,11... | collective-permute-start | bytes 6291464 | tf_op jit(solution)/shard_map/ppermute | solution.py:60
  579.4 76.7 %collective-permute-start.33 = (bf16[256,2048]{1,0:T(8,128)(2,1)}, bf16[256,2048]{1,0:T(8,128)(2,1)}, u32[]{:S(2)}, u32[]{:S(2)}) collective-permute-start(bf16[256,2048]{1,0:T(8,128)(2,1)} %slice.1128), channel_id=1, source_target_pairs={{0,2},{2,0},{1,3},{3,1},{4,6},{6,4},{5,7},{7,5},{8,10},{10,8},{9,1... | collective-permute-start | bytes 3145736 | tf_op jit(solution)/shard_map/ppermute | solution.py:60
  582.3 75.3 %collective-permute-start.38 = (bf16[256,2048]{1,0:T(8,128)(2,1)}, bf16[256,2048]{1,0:T(8,128)(2,1)}, u32[]{:S(2)}, u32[]{:S(2)}) collective-permute-start(bf16[256,2048]{1,0:T(8,128)(2,1)} %slice.1136), channel_id=1, source_target_pairs={{0,16},{16,0},{1,17},{17,1},{2,18},{18,2},{3,19},{19,3},{4,20},{20... | collective-permute-start | bytes 3145736 | tf_op jit(solution)/shard_map/ppermute | solution.py:60
  583.8 44.4 %collective-permute-start.36 = (bf16[256,2048]{1,0:T(8,128)(2,1)}, bf16[256,2048]{1,0:T(8,128)(2,1)}, u32[]{:S(2)}, u32[]{:S(2)}) collective-permute-start(bf16[256,2048]{1,0:T(8,128)(2,1)} %get-tuple-element.108), channel_id=1, source_target_pairs={{0,2},{2,0},{1,3},{3,1},{4,6},{6,4},{5,7},{7,5},{8,10},{10,8},{9,1... | collective-permute-start | bytes 3145736 | tf_op jit(solution)/shard_map/ppermute | solution.py:60
  584.4 47.0 %collective-permute-start.39 = (bf16[256,2048]{1,0:T(8,128)(2,1)}, bf16[256,2048]{1,0:T(8,128)(2,1)}, u32[]{:S(2)}, u32[]{:S(2)}) collective-permute-start(bf16[256,2048]{1,0:T(8,128)(2,1)} %get-tuple-element.109), channel_id=1, source_target_pairs={{0,16},{16,0},{1,17},{17,1},{2,18},{18,2},{3,19},{19,3},{4,20},{20... | collective-permute-start | bytes 3145736 | tf_op jit(solution)/shard_map/ppermute | solution.py:60
  593.3 56.9 %collective-permute-start.17 = (bf16[256,2048]{1,0:T(8,128)(2,1)S(1)}, bf16[256,2048]{1,0:T(8,128)(2,1)S(1)}, u32[]{:S(2)}, u32[]{:S(2)}) collective-permute-start(bf16[256,2048]{1,0:T(8,128)(2,1)S(1)} %get-tuple-element.110), channel_id=1, source_target_pairs={{0,2},{2,0},{1,3},{3,1},{4,6},{6,4},{5,7},{7,5},{8,10},{10,8},{9,1... | collective-permute-start | bytes 3145736 | tf_op jit(solution)/shard_map/ppermute | solution.py:60
  628.2 26.0 %collective-permute-start.20 = (bf16[256,2048]{1,0:T(8,128)(2,1)S(1)}, bf16[256,2048]{1,0:T(8,128)(2,1)S(1)}, u32[]{:S(2)}, u32[]{:S(2)}) collective-permute-start(bf16[256,2048]{1,0:T(8,128)(2,1)S(1)} %get-tuple-element.111), channel_id=1, source_target_pairs={{0,16},{16,0},{1,17},{17,1},{2,18},{18,2},{3,19},{19,3},{4,20},{20... | collective-permute-start | bytes 3145736 | tf_op jit(solution)/shard_map/ppermute | solution.py:60
  631.4 45.4 %collective-permute-start.37 = (bf16[256,2048]{1,0:T(8,128)(2,1)S(1)}, bf16[256,2048]{1,0:T(8,128)(2,1)S(1)}, u32[]{:S(2)}, u32[]{:S(2)}) collective-permute-start(bf16[256,2048]{1,0:T(8,128)(2,1)S(1)} %add_convert_fusion.13), channel_id=1, source_target_pairs={{0,16},{16,0},{1,17},{17,1},{2,18},{18,2},{3,19},{19,3},{4,20},{20... | collective-permute-start | bytes 3145736 | tf_op jit(solution)/shard_map/ppermute | solution.py:60
  650.1 28.1 %collective-permute-start.40 = (bf16[256,2048]{1,0:T(8,128)(2,1)S(1)}, bf16[256,2048]{1,0:T(8,128)(2,1)S(1)}, u32[]{:S(2)}, u32[]{:S(2)}) collective-permute-start(bf16[256,2048]{1,0:T(8,128)(2,1)S(1)} %add_convert_fusion.12), channel_id=1, source_target_pairs={{0,2},{2,0},{1,3},{3,1},{4,6},{6,4},{5,7},{7,5},{8,10},{10,8},{9,1... | collective-permute-start | bytes 3145736 | tf_op jit(solution)/shard_map/ppermute | solution.py:60
  654.3 44.4 %collective-permute-start.14 = (bf16[256,2048]{1,0:T(8,128)(2,1)}, bf16[256,2048]{1,0:T(8,128)(2,1)S(1)}, u32[]{:S(2)}, u32[]{:S(2)}) collective-permute-start(bf16[256,2048]{1,0:T(8,128)(2,1)} %slice.1108), channel_id=1, source_target_pairs={{0,2},{2,0},{1,3},{3,1},{4,6},{6,4},{5,7},{7,5},{8,10},{10,8},{9,1... | collective-permute-start | bytes 3145736 | tf_op jit(solution)/shard_map/ppermute | solution.py:60
  656.1 43.0 %collective-permute-start.19 = (bf16[256,2048]{1,0:T(8,128)(2,1)}, bf16[256,2048]{1,0:T(8,128)(2,1)S(1)}, u32[]{:S(2)}, u32[]{:S(2)}) collective-permute-start(bf16[256,2048]{1,0:T(8,128)(2,1)} %slice.1116), channel_id=1, source_target_pairs={{0,16},{16,0},{1,17},{17,1},{2,18},{18,2},{3,19},{19,3},{4,20},{20... | collective-permute-start | bytes 3145736 | tf_op jit(solution)/shard_map/ppermute | solution.py:60
  657.7 62.5 %collective-permute-start.18 = (bf16[256,2048]{1,0:T(8,128)(2,1)S(1)}, bf16[256,2048]{1,0:T(8,128)(2,1)S(1)}, u32[]{:S(2)}, u32[]{:S(2)}) collective-permute-start(bf16[256,2048]{1,0:T(8,128)(2,1)S(1)} %add_convert_fusion.15), channel_id=1, source_target_pairs={{0,16},{16,0},{1,17},{17,1},{2,18},{18,2},{3,19},{19,3},{4,20},{20... | collective-permute-start | bytes 3145736 | tf_op jit(solution)/shard_map/ppermute | solution.py:60
  676.7 43.5 %collective-permute-start.21 = (bf16[256,2048]{1,0:T(8,128)(2,1)S(1)}, bf16[256,2048]{1,0:T(8,128)(2,1)S(1)}, u32[]{:S(2)}, u32[]{:S(2)}) collective-permute-start(bf16[256,2048]{1,0:T(8,128)(2,1)S(1)} %add_convert_fusion.14), channel_id=1, source_target_pairs={{0,2},{2,0},{1,3},{3,1},{4,6},{6,4},{5,7},{7,5},{8,10},{10,8},{9,1... | collective-permute-start | bytes 3145736 | tf_op jit(solution)/shard_map/ppermute | solution.py:60
  731.4 20.6 %collective-permute-start.55 = (bf16[512,1024]{1,0:T(8,128)(2,1)S(1)}, bf16[512,1024]{1,0:T(8,128)(2,1)S(1)}, u32[]{:S(2)}, u32[]{:S(2)}) collective-permute-start(bf16[512,1024]{1,0:T(8,128)(2,1)S(1)} %convolution_convert_fusion.18), channel_id=1, source_target_pairs={{0,1},{1,0},{2,3},{3,2},{4,5},{5,4},{6,7},{7,6},{8,9},{9,8},{10,11... | collective-permute-start | bytes 3145736 | tf_op jit(solution)/shard_map/ppermute | solution.py:60
  734.9 24.0 %collective-permute-start.57 = (bf16[256,1024]{1,0:T(8,128)(2,1)S(1)}, bf16[256,1024]{1,0:T(8,128)(2,1)S(1)}, u32[]{:S(2)}, u32[]{:S(2)}) collective-permute-start(bf16[256,1024]{1,0:T(8,128)(2,1)S(1)} %slice.1186), channel_id=1, source_target_pairs={{0,2},{2,0},{1,3},{3,1},{4,6},{6,4},{5,7},{7,5},{8,10},{10,8},{9,1... | collective-permute-start | bytes 1572872 | tf_op jit(solution)/shard_map/ppermute | solution.py:60
  738.1 23.8 %collective-permute-start.62 = (bf16[256,1024]{1,0:T(8,128)(2,1)S(1)}, bf16[256,1024]{1,0:T(8,128)(2,1)S(1)}, u32[]{:S(2)}, u32[]{:S(2)}) collective-permute-start(bf16[256,1024]{1,0:T(8,128)(2,1)S(1)} %slice.1190), channel_id=1, source_target_pairs={{0,16},{16,0},{1,17},{17,1},{2,18},{18,2},{3,19},{19,3},{4,20},{20... | collective-permute-start | bytes 1572872 | tf_op jit(solution)/shard_map/ppermute | solution.py:60
  747.9 23.7 %collective-permute-start.61 = (bf16[256,1024]{1,0:T(8,128)(2,1)S(1)}, bf16[256,1024]{1,0:T(8,128)(2,1)S(1)}, u32[]{:S(2)}, u32[]{:S(2)}) collective-permute-start(bf16[256,1024]{1,0:T(8,128)(2,1)S(1)} %add_convert_fusion.19), channel_id=1, source_target_pairs={{0,16},{16,0},{1,17},{17,1},{2,18},{18,2},{3,19},{19,3},{4,20},{20... | collective-permute-start | bytes 1572872 | tf_op jit(solution)/shard_map/ppermute | solution.py:60
  750.8 20.8 %collective-permute-start.64 = (bf16[256,1024]{1,0:T(8,128)(2,1)S(1)}, bf16[256,1024]{1,0:T(8,128)(2,1)S(1)}, u32[]{:S(2)}, u32[]{:S(2)}) collective-permute-start(bf16[256,1024]{1,0:T(8,128)(2,1)S(1)} %add_convert_fusion.18), channel_id=1, source_target_pairs={{0,2},{2,0},{1,3},{3,1},{4,6},{6,4},{5,7},{7,5},{8,10},{10,8},{9,1... | collective-permute-start | bytes 1572872 | tf_op jit(solution)/shard_map/ppermute | solution.py:60
  773.2 210.4 %reduce-scatter.10.cloned.1.call-start = ((), (), s32[]{:S(2)}) async-start(), calls=%async_computation.11 | async-start | bytes 5242880 | tf_op jit(solution)/shard_map/reduce_scatter | solution.py:451
  797.2 188.6 %reduce-scatter.12.cloned.1.call-start = ((), (), s32[]{:S(2)}) async-start(), calls=%async_computation.12 | async-start | bytes 5242880 | tf_op jit(solution)/shard_map/reduce_scatter | solution.py:451
  821.2 215.6 %reduce-scatter.14.cloned.1.call-start = ((), (), s32[]{:S(2)}) async-start(), calls=%async_computation.13 | async-start | bytes 5242880 | tf_op jit(solution)/shard_map/reduce_scatter | solution.py:434
  848.9 277.4 %reduce-scatter.6.cloned.1.call-start = ((), (), s32[]{:S(2)}) async-start(), calls=%async_computation.9 | async-start | bytes 2129920 | tf_op jit(solution)/shard_map/reduce_scatter | solution.py:539
  908.0 41.9 %collective-permute-start.41 = (bf16[512,1536]{1,0:T(8,128)(2,1)}, bf16[512,1536]{1,0:T(8,128)(2,1)S(1)}, u32[]{:S(2)}, u32[]{:S(2)}) collective-permute-start(bf16[512,1536]{1,0:T(8,128)(2,1)} %convolution_convert_fusion.9), channel_id=1, source_target_pairs={{0,1},{1,0},{2,3},{3,2},{4,5},{5,4},{6,7},{7,6},{8,9},{9,8},{10,11... | collective-permute-start | bytes 4718600 | tf_op jit(solution)/shard_map/ppermute | solution.py:60
  908.6 18.1 %collective-permute-start.44 = (bf16[512,1536]{1,0:T(8,128)(2,1)S(1)}, bf16[512,1536]{1,0:T(8,128)(2,1)S(1)}, u32[]{:S(2)}, u32[]{:S(2)}) collective-permute-start(bf16[512,1536]{1,0:T(8,128)(2,1)S(1)} %convolution_convert_fusion.5), channel_id=1, source_target_pairs={{0,1},{1,0},{2,3},{3,2},{4,5},{5,4},{6,7},{7,6},{8,9},{9,8},{10,11... | collective-permute-start | bytes 4718600 | tf_op jit(solution)/shard_map/ppermute | solution.py:60
  919.6 20.5 %collective-permute-start.46 = (bf16[256,1536]{1,0:T(8,128)(2,1)S(1)}, bf16[256,1536]{1,0:T(8,128)(2,1)S(1)}, u32[]{:S(2)}, u32[]{:S(2)}) collective-permute-start(bf16[256,1536]{1,0:T(8,128)(2,1)S(1)} %get-tuple-element.146), channel_id=1, source_target_pairs={{0,2},{2,0},{1,3},{3,1},{4,6},{6,4},{5,7},{7,5},{8,10},{10,8},{9,1... | collective-permute-start | bytes 2359304 | tf_op jit(solution)/shard_map/ppermute | solution.py:60
  924.3 32.8 %collective-permute-start.43 = (bf16[256,1536]{1,0:T(8,128)(2,1)}, bf16[256,1536]{1,0:T(8,128)(2,1)}, u32[]{:S(2)}, u32[]{:S(2)}) collective-permute-start(bf16[256,1536]{1,0:T(8,128)(2,1)} %slice.1158), channel_id=1, source_target_pairs={{0,2},{2,0},{1,3},{3,1},{4,6},{6,4},{5,7},{7,5},{8,10},{10,8},{9,1... | collective-permute-start | bytes 2359304 | tf_op jit(solution)/shard_map/ppermute | solution.py:60
  925.2 20.4 %collective-permute-start.49 = (bf16[256,1536]{1,0:T(8,128)(2,1)S(1)}, bf16[256,1536]{1,0:T(8,128)(2,1)S(1)}, u32[]{:S(2)}, u32[]{:S(2)}) collective-permute-start(bf16[256,1536]{1,0:T(8,128)(2,1)S(1)} %get-tuple-element.147), channel_id=1, source_target_pairs={{0,16},{16,0},{1,17},{17,1},{2,18},{18,2},{3,19},{19,3},{4,20},{20... | collective-permute-start | bytes 2359304 | tf_op jit(solution)/shard_map/ppermute | solution.py:60
  928.7 33.9 %collective-permute-start.48 = (bf16[256,1536]{1,0:T(8,128)(2,1)}, bf16[256,1536]{1,0:T(8,128)(2,1)}, u32[]{:S(2)}, u32[]{:S(2)}) collective-permute-start(bf16[256,1536]{1,0:T(8,128)(2,1)} %slice.1162), channel_id=1, source_target_pairs={{0,16},{16,0},{1,17},{17,1},{2,18},{18,2},{3,19},{19,3},{4,20},{20... | collective-permute-start | bytes 2359304 | tf_op jit(solution)/shard_map/ppermute | solution.py:60
  941.2 37.0 %collective-permute-start.47 = (bf16[256,1536]{1,0:T(8,128)(2,1)}, bf16[256,1536]{1,0:T(8,128)(2,1)}, u32[]{:S(2)}, u32[]{:S(2)}) collective-permute-start(bf16[256,1536]{1,0:T(8,128)(2,1)} %add_convert_fusion.17), channel_id=1, source_target_pairs={{0,16},{16,0},{1,17},{17,1},{2,18},{18,2},{3,19},{19,3},{4,20},{20... | collective-permute-start | bytes 2359304 | tf_op jit(solution)/shard_map/ppermute | solution.py:60
  946.8 31.4 %collective-permute-start.50 = (bf16[256,1536]{1,0:T(8,128)(2,1)}, bf16[256,1536]{1,0:T(8,128)(2,1)}, u32[]{:S(2)}, u32[]{:S(2)}) collective-permute-start(bf16[256,1536]{1,0:T(8,128)(2,1)} %add_convert_fusion.16), channel_id=1, source_target_pairs={{0,2},{2,0},{1,3},{3,1},{4,6},{6,4},{5,7},{7,5},{8,10},{10,8},{9,1... | collective-permute-start | bytes 2359304 | tf_op jit(solution)/shard_map/ppermute | solution.py:60
  982.1 56.2 %collective-permute-start.65 = (bf16[128,1024]{1,0:T(8,128)(2,1)}, bf16[128,1024]{1,0:T(8,128)(2,1)}, u32[]{:S(2)}, u32[]{:S(2)}) collective-permute-start(bf16[128,1024]{1,0:T(8,128)(2,1)} %reduce-scatter.8.cloned.1.call-done), channel_id=1, source_target_pairs={{0,16},{16,0},{1,17},{17,1},{2,18},{18,2},{3,19},{19,3},{4,20},{20... | collective-permute-start | bytes 786440 | tf_op jit(solution)/shard_map/ppermute | solution.py:60
  984.9 55.5 %collective-permute-start.66 = (bf16[256,1024]{1,0:T(8,128)(2,1)S(1)}, bf16[256,1024]{1,0:T(8,128)(2,1)S(1)}, u32[]{:S(2)}, u32[]{:S(2)}) collective-permute-start(bf16[256,1024]{1,0:T(8,128)(2,1)S(1)} %broadcast_select_fusion.20), channel_id=1, source_target_pairs={{0,2},{2,0},{1,3},{3,1},{4,6},{6,4},{5,7},{7,5},{8,10},{10,8},{9,1... | collective-permute-start | bytes 1572872 | tf_op jit(solution)/shard_map/ppermute | solution.py:60
  987.1 53.4 %collective-permute-start.70 = (bf16[256,1024]{1,0:T(8,128)(2,1)S(1)}, bf16[256,1024]{1,0:T(8,128)(2,1)S(1)}, u32[]{:S(2)}, u32[]{:S(2)}) collective-permute-start(bf16[256,1024]{1,0:T(8,128)(2,1)S(1)} %broadcast_select_fusion.16), channel_id=1, source_target_pairs={{0,2},{2,0},{1,3},{3,1},{4,6},{6,4},{5,7},{7,5},{8,10},{10,8},{9,1... | collective-permute-start | bytes 1572872 | tf_op jit(solution)/shard_map/ppermute | solution.py:60
  1036.8 26.2 %collective-permute-start.74 = (bf16[256,2048]{1,0:T(8,128)(2,1)}, bf16[256,2048]{1,0:T(8,128)(2,1)S(1)}, u32[]{:S(2)}, u32[]{:S(2)}) collective-permute-start(bf16[256,2048]{1,0:T(8,128)(2,1)} %reduce-scatter.14.cloned.1.call-done), channel_id=1, source_target_pairs={{0,16},{16,0},{1,17},{17,1},{2,18},{18,2},{3,19},{19,3},{4,20},{20... | collective-permute-start | bytes 3145736 | tf_op jit(solution)/shard_map/ppermute | solution.py:60
  1043.8 41.7 %collective-permute-start.73 = (bf16[512,1024]{1,0:T(8,128)(2,1)S(1)}, bf16[512,1024]{1,0:T(8,128)(2,1)S(1)}, u32[]{:S(2)}, u32[]{:S(2)}) collective-permute-start(bf16[512,1024]{1,0:T(8,128)(2,1)S(1)} %pad_maximum_fusion.6), channel_id=1, source_target_pairs={{0,16},{16,0},{1,17},{17,1},{2,18},{18,2},{3,19},{19,3},{4,20},{20... | collective-permute-start | bytes 3145736 | tf_op jit(solution)/shard_map/ppermute | solution.py:60
  1044.8 61.7 %collective-permute-start.69 = (bf16[512,1024]{1,0:T(8,128)(2,1)S(1)}, bf16[512,1024]{1,0:T(8,128)(2,1)S(1)}, u32[]{:S(2)}, u32[]{:S(2)}) collective-permute-start(bf16[512,1024]{1,0:T(8,128)(2,1)S(1)} %pad_maximum_fusion.5), channel_id=1, source_target_pairs={{0,16},{16,0},{1,17},{17,1},{2,18},{18,2},{3,19},{19,3},{4,20},{20... | collective-permute-start | bytes 3145736 | tf_op jit(solution)/shard_map/ppermute | solution.py:60
  (73 other events, 913.1 us)
Sparse Core Ops, SparseCore 0:
  10.8 136.2 all-gather.4
  149.3 76.1 all-gather.6
  227.6 148.1 all-gather.8
  377.9 78.9 all-gather.10
  773.4 25.4 reduce-scatter.7
  801.6 75.3 reduce-scatter.9
  879.8 77.2 reduce-scatter.11
  959.5 77.2 reduce-scatter.13
  1039.1 37.9 reduce-scatter.5
